TPU v7x, 512 devices: a whole 4x4x16 slice. The times are simulated.
512 devices in a mesh: row: 16 (over y, x), col: 32 (over z, core).
Axes of the slice: x: 4, y: 4, z: 16, core: 2. Of those that a mesh axis runs over, the one named last changes fastest.
Arguments:
- inverse_sep: float32 [12288, 12288], P('row', 'col'), may hold values from -105 to 105, as said below
- sep_panels: float32 [3, 12288, 256], P(None, 'row', 'col'), may hold values from -0.0546875 to 0.0546875
- chain_panels: float32 [3, 256, 256], P(None, 'row', 'col'), may hold values from -0.375 to 0.375
- diag_inverse: float32 [3, 256, 256], P(None, 'row'), may hold values from -5 to 5, as said below
- tile_list: int32 [3, 96], replicated, may hold values from 0 to 1, as said below
Outputs:
- sep_rows: float32 [3, 256, 12288], P(None, 'row', 'col')
- chain_inverse: float32 [3, 256, 768], P(None, 'row')
Inputs may be any that keep to these rules, and one draw needn't show every extreme that they name: `inverse_sep`: symmetric. `diag_inverse`: each block symmetric. `tile_list`: a tile listed for supernode k is listed for every earlier supernode.
All inputs are finite; a program needn't handle non-finite values.
Results may differ from a plain program's by a relative error of at most 0.00013.
Values sent between devices are 32-bit elements; how exact they have to be, the bound alone decides.
No kernel may reach another device: no remote copies, remote signals or barrier semaphores. Data moves between devices by JAX's collectives and lax.ppermute only.
A program may use at most 64 MiB of HBM per device.

v0:
```python
import jax
import jax.numpy as jnp
from jax import lax
from jax.sharding import PartitionSpec as P

NB = 256
TILE = 128
NSUPER = 3


def broadcast(block, axis, source):
    block = jnp.where(lax.axis_index(axis) == source, block, jnp.zeros_like(block))
    return lax.psum(block, axis)


def pair_index(current, earlier):
    return current * (current - 1) // 2 + earlier


def product(left, right):
    return jnp.dot(left, right, precision=lax.Precision.HIGHEST, preferred_element_type=jnp.float32)


def inner_product(left, right):
    return lax.dot_general(
        left,
        right,
        (((0,), (0,)), ((), ())),
        precision=lax.Precision.HIGHEST,
        preferred_element_type=jnp.float32,
    )


def per_device(inverse_sep, sep_panels, chain_panels, diag_inverse, tile_list):
    row_count = lax.axis_size("row")
    col_count = lax.axis_size("col")
    row_place = lax.axis_index("row")
    col_place = lax.axis_index("col")
    row_cells, col_cells = inverse_sep.shape
    nb_rows = NB // row_count
    nb_cols = NB // col_count
    ratio_cols = col_count // row_count
    root_row = col_place // ratio_cols
    inner_part = col_place % ratio_cols
    tile_rows = row_cells // TILE
    listed = lax.dynamic_slice_in_dim(tile_list, row_place * tile_rows, tile_rows, 1).astype(
        jnp.float32
    )
    panels = [None] * NSUPER
    column_panels = [None] * NSUPER
    chain_rowlay = [None] * NSUPER
    chain_colrows = [None] * NSUPER
    state = jnp.zeros((NSUPER, nb_rows, NSUPER * NB), jnp.float32)
    new_rows = []
    for current in range(NSUPER):
        gathered, chains = (
            lax.all_gather(sep_panels[current : current + 1], "col", axis=2, tiled=True),
            lax.all_gather(chain_panels[current : current + 1], "col", axis=2, tiled=True),
        )
        panels[current] = (
            gathered[0].reshape(tile_rows, TILE, NB) * listed[current][:, None, None]
        ).reshape(row_cells, NB)
        chain_rowlay[current] = chains[0]
        local_col = lax.dynamic_slice_in_dim(panels[current], inner_part * col_cells, col_cells, 0)
        payload = jnp.concatenate(
            [local_col, lax.dynamic_slice_in_dim(chains[0], inner_part * nb_cols, nb_cols, 0)],
            axis=0,
        )
        shared = broadcast(payload, "row", root_row)
        column_panels[current] = shared[:col_cells]
        chain_colrows[current] = shared[col_cells:]
        panel = panels[current]
        earlier_pairs = [
            (chain_rowlay[pair_index(current, earlier)], new_rows[earlier])
            for earlier in range(current)
        ]
        summed = inner_product(panel, inverse_sep)
        for chain_block, old_rows in earlier_pairs:
            summed = summed + inner_product(chain_block, old_rows)
        rows_now = -lax.psum_scatter(summed, "row", scatter_dimension=0, tiled=True)
        col_panel = column_panels[current]
        parts = [product(rows_now, col_panel)]
        for earlier in range(current):
            crossed = product(new_rows[earlier], col_panel)
            for middle in range(current):
                state_cols = lax.dynamic_slice_in_dim(
                    state[earlier], middle * NB + col_place * nb_cols, nb_cols, 1
                )
                crossed = crossed + product(state_cols, chain_colrows[pair_index(current, middle)])
            parts.append(crossed)
        totals = lax.psum(jnp.stack(parts), "col")
        first_term = totals[0]
        crossing = [-totals[1 + earlier] for earlier in range(current)]
        second_term = jnp.zeros((nb_rows, NB), jnp.float32)
        if current > 0:
            mirrored = jnp.swapaxes(
                lax.all_to_all(jnp.stack(crossing), "row", split_axis=2, concat_axis=1, tiled=True),
                1,
                2,
            )
            partial_sum = jnp.zeros((nb_rows, NB), jnp.float32)
            for earlier in range(current):
                mirror_cols = lax.dynamic_slice_in_dim(
                    mirrored[earlier], col_place * nb_cols, nb_cols, 1
                )
                partial_sum = partial_sum + product(
                    mirror_cols, chain_colrows[pair_index(current, earlier)]
                )
            second_term = lax.psum(partial_sum, "col")
            for earlier in range(current):
                state = state.at[earlier, :, current * NB : (current + 1) * NB].set(
                    crossing[earlier]
                )
                state = state.at[current, :, earlier * NB : (earlier + 1) * NB].set(
                    mirrored[earlier]
                )
        state = state.at[current, :, current * NB : (current + 1) * NB].set(
            diag_inverse[current] - first_term - second_term
        )
        new_rows.append(rows_now)
    return (jnp.stack(new_rows), state)


def solution(mesh):
    in_specs = (
        P("row", "col"),
        P(None, "row", "col"),
        P(None, "row", "col"),
        P(None, "row", None),
        P(),
    )
    out_specs = (P(None, "row", "col"), P(None, "row", None))
    return jax.shard_map(
        per_device, mesh=mesh, in_specs=in_specs, out_specs=out_specs, check_vma=False
    )
```

profile of v0, /device:TPU:1, one launch (start us, length us, event | category | flops | bytes accessed | tf_op | source)
XLA Modules:
  0.0 953.9 jit_solution(4085583582345847917)
XLA Ops:
  7.2 1.5 fusion.77
  9.5 39.7 %all_gather.18 = f32[1,768,256]{1,2,0:T(8,128)S(1)} all-gather(f32[1,768,8]{1,2,0:T(8,128)S(1)} %get-tuple-element.119), channel_id=1, replica_groups=mesh['row'=16,'col'=32] {'col'}, dimensions={2}, use_global_device_ids=true | all-gather | bytes 811008 | tf_op jit(solution)/shard_map/all_gather | solution.py:57
  49.3 2.2 fusion.82
  51.6 29.2 %all_gather.21 = f32[1,768,256]{1,2,0:T(8,128)S(1)} all-gather(f32[1,768,8]{1,2,0:T(8,128)S(1)} %get-tuple-element.120), channel_id=1, replica_groups=mesh['row'=16,'col'=32] {'col'}, dimensions={2}, use_global_device_ids=true | all-gather | bytes 811008 | tf_op jit(solution)/shard_map/all_gather | solution.py:57
  81.0 2.2 fusion.84
  83.2 31.4 %all_gather.22 = f32[1,16,256]{1,2,0:T(8,128)} all-gather(f32[1,16,8]{1,2,0:T(8,128)S(1)} %get-tuple-element.131), channel_id=1, replica_groups=mesh['row'=16,'col'=32] {'col'}, dimensions={2}, use_global_device_ids=true | all-gather | bytes 16896 | tf_op jit(solution)/shard_map/all_gather | solution.py:58
  114.6 30.1 %all_gather.23 = f32[1,16,256]{1,2,0:T(8,128)} all-gather(f32[1,16,8]{1,2,0:T(8,128)S(1)} %get-tuple-element.130), channel_id=1, replica_groups=mesh['row'=16,'col'=32] {'col'}, dimensions={2}, use_global_device_ids=true | all-gather | bytes 16896 | tf_op jit(solution)/shard_map/all_gather | solution.py:58
  144.7 30.5 %all_gather.19 = f32[1,768,256]{1,2,0:T(8,128)S(1)} all-gather(f32[1,768,8]{1,2,0:T(8,128)S(1)} %copy-done.9), channel_id=1, replica_groups=mesh['row'=16,'col'=32] {'col'}, dimensions={2}, use_global_device_ids=true | all-gather | bytes 811008 | tf_op jit(solution)/shard_map/all_gather | solution.py:57
  175.3 30.1 %all_gather.20 = f32[1,16,256]{1,2,0:T(8,128)} all-gather(f32[1,16,8]{1,2,0:T(8,128)S(1)} %get-tuple-element.129), channel_id=1, replica_groups=mesh['row'=16,'col'=32] {'col'}, dimensions={2}, use_global_device_ids=true | all-gather | bytes 16896 | tf_op jit(solution)/shard_map/all_gather | solution.py:58
  206.2 1.7 dynamic-slice_bitcast_fusion.2
  207.8 1.7 dynamic-slice_bitcast_fusion.1
  211.5 1.9 maximum_select_fusion
  214.4 1.4 fusion.83
  215.9 2.0 fusion.2
  220.2 107.6 %all-reduce.11.cloned.1.call-done = f32[256,384]{1,0:T(8,128)} async-done(((f32[256,384]{1,0:T(8,128)}), f32[256,384]{1,0:T(8,128)}) %all-reduce.11.cloned.1.call-update) | async-done | bytes 393232
  327.7 1.9 fusion
  330.4 3.2 and_reduce_fusion
  335.1 117.5 %all-reduce.13.cloned.1.call-done = (f32[256,384]{1,0:T(8,128)}, f32[392,256]{0,1:T(8,128)}, f32[392,256]{0,1:T(8,128)}, f32[392,256]{0,1:T(8,128)}) async-done(((f32[256,384]{1,0:T(8,128)}, f32[392,256]{0,1:T(8,128)}, f32[392,256]{0,1:T(8,128)}, f32[392,256]{0,1:T(8,128)}), (f32[256,384]{1,0:T(8,128)}, f32[392,256]{0,1:T(8,128)}, f32[392,256]{0,1:T(8,128)}, ...) | async-done | bytes 1597456
  452.6 1.5 convolution_bitcast_fusion.5
  454.1 90.6 %psum.57 = f32[1,16,256]{2,1,0:T(8,128)S(1)} all-reduce(f32[1,16,256]{2,1,0:T(8,128)S(1)} %convolution_bitcast_fusion.5), channel_id=1, replica_groups=mesh['row'=16,'col'=32] {'col'}, use_global_device_ids=true, to_apply=%region_4.5 | all-reduce | flops 4096 | bytes 32768 | tf_op jit(solution)/shard_map/psum | solution.py:91
  544.8 1.4 fusion.7
  548.5 90.0 %psum.59 = f32[2,16,256]{2,1,0:T(8,128)S(1)} all-reduce(f32[2,16,256]{2,1,0:T(8,128)S(1)} %pad_maximum_fusion.2), channel_id=1, replica_groups=mesh['row'=16,'col'=32] {'col'}, use_global_device_ids=true, to_apply=%region_7.8 | all-reduce | flops 8192 | bytes 65536 | tf_op jit(solution)/shard_map/psum | solution.py:91
  638.6 2.0 slice_negate_fusion.2
  642.9 4.4 all-to-all-start
  651.6 1.7 scatter.31
  656.0 91.5 %psum.60 = f32[16,256]{1,0:T(8,128)S(1)} all-reduce(f32[16,256]{1,0:T(8,128)S(1)} %fusion.18), channel_id=1, replica_groups=mesh['row'=16,'col'=32] {'col'}, use_global_device_ids=true, to_apply=%region_8.9 | all-reduce | flops 4096 | bytes 32768 | tf_op jit(solution)/shard_map/psum | solution.py:109
  748.6 90.0 %psum.62 = f32[3,16,256]{2,1,0:T(8,128)S(1)} all-reduce(f32[3,16,256]{2,1,0:T(8,128)S(1)} %pad_maximum_fusion.1), channel_id=1, replica_groups=mesh['row'=16,'col'=32] {'col'}, use_global_device_ids=true, to_apply=%region_11.12 | all-reduce | flops 12288 | bytes 98304 | tf_op jit(solution)/shard_map/psum | solution.py:91
  838.6 1.8 slice_negate_fusion.1
  841.5 5.3 all-to-all-start.1
  847.5 1.4 scatter.36
  848.9 4.4 all-to-all-done.1
  855.2 91.5 %psum.63 = f32[16,256]{1,0:T(8,128)S(1)} all-reduce(f32[16,256]{1,0:T(8,128)S(1)} %convolution_add_fusion), channel_id=1, replica_groups=mesh['row'=16,'col'=32] {'col'}, use_global_device_ids=true, to_apply=%region_12.13 | all-reduce | flops 4096 | bytes 32768 | tf_op jit(solution)/shard_map/psum | solution.py:109
  (97 shorter events, 25.6 us)
Async XLA Ops:
  7.2 42.1 %copy-start = (f32[768,384]{1,0:T(8,128)S(1)}, f32[768,384]{1,0:T(8,128)}, u32[]{:S(2)}) copy-start(f32[768,384]{1,0:T(8,128)} %param.23) | copy-start | bytes 3538948
  7.2 208.7 %all-reduce.9.cloned.1.call-start = ((), (), s32[]{:S(2)}) async-start(), calls=%async_computation.2 | async-start | bytes 786432
  51.5 276.2 %all-reduce.11.cloned.1.call-start = ((), (), s32[]{:S(2)}) async-start(), calls=%async_computation.3 | async-start | bytes 786432
  81.0 2.2 copy-start.11
  81.0 63.7 %copy-start.9 = (f32[1,768,8]{1,2,0:T(8,128)S(1)}, f32[1,768,8]{1,2,0:T(8,128)}, u32[]{:S(2)}) copy-start(f32[1,768,8]{1,2,0:T(8,128)} %get-tuple-element.118) | copy-start | bytes 73732
  209.5 3.9 copy-start.7
  214.4 1.5 copy-start.6
  215.8 2.2 copy-start.4
  215.8 3.2 copy-start.3
  215.8 3.1 copy-start.5
  217.9 234.7 %all-reduce.13.cloned.1.call-start = ((), (), s32[]{:S(2)}) async-start(), calls=%async_computation.4 | async-start | bytes 3932160
  329.7 0.7 copy-start.12
  329.7 215.1 %copy-start.10 = (f32[3,16,256]{2,1,0:T(8,128)S(1)}, f32[3,16,256]{2,1,0:T(8,128)}, u32[]{:S(2)}) copy-start(f32[3,16,256]{2,1,0:T(8,128)} %param.26) | copy-start | bytes 147460
  452.6 94.8 %copy-start.2 = (f32[392,256]{0,1:T(8,128)S(1)}, f32[392,256]{0,1:T(8,128)}, u32[]{:S(2)}) copy-start(f32[392,256]{0,1:T(8,128)} %get-tuple-element.114) | copy-start | bytes 1204228
  452.6 194.8 %copy-start.1 = (f32[392,256]{0,1:T(8,128)S(1)}, f32[392,256]{0,1:T(8,128)}, u32[]{:S(2)}) copy-start(f32[392,256]{0,1:T(8,128)} %get-tuple-element.115) | copy-start | bytes 1204228
  642.9 10.9 %all-to-all-start = ((f32[16,1,256]{2,1,0:T(1,128)}), f32[16,1,256]{2,1,0:T(1,128)S(1)}, u32[]{:S(2)}, u32[]{:S(2)}) async-start(f32[16,1,256]{2,1,0:T(1,128)} %reshape.358), calls=%async_computation | async-start | bytes 32768 | tf_op jit(solution)/shard_map/all_to_all | solution.py:97
  841.5 11.8 %all-to-all-start.1 = ((f32[16,1,512]{2,1,0:T(1,128)}), f32[16,1,512]{2,1,0:T(1,128)S(1)}, u32[]{:S(2)}, u32[]{:S(2)}) async-start(f32[16,1,512]{2,1,0:T(1,128)} %reshape.360), calls=%async_computation.1 | async-start | bytes 65536 | tf_op jit(solution)/shard_map/all_to_all | solution.py:97
  946.7 0.7 copy-start.8
Sparse Core Ops, SparseCore 0:
  51.6 109.0 all-reduce.8
  218.1 109.6 all-reduce.10
  331.5 121.0 all-reduce.12
where the time goes:
time: 956 us; the launch traced here: 954 us
  blocking collectives  645 us (67%)
  waiting for transfers between devices  230 us (24%)
  matrix products  22.4 us (2%)
  other arithmetic  16.9 us (2%)
  local copies, waits for them, and re-layouts  15.3 us (2%)
  between operations  14.9 us (2%)
  starting transfers between devices  9.87 us (1%)
    psum x3, blocking collectives, per_device(): totals = lax.psum(jnp.stack(parts), 'col')  271 us
    unnamed x6, waiting for transfers between devices  225 us
    psum x2, blocking collectives, per_device(): second_term = lax.psum(partial_sum, 'col')  183 us
    all_gather x3, blocking collectives, per_device(): lax.all_gather(sep_panels[current:current + 1], 'col', axis=2, tiled=True)  99.5 us
    all_gather x3, blocking collectives, per_device(): lax.all_gather(chain_panels[current:current + 1], 'col', axis=2, tiled=True)  91.6 us
  transfers between devices with their start and end apart: 5, of which 4 were waited for; matrix products, arithmetic and copies ran while one was open for 3% of the time, Pallas kernels for 0%

commit v1 on v0

v1 whole, which is shorter than its diff:
```python
import jax
import jax.numpy as jnp
from jax import lax
from jax.sharding import PartitionSpec as P

TILE = 128
NSUPER = 3


def contract(left, right, left_dim, right_dim):
    return lax.dot_general(
        left,
        right,
        (((left_dim,), (right_dim,)), ((), ())),
        precision=lax.Precision.HIGH,
        preferred_element_type=jnp.float32,
    )


def spread(block, axis):
    count = lax.axis_size(axis)
    copies = jnp.broadcast_to(block[None], (count,) + block.shape)
    return lax.all_to_all(copies, axis, 0, 0, tiled=True)


def per_device(inverse_sep, sep_panels, chain_panels, diag_inverse, tile_list):
    rows = lax.axis_size("row")
    cols = lax.axis_size("col")
    row = lax.axis_index("row")
    col = lax.axis_index("col")
    height, width = inverse_sep.shape
    nb_cols = sep_panels.shape[2]
    nb_rows = chain_panels.shape[1]
    nb = nb_cols * cols
    ratio = cols // rows
    core = col % ratio
    tiles = height // TILE
    npair = chain_panels.shape[0]

    listed = lax.dynamic_slice_in_dim(tile_list, row * tiles, tiles, 1).astype(jnp.float32)
    mask = jnp.broadcast_to(listed[:, :, None], (NSUPER, tiles, TILE)).reshape(NSUPER, 1, height)
    local_panel = (jnp.swapaxes(sep_panels, 1, 2) * mask).reshape(NSUPER * nb_cols, height)

    chain_local = jnp.swapaxes(chain_panels, 1, 2).reshape(1, npair * nb_cols * nb_rows)
    chain_cols = spread(chain_local, "row").reshape(rows, npair, nb_cols, nb_rows)
    chain_cols = jnp.transpose(chain_cols, (1, 2, 0, 3)).reshape(npair * nb_cols, nb)

    gathered = lax.all_gather(
        jnp.concatenate([local_panel, chain_cols], axis=1), "col", axis=0, tiled=True
    ).reshape(cols, NSUPER, nb_cols, height + nb)
    panel = [gathered[:, k, :, :height].reshape(nb, height) for k in range(NSUPER)]
    chain = [gathered[:, p, :, height:].reshape(nb, nb) for p in range(npair)]

    part = []
    for k in range(NSUPER):
        acc = contract(panel[k], inverse_sep, 1, 0)
        for j in range(k):
            acc = acc + contract(chain[k * (k - 1) // 2 + j], part[j], 1, 0)
        part.append(-acc)
    outgoing = jnp.stack([x.reshape(rows, nb_rows, width) for x in part], axis=1)
    incoming = lax.all_to_all(
        outgoing.reshape(rows, NSUPER * nb_rows, width), "row", 0, 0, tiled=True
    )
    new_rows = jnp.sum(incoming, axis=0).reshape(NSUPER, nb_rows, width)

    def route(flip):
        return [
            (r * cols + c, (c // ratio) * cols + ratio * r + ((c % ratio) ^ flip))
            for r in range(rows)
            for c in range(cols)
        ]

    lower, upper = new_rows[:, :nb_cols], new_rows[:, nb_cols:]
    same = jnp.where(core == 0, lower, upper).reshape(NSUPER * nb_cols, width)
    other = jnp.where(core == 0, upper, lower).reshape(NSUPER * nb_cols, width)
    same = lax.ppermute(same, ("row", "col"), route(0))
    other = lax.ppermute(other, ("row", "col"), route(1))
    turned = jnp.concatenate(
        [jnp.where(core == 0, same, other), jnp.where(core == 0, other, same)], axis=1
    )

    cc = chain_cols.reshape(npair, nb_cols, nb)
    place = col * nb_cols + lax.broadcasted_iota(jnp.int32, (nb_cols, nb), 0)
    unit = (lax.broadcasted_iota(jnp.int32, (nb_cols, nb), 1) == place).astype(jnp.float32)
    zero = jnp.zeros((nb_cols, nb), jnp.float32)
    solve = []
    solve.append(jnp.concatenate([unit, -cc[0], contract(cc[2], chain[0], 1, 0) - cc[1]], axis=0))
    solve.append(jnp.concatenate([zero, unit, -cc[2]], axis=0))
    solve.append(jnp.concatenate([zero, zero, unit], axis=0))
    inner = []
    for k in range(NSUPER):
        mine = lax.dynamic_slice_in_dim(solve[k], row * nb_rows, nb_rows, 1)
        acc = contract(mine, diag_inverse[k], 1, 0) - contract(turned, panel[k], 1, 1)
        for j in range(k):
            acc = acc - contract(inner[j], chain[k * (k - 1) // 2 + j], 1, 1)
        inner.append(acc)
    packed = jnp.stack(inner, axis=1).reshape(NSUPER * nb_cols, NSUPER, rows, nb_rows)
    packed = jnp.transpose(packed, (2, 0, 1, 3)).reshape(rows, 1, nb_cols * NSUPER * NSUPER * nb_rows)
    summed = jnp.sum(lax.all_to_all(packed, "row", 0, 0, tiled=True), axis=0)
    whole = spread(summed, "col").reshape(cols, NSUPER, nb_cols, NSUPER, nb_rows)
    state = jnp.transpose(whole, (3, 4, 1, 0, 2)).reshape(NSUPER, nb_rows, NSUPER * nb)
    return (new_rows, state)


def solution(mesh):
    in_specs = (
        P("row", "col"),
        P(None, "row", "col"),
        P(None, "row", "col"),
        P(None, "row", None),
        P(),
    )
    out_specs = (P(None, "row", "col"), P(None, "row", None))
    return jax.shard_map(
        per_device, mesh=mesh, in_specs=in_specs, out_specs=out_specs, check_vma=False
    )
```

time: 956 us -> 211 us (0.22)
  blocking collectives: 645 us -> 55.3 us
  waiting for transfers between devices: 230 us -> 97 us
  other arithmetic: 16.9 us -> 3.78 us
  local copies, waits for them, and re-layouts: 15.3 us -> 5.2 us
    psum x5 -> x0, blocking collectives: 454 us -> none  [the longest x3 271 us: per_device(): totals = lax.psum(jnp.stack(parts), 'col')]
    unnamed x6 -> x1, waiting for transfers between devices: 225 us -> 0.02 us
    all_gather x6 -> x0, blocking collectives: 191 us -> none  [the longest x3 99.5 us: per_device(): lax.all_gather(sep_panels[current:current + 1], 'col', axis=2, tiled=True)]
    all_gather x0 -> x1, waiting for transfers between devices: none -> 75.3 us  [per_device(): lax.all_gather(jnp.concatenate([local_panel, chain_cols], axis=1), 'col',...]
    all_to_all x0 -> x2, blocking collectives: none -> 55.3 us  [the longest x1 30.9 us: per_device(): summed = jnp.sum(lax.all_to_all(packed, 'row', 0, 0, tiled=True), axis=0)]
    all_to_all x2, waiting for transfers between devices: 4.86 us -> 21.1 us  [the longest x1 16.4 us: per_device(): lax.all_to_all(outgoing.reshape(rows, NSUPER * nb_rows, width), 'row', 0,...]
    dot_general x20 -> x16, matrix products: 22.4 us -> 15.7 us  [contract(): lax.dot_general(left, right, (((left_dim,), (right_dim,)), ((), ())), pre...]
  transfers between devices with their start and end apart: 5 -> 5, of which waited for: 4 -> 4; matrix products, arithmetic and copies ran while one was open for 3% -> 2% of each run, Pallas kernels for 0% -> 0%
where the time goes in v1:
time: 211 us; the launch traced here: 210 us
  waiting for transfers between devices  97 us (46%)
  blocking collectives  55.3 us (26%)
  starting transfers between devices  18.8 us (9%)
  matrix products  15.7 us (7%)
  between operations  14.6 us (7%)
  local copies, waits for them, and re-layouts  5.2 us (2%)
  other arithmetic  3.78 us (2%)
    all_gather x1, waiting for transfers between devices, per_device(): lax.all_gather(jnp.concatenate([local_panel, chain_cols], axis=1), 'col',...  75.3 us
    all_to_all x1, blocking collectives, per_device(): summed = jnp.sum(lax.all_to_all(packed, 'row', 0, 0, tiled=True), axis=0)  30.9 us
    all_to_all x1, blocking collectives, spread(): return lax.all_to_all(copies, axis, 0, 0, tiled=True)  24.4 us
    all_to_all x1, waiting for transfers between devices, per_device(): lax.all_to_all(outgoing.reshape(rows, NSUPER * nb_rows, width), 'row', 0,...  16.4 us
    dot_general x16, matrix products, contract(): lax.dot_general(left, right, (((left_dim,), (right_dim,)), ((), ())), pre...  15.7 us
    all_to_all x1, starting transfers between devices, spread(): return lax.all_to_all(copies, axis, 0, 0, tiled=True)  7.57 us
    all_to_all x1, starting transfers between devices, per_device(): lax.all_to_all(outgoing.reshape(rows, NSUPER * nb_rows, width), 'row', 0,...  6.6 us
    all_to_all x1, waiting for transfers between devices, spread(): return lax.all_to_all(copies, axis, 0, 0, tiled=True)  4.65 us
  transfers between devices with their start and end apart: 5, of which 4 were waited for; matrix products, arithmetic and copies ran while one was open for 2% of the time, Pallas kernels for 0%

profile of v1, /device:TPU:1, one launch (start us, length us, event | category | flops | bytes accessed | tf_op | source)
XLA Modules:
  0.0 210.4 jit_solution(3932723138883772412)
XLA Ops:
  7.2 0.9 broadcast_in_dim.11
  8.1 0.6 broadcast_in_dim.24
  8.7 7.6 %all-to-all-start = ((f32[16,1,384]{2,1,0:T(1,128)}), f32[16,1,384]{2,1,0:T(1,128)S(1)}, u32[]{:S(2)}, u32[]{:S(2)}) async-start(f32[16,1,384]{2,1,0:T(1,128)} %broadcast_in_dim.24), calls=%async_computation | async-start | bytes 49152 | tf_op jit(solution)/shard_map/all_to_all | solution.py:23
  16.3 0.8 dynamic-slice_convert_fusion
  17.2 0.9 multiply_bitcast_fusion
  18.1 4.7 %all-to-all-done = f32[16,1,384]{2,1,0:T(1,128)S(1)} async-done(((f32[16,1,384]{2,1,0:T(1,128)}), f32[16,1,384]{2,1,0:T(1,128)S(1)}, u32[]{:S(2)}, u32[]{:S(2)}) %all-to-all-start) | async-done | bytes 24608 | tf_op jit(solution)/shard_map/all_to_all | solution.py:23
  23.1 0.6 pad_maximum_fusion.1
  23.8 75.3 %all-gather.2.cloned.1.call-done = f32[768,1024]{1,0:T(8,128)} async-done(((f32[24,1024]{1,0:T(8,128)}), f32[768,1024]{1,0:T(8,128)}) %all-gather.2.cloned.1.call-update) | async-done | bytes 3145744 | tf_op jit(solution)/shard_map/all_gather | solution.py:48
  99.1 2.1 convolution_negate_fusion
  101.2 1.3 fusion.4
  102.9 0.8 fusion.2
  103.7 0.4 fusion.5
  104.1 0.8 fusion.1
  104.9 1.1 pad_maximum_fusion
  106.0 6.6 %all-to-all-start.1 = ((f32[16,48,384]{2,1,0:T(8,128)}), f32[16,48,384]{2,1,0:T(8,128)S(1)}, u32[]{:S(2)}, u32[]{:S(2)}) async-start(f32[16,48,384]{2,1,0:T(8,128)} %bitcast.17), calls=%async_computation.1 | async-start | bytes 2359296 | tf_op jit(solution)/shard_map/all_to_all | solution.py:61
  113.5 1.1 fusion.3
  114.6 16.4 %all-to-all-done.1 = f32[16,48,384]{2,1,0:T(8,128)S(1)} async-done(((f32[16,48,384]{2,1,0:T(8,128)}), f32[16,48,384]{2,1,0:T(8,128)S(1)}, u32[]{:S(2)}, u32[]{:S(2)}) %all-to-all-start.1) | async-done | bytes 1179680 | tf_op jit(solution)/shard_map/all_to_all | solution.py:61
  131.1 0.7 collective-permute-start
  131.8 4.0 %collective-permute-start.1 = (f32[24,384]{1,0:T(8,128)S(1)}, f32[24,384]{1,0:T(8,128)S(1)}, u32[]{:S(2)}, u32[]{:S(2)}) collective-permute-start(f32[24,384]{1,0:T(8,128)S(1)} %get-tuple-element.14), channel_id=1, source_target_pairs={{0,1},{1,0},{2,33},{3,32},{4,65},{5,64},{6,97},{7,96},{8,129},{9,1... | collective-permute-start | bytes 110600 | tf_op jit(solution)/shard_map/ppermute | solution.py:77
  136.0 0.6 collective-permute-done.1
  136.6 1.6 convolution_subtract_fusion.5
  138.2 1.6 convolution_subtract_fusion.4
  139.8 1.6 convolution_subtract_fusion.2
  141.5 1.1 convolution_subtract_fusion.3
  142.7 1.1 convolution_subtract_fusion.1
  144.1 1.1 convolution_subtract_fusion
  145.5 0.4 copy.30
  145.9 0.5 reshape.73
  146.4 30.9 %all_to_all.20 = f32[16,1,1152]{2,1,0:T(1,128)S(1)} all-to-all(f32[16,1,1152]{2,1,0:T(1,128)S(1)} %reshape.73), channel_id=1, replica_groups=mesh['row'=16,'col'=32] {'row'}, dimensions={0} | all-to-all | bytes 147456 | tf_op jit(solution)/shard_map/all_to_all | solution.py:99
  177.4 24.4 %all_to_all.21 = f32[32,1,1152]{2,1,0:T(1,128)S(1)} all-to-all(f32[32,1,1152]{2,1,0:T(1,128)S(1)} %broadcast_in_dim.26), channel_id=1, replica_groups=mesh['row'=16,'col'=32] {'col'}, dimensions={0} | all-to-all | bytes 294912 | tf_op jit(solution)/shard_map/all_to_all | solution.py:23
  202.1 0.4 copy.33
  202.5 1.0 copy.34
  (43 shorter events, 2.7 us)
Async XLA Ops:
  7.2 91.9 %copy-start = (f32[768,384]{1,0:T(8,128)S(1)}, f32[768,384]{1,0:T(8,128)}, u32[]{:S(2)}) copy-start(f32[768,384]{1,0:T(8,128)} %param.5) | copy-start | bytes 3538948
  8.7 14.0 %all-to-all-start = ((f32[16,1,384]{2,1,0:T(1,128)}), f32[16,1,384]{2,1,0:T(1,128)S(1)}, u32[]{:S(2)}, u32[]{:S(2)}) async-start(f32[16,1,384]{2,1,0:T(1,128)} %broadcast_in_dim.24), calls=%async_computation | async-start | bytes 49152 | tf_op jit(solution)/shard_map/all_to_all | solution.py:23
  16.3 82.8 %all-gather.2.cloned.1.call-start = ((), (), s32[]{:S(2)}) async-start(), calls=%async_computation.4 | async-start | bytes 3244032 | tf_op jit(solution)/shard_map/all_gather | solution.py:48
  99.0 3.4 %copy-start.1 = (f32[768,1024]{1,0:T(8,128)S(1)}, f32[768,1024]{1,0:T(8,128)}, u32[]{:S(2)}) copy-start(f32[768,1024]{1,0:T(8,128)} %all-gather.2.cloned.1.call-done) | copy-start | bytes 9437188
  104.9 7.8 %copy-start.3 = (f32[3,16,256]{2,1,0:T(8,128)S(1)}, f32[3,16,256]{2,1,0:T(8,128)}, u32[]{:S(2)}) copy-start(f32[3,16,256]{2,1,0:T(8,128)} %param.8) | copy-start | bytes 147460
  106.0 25.0 %all-to-all-start.1 = ((f32[16,48,384]{2,1,0:T(8,128)}), f32[16,48,384]{2,1,0:T(8,128)S(1)}, u32[]{:S(2)}, u32[]{:S(2)}) async-start(f32[16,48,384]{2,1,0:T(8,128)} %bitcast.17), calls=%async_computation.1 | async-start | bytes 2359296 | tf_op jit(solution)/shard_map/all_to_all | solution.py:61
  131.1 14.8 %copy-start.2 = (f32[48,384]{1,0:T(8,128)}, f32[48,384]{1,0:T(8,128)S(1)}, u32[]{:S(2)}) copy-start(f32[48,384]{1,0:T(8,128)S(1)} %reduce_sum.18) | copy-start | bytes 221188
  131.1 4.8 %collective-permute-start = (f32[24,384]{1,0:T(8,128)S(1)}, f32[24,384]{1,0:T(8,128)S(1)}, u32[]{:S(2)}, u32[]{:S(2)}) collective-permute-start(f32[24,384]{1,0:T(8,128)S(1)} %get-tuple-element.13), channel_id=1, source_target_pairs={{0,0},{1,1},{2,32},{3,33},{4,64},{5,65},{6,96},{7,97},{8,128},{9,1... | collective-permute-start | bytes 110600 | tf_op jit(solution)/shard_map/ppermute | solution.py:76
  131.8 4.8 %collective-permute-start.1 = (f32[24,384]{1,0:T(8,128)S(1)}, f32[24,384]{1,0:T(8,128)S(1)}, u32[]{:S(2)}, u32[]{:S(2)}) collective-permute-start(f32[24,384]{1,0:T(8,128)S(1)} %get-tuple-element.14), channel_id=1, source_target_pairs={{0,1},{1,0},{2,33},{3,32},{4,65},{5,64},{6,97},{7,96},{8,129},{9,1... | collective-permute-start | bytes 110600 | tf_op jit(solution)/shard_map/ppermute | solution.py:77
Sparse Core Ops, SparseCore 0:
  23.9 75.1 all-gather.1

commit v2 on v1

v2 whole, which is shorter than its diff:
```python
import jax
import jax.numpy as jnp
from jax import lax
from jax.sharding import PartitionSpec as P

TILE = 128
NSUPER = 3
NEAR = 4


def contract(left, right, left_dim, right_dim, precision=lax.Precision.HIGH):
    return lax.dot_general(
        left,
        right,
        (((left_dim,), (right_dim,)), ((), ())),
        precision=precision,
        preferred_element_type=jnp.float32,
    )


def spread(block, axis):
    count = lax.axis_size(axis)
    copies = jnp.broadcast_to(block[None], (count,) + block.shape)
    return lax.all_to_all(copies, axis, 0, 0, tiled=True)


def per_device(inverse_sep, sep_panels, chain_panels, diag_inverse, tile_list):
    rows = lax.axis_size("row")
    cols = lax.axis_size("col")
    row = lax.axis_index("row")
    col = lax.axis_index("col")
    height, width = inverse_sep.shape
    nb_cols = sep_panels.shape[2]
    nb_rows = chain_panels.shape[1]
    nb = nb_cols * cols
    cores = cols // rows
    chips = cols // cores
    far = chips // NEAR
    core = col % cores
    chip = col // cores
    tiles = height // TILE
    npair = chain_panels.shape[0]
    slab = NSUPER * nb_cols

    chain_rows = spread(chain_panels.reshape(1, npair * nb_rows * nb_cols), "col")

    listed = lax.dynamic_slice_in_dim(tile_list, row * tiles, tiles, 1).astype(jnp.float32)
    mask = jnp.broadcast_to(listed[:, :, None], (NSUPER, tiles, TILE)).reshape(NSUPER, 1, height)
    local_panel = (jnp.swapaxes(sep_panels, 1, 2) * mask).reshape(slab, height)
    far_groups = [
        [cores * (first + NEAR * i) + c for i in range(far)]
        for first in range(NEAR)
        for c in range(cores)
    ]
    own = lax.all_gather(local_panel, "col", axis=0, tiled=True, axis_index_groups=far_groups)

    chain_rows, _ = lax.optimization_barrier((chain_rows, own))
    chain_rows = chain_rows.reshape(cols, npair * nb_rows, nb_cols)
    chain_rows = jnp.transpose(chain_rows, (1, 0, 2)).reshape(npair * nb_rows, nb)
    chain_all = spread(chain_rows, "row").reshape(rows, npair, nb_rows, nb)
    chain = [chain_all[:, p].reshape(nb, nb) for p in range(npair)]

    def from_chip(block, step):
        moves = [((c + cores * step) % cols, c) for c in range(cols)]
        return lax.ppermute(block, "col", moves)

    near = [own] + [from_chip(own, step) for step in (1, 2, -1)]
    swap = [(c, c ^ 1) for c in range(cols)]
    mine = jnp.stack(near)
    theirs = lax.ppermute(mine, "col", swap)
    both = jnp.stack([jnp.where(core == 0, mine, theirs), jnp.where(core == 0, theirs, mine)])
    both = both.reshape(cores, NEAR, far, NSUPER, nb_cols, height)
    turnover = chip % NEAR
    places = []
    for place in range(NEAR):
        choice = both[:, place]
        for t in range(1, NEAR):
            choice = jnp.where(turnover == t, both[:, (place - t) % NEAR], choice)
        places.append(choice)
    ordered = jnp.stack(places)
    ordered = jnp.transpose(ordered, (3, 2, 0, 1, 4, 5)).reshape(NSUPER, nb, height)

    part = []
    for k in range(NSUPER):
        acc = contract(ordered[k], inverse_sep, 1, 0)
        for j in range(k):
            acc = acc + contract(chain[k * (k - 1) // 2 + j], part[j], 0, 0)
        part.append(-acc)
    outgoing = jnp.stack([x.reshape(rows, nb_rows, width) for x in part], axis=1)
    incoming = lax.all_to_all(
        outgoing.reshape(rows, NSUPER * nb_rows, width), "row", 0, 0, tiled=True
    )
    new_rows = jnp.sum(incoming, axis=0).reshape(NSUPER, nb_rows, width)

    solved = []
    for k in range(NSUPER):
        acc = ordered[k]
        for j in range(k):
            acc = acc - contract(chain[k * (k - 1) // 2 + j], solved[j], 0, 0)
        solved.append(acc)
    solved = jnp.concatenate(solved, axis=0).T
    place = col * nb_cols + lax.broadcasted_iota(jnp.int32, (nb_cols, nb), 0)
    unit = (lax.broadcasted_iota(jnp.int32, (nb_cols, nb), 1) == place).astype(jnp.float32)
    zero = jnp.zeros((nb_cols, nb), jnp.float32)
    cc = [contract(unit, chain[p], 1, 1, lax.Precision.HIGHEST) for p in range(npair)]
    lead = [
        jnp.concatenate([unit, -cc[0], contract(cc[2], chain[0], 1, 1) - cc[1]], axis=0),
        jnp.concatenate([zero, unit, -cc[2]], axis=0),
        jnp.concatenate([zero, zero, unit], axis=0),
    ]
    base = []
    for k in range(NSUPER):
        acc = contract(
            lax.dynamic_slice_in_dim(lead[k], row * nb_rows, nb_rows, 1), diag_inverse[k], 1, 0
        )
        for j in range(k):
            acc = acc - contract(base[j], chain[k * (k - 1) // 2 + j], 1, 0)
        base.append(acc)
    base = jnp.concatenate(base, axis=1)

    lower, upper = new_rows[:, :nb_cols], new_rows[:, nb_cols:]
    kept = jnp.where(core == 0, lower, upper).reshape(slab, width)
    sent = jnp.where(core == 0, upper, lower).reshape(slab, width)
    other = lax.ppermute(sent, "col", swap)
    wide = jnp.concatenate(
        [jnp.where(core == 0, kept, other), jnp.where(core == 0, other, kept)], axis=1
    )
    turn = [
        (r * cols + c, (c // cores) * cols + cores * r + c % cores)
        for r in range(rows)
        for c in range(cols)
    ]
    turned = lax.ppermute(wide, ("row", "col"), turn)

    inner = (base - contract(turned, solved, 1, 0)).reshape(slab, NSUPER, rows, nb_rows)
    packed = jnp.transpose(inner, (2, 0, 1, 3)).reshape(rows, 1, slab * NSUPER * nb_rows)
    summed = jnp.sum(lax.all_to_all(packed, "row", 0, 0, tiled=True), axis=0)
    whole = spread(summed, "col").reshape(cols, NSUPER, nb_cols, NSUPER, nb_rows)
    state = jnp.transpose(whole, (3, 4, 1, 0, 2)).reshape(NSUPER, nb_rows, NSUPER * nb)
    return (new_rows, state)


def solution(mesh):
    in_specs = (
        P("row", "col"),
        P(None, "row", "col"),
        P(None, "row", "col"),
        P(None, "row", None),
        P(),
    )
    out_specs = (P(None, "row", "col"), P(None, "row", None))
    return jax.shard_map(
        per_device, mesh=mesh, in_specs=in_specs, out_specs=out_specs, check_vma=False
    )
```

time: 211 us -> 184 us (0.87)
  waiting for transfers between devices: 97 us -> 26 us
  starting transfers between devices: 18.8 us -> 52.9 us
  blocking collectives: 55.3 us -> 74.5 us
  between operations: 14.6 us -> 1.19 us
  other arithmetic: 3.78 us -> 7.52 us
    all_gather x1 -> x0, waiting for transfers between devices: 75.3 us -> none  [per_device(): lax.all_gather(jnp.concatenate([local_panel, chain_cols], axis=1), 'col',...]
    all_gather x0 -> x1, blocking collectives: none -> 21 us  [per_device(): lax.all_gather(local_panel, 'col', axis=0, tiled=True, axis_index_groups=...]
    ppermute x2 -> x6, starting transfers between devices: 4.62 us -> 22.7 us  [the longest x3 12.6 us: from_chip(): return lax.ppermute(block, 'col', moves)]
    all_to_all x1 -> x2, starting transfers between devices: 7.57 us -> 23.5 us  [spread(): return lax.all_to_all(copies, axis, 0, 0, tiled=True)]
    ppermute x2 -> x6, waiting for transfers between devices: 0.63 us -> 13.7 us  [the longest x3 13.1 us: from_chip(): return lax.ppermute(block, 'col', moves)]
    all_to_all x1 -> x2, waiting for transfers between devices: 4.65 us -> 0.01 us  [spread(): return lax.all_to_all(copies, axis, 0, 0, tiled=True)]
    all_to_all x1, waiting for transfers between devices: 16.4 us -> 12.3 us  [per_device(): lax.all_to_all(outgoing.reshape(rows, NSUPER * nb_rows, width), 'row', 0,...]
    dot_general x16 -> x20, matrix products: 15.7 us -> 14.2 us  [contract(): lax.dot_general(left, right, (((left_dim,), (right_dim,)), ((), ())), pre...]
  transfers between devices with their start and end apart: 5 -> 9, of which waited for: 4 -> 5; matrix products, arithmetic and copies ran while one was open for 2% -> 7% of each run, Pallas kernels for 0% -> 0%
where the time goes in v2:
time: 184 us; the launch traced here: 183 us
  blocking collectives  74.5 us (40%)
  starting transfers between devices  52.9 us (29%)
  waiting for transfers between devices  26 us (14%)
  matrix products  14.2 us (8%)
  other arithmetic  7.52 us (4%)
  local copies, waits for them, and re-layouts  7.09 us (4%)
    all_to_all x1, blocking collectives, per_device(): summed = jnp.sum(lax.all_to_all(packed, 'row', 0, 0, tiled=True), axis=0)  29.4 us
    all_to_all x1, blocking collectives, spread(): return lax.all_to_all(copies, axis, 0, 0, tiled=True)  24.1 us
    all_to_all x2, starting transfers between devices, spread(): return lax.all_to_all(copies, axis, 0, 0, tiled=True)  23.5 us
    all_gather x1, blocking collectives, per_device(): lax.all_gather(local_panel, 'col', axis=0, tiled=True, axis_index_groups=...  21 us
    dot_general x20, matrix products, contract(): lax.dot_general(left, right, (((left_dim,), (right_dim,)), ((), ())), pre...  14.2 us
    ppermute x3, waiting for transfers between devices, from_chip(): return lax.ppermute(block, 'col', moves)  13.1 us
    ppermute x3, starting transfers between devices, from_chip(): return lax.ppermute(block, 'col', moves)  12.6 us
    all_to_all x1, waiting for transfers between devices, per_device(): lax.all_to_all(outgoing.reshape(rows, NSUPER * nb_rows, width), 'row', 0,...  12.3 us
  transfers between devices with their start and end apart: 9, of which 5 were waited for; matrix products, arithmetic and copies ran while one was open for 7% of the time, Pallas kernels for 0%

profile of v2, /device:TPU:1, one launch (start us, length us, event | category | flops | bytes accessed | tf_op | source)
XLA Modules:
  0.0 183.3 jit_solution(12270675417646038822)
XLA Ops:
  0.6 0.9 copy.27
  2.3 16.7 %all-to-all-start = ((f32[32,1,384]{2,1,0:T(1,128)}), f32[32,1,384]{2,1,0:T(1,128)S(1)}, u32[]{:S(2)}, u32[]{:S(2)}) async-start(f32[32,1,384]{2,1,0:T(1,128)} %broadcast_in_dim.31), calls=%async_computation | async-start | bytes 98304 | tf_op jit(solution)/shard_map/all_to_all | solution.py:24
  19.9 0.9 multiply_bitcast_fusion
  20.8 21.0 %all_gather.3 = f32[96,768]{1,0:T(8,128)S(1)} all-gather(f32[24,768]{1,0:T(8,128)S(1)} %multiply_bitcast_fusion), channel_id=1, replica_groups={{0,8,16,24},{1,9,17,25},{2,10,18,26},{3,11,19,27},{4,12,20,28},{5,13,21..., dimensions={0}, use_global_device_ids=true | all-gather | bytes 368640 | tf_op jit(solution)/shard_map/all_gather | solution.py:55
  42.1 1.0 broadcast_in_dim.33
  43.1 6.8 %all-to-all-start.1 = ((f32[16,48,256]{2,1,0:T(8,128)}), f32[16,48,256]{2,1,0:T(8,128)S(1)}, u32[]{:S(2)}, u32[]{:S(2)}) async-start(f32[16,48,256]{2,1,0:T(8,128)} %broadcast_in_dim.33), calls=%async_computation.1 | async-start | bytes 1572864 | tf_op jit(solution)/shard_map/all_to_all | solution.py:24
  49.9 5.6 %collective-permute-start.2 = (f32[96,768]{1,0:T(8,128)S(1)}, f32[96,768]{1,0:T(8,128)S(1)}, u32[]{:S(2)}, u32[]{:S(2)}) collective-permute-start(f32[96,768]{1,0:T(8,128)S(1)} %all_gather.3), channel_id=1, source_target_pairs={{30,0},{31,1},{0,2},{1,3},{2,4},{3,5},{4,6},{5,7},{6,8},{7,9},{8,1... | collective-permute-start | bytes 884744 | tf_op jit(solution)/shard_map/ppermute | solution.py:65
  55.4 3.7 %collective-permute-start.1 = (f32[96,768]{1,0:T(8,128)S(1)}, f32[96,768]{1,0:T(8,128)S(1)}, u32[]{:S(2)}, u32[]{:S(2)}) collective-permute-start(f32[96,768]{1,0:T(8,128)S(1)} %all_gather.3), channel_id=1, source_target_pairs={{4,0},{5,1},{6,2},{7,3},{8,4},{9,5},{10,6},{11,7},{12,8},{13,9},{1... | collective-permute-start | bytes 884744 | tf_op jit(solution)/shard_map/ppermute | solution.py:65
  59.1 3.4 %collective-permute-start = (f32[96,768]{1,0:T(8,128)S(1)}, f32[96,768]{1,0:T(8,128)S(1)}, u32[]{:S(2)}, u32[]{:S(2)}) collective-permute-start(f32[96,768]{1,0:T(8,128)S(1)} %all_gather.3), channel_id=1, source_target_pairs={{2,0},{3,1},{4,2},{5,3},{6,4},{7,5},{8,6},{9,7},{10,8},{11,9},{12,... | collective-permute-start | bytes 884744 | tf_op jit(solution)/shard_map/ppermute | solution.py:65
  62.6 0.8 fusion.19
  63.4 5.2 %collective-permute-done.1 = f32[96,768]{1,0:T(8,128)S(1)} collective-permute-done((f32[96,768]{1,0:T(8,128)S(1)}, f32[96,768]{1,0:T(8,128)S(1)}, u32[]{:S(2)}, u32[]{:S(2)}) %collective-permute-start.1) | collective-permute-done | bytes 294944 | tf_op jit(solution)/shard_map/ppermute | solution.py:65
  68.6 8.0 %collective-permute-done = f32[96,768]{1,0:T(8,128)S(1)} collective-permute-done((f32[96,768]{1,0:T(8,128)S(1)}, f32[96,768]{1,0:T(8,128)S(1)}, u32[]{:S(2)}, u32[]{:S(2)}) %collective-permute-start) | collective-permute-done | bytes 294944 | tf_op jit(solution)/shard_map/ppermute | solution.py:65
  76.5 1.1 pad_maximum_fusion
  77.7 4.9 %collective-permute-start.3 = (f32[4,96,768]{2,1,0:T(8,128)}, f32[4,96,768]{2,1,0:T(8,128)}, u32[]{:S(2)}, u32[]{:S(2)}) collective-permute-start(f32[4,96,768]{2,1,0:T(8,128)} %pad_maximum_fusion), channel_id=1, source_target_pairs={{0,1},{1,0},{2,3},{3,2},{4,5},{5,4},{6,7},{7,6},{8,9},{9,8},{10,11... | collective-permute-start | bytes 3538952 | tf_op jit(solution)/shard_map/ppermute | solution.py:70
  82.9 0.9 fusion.21
  84.2 0.9 convolution_subtract_fusion.6
  85.4 1.5 broadcast_select_fusion.1
  87.9 0.8 convolution_negate_fusion
  91.0 0.8 fusion.7
  91.9 1.1 pad_maximum_fusion.1
  93.0 6.7 %all-to-all-start.2 = ((f32[16,48,384]{2,1,0:T(8,128)}), f32[16,48,384]{2,1,0:T(8,128)}, u32[]{:S(2)}, u32[]{:S(2)}) async-start(f32[16,48,384]{2,1,0:T(8,128)} %bitcast.128), calls=%async_computation.2 | async-start | bytes 2359296 | tf_op jit(solution)/shard_map/all_to_all | solution.py:90
  99.7 1.0 fusion.23
  100.7 0.9 convolution_subtract_fusion.4
  101.7 0.9 convolution_subtract_fusion.5
  104.0 1.4 convolution_subtract_fusion.1
  105.4 12.3 %all-to-all-done.2 = f32[16,48,384]{2,1,0:T(8,128)} async-done(((f32[16,48,384]{2,1,0:T(8,128)}), f32[16,48,384]{2,1,0:T(8,128)}, u32[]{:S(2)}, u32[]{:S(2)}) %all-to-all-start.2) | async-done | bytes 1179680 | tf_op jit(solution)/shard_map/all_to_all | solution.py:90
  117.7 1.3 reduce_sum.18
  119.1 4.4 %collective-permute-start.4 = (f32[24,384]{1,0:T(8,128)S(1)}, f32[24,384]{1,0:T(8,128)S(1)}, u32[]{:S(2)}, u32[]{:S(2)}) collective-permute-start(f32[24,384]{1,0:T(8,128)S(1)} %select_bitcast_fusion), channel_id=1, source_target_pairs={{0,1},{1,0},{2,3},{3,2},{4,5},{5,4},{6,7},{7,6},{8,9},{9,8},{10,11... | collective-permute-start | bytes 110600 | tf_op jit(solution)/shard_map/ppermute | solution.py:124
  125.9 1.1 fusion.9
  128.0 29.4 %all_to_all.25 = f32[16,1,1152]{2,1,0:T(1,128)S(1)} all-to-all(f32[16,1,1152]{2,1,0:T(1,128)S(1)} %reshape.220), channel_id=1, replica_groups=mesh['row'=16,'col'=32] {'row'}, dimensions={0} | all-to-all | bytes 147456 | tf_op jit(solution)/shard_map/all_to_all | solution.py:137
  157.5 24.1 %all_to_all.26 = f32[32,1,1152]{2,1,0:T(1,128)S(1)} all-to-all(f32[32,1,1152]{2,1,0:T(1,128)S(1)} %broadcast_in_dim.35), channel_id=1, replica_groups=mesh['row'=16,'col'=32] {'col'}, dimensions={0} | all-to-all | bytes 294912 | tf_op jit(solution)/shard_map/all_to_all | solution.py:24
  182.3 1.0 copy.39
  (77 shorter events, 11.8 us)
Async XLA Ops:
  0.6 87.2 %copy-start = (f32[768,384]{1,0:T(8,128)S(1)}, f32[768,384]{1,0:T(8,128)}, u32[]{:S(2)}) copy-start(f32[768,384]{1,0:T(8,128)} %param.5) | copy-start | bytes 3538948
  2.3 39.5 %all-to-all-start = ((f32[32,1,384]{2,1,0:T(1,128)}), f32[32,1,384]{2,1,0:T(1,128)S(1)}, u32[]{:S(2)}, u32[]{:S(2)}) async-start(f32[32,1,384]{2,1,0:T(1,128)} %broadcast_in_dim.31), calls=%async_computation | async-start | bytes 98304 | tf_op jit(solution)/shard_map/all_to_all | solution.py:24
  42.1 20.4 %copy-start.14 = (f32[3,16,256]{2,1,0:T(8,128)S(1)}, f32[3,16,256]{2,1,0:T(8,128)}, u32[]{:S(2)}) copy-start(f32[3,16,256]{2,1,0:T(8,128)} %param.8) | copy-start | bytes 147460
  43.1 39.5 %all-to-all-start.1 = ((f32[16,48,256]{2,1,0:T(8,128)}), f32[16,48,256]{2,1,0:T(8,128)S(1)}, u32[]{:S(2)}, u32[]{:S(2)}) async-start(f32[16,48,256]{2,1,0:T(8,128)} %broadcast_in_dim.33), calls=%async_computation.1 | async-start | bytes 1572864 | tf_op jit(solution)/shard_map/all_to_all | solution.py:24
  49.9 13.5 %collective-permute-start.2 = (f32[96,768]{1,0:T(8,128)S(1)}, f32[96,768]{1,0:T(8,128)S(1)}, u32[]{:S(2)}, u32[]{:S(2)}) collective-permute-start(f32[96,768]{1,0:T(8,128)S(1)} %all_gather.3), channel_id=1, source_target_pairs={{30,0},{31,1},{0,2},{1,3},{2,4},{3,5},{4,6},{5,7},{6,8},{7,9},{8,1... | collective-permute-start | bytes 884744 | tf_op jit(solution)/shard_map/ppermute | solution.py:65
  55.4 13.1 %collective-permute-start.1 = (f32[96,768]{1,0:T(8,128)S(1)}, f32[96,768]{1,0:T(8,128)S(1)}, u32[]{:S(2)}, u32[]{:S(2)}) collective-permute-start(f32[96,768]{1,0:T(8,128)S(1)} %all_gather.3), channel_id=1, source_target_pairs={{4,0},{5,1},{6,2},{7,3},{8,4},{9,5},{10,6},{11,7},{12,8},{13,9},{1... | collective-permute-start | bytes 884744 | tf_op jit(solution)/shard_map/ppermute | solution.py:65
  59.1 17.4 %collective-permute-start = (f32[96,768]{1,0:T(8,128)S(1)}, f32[96,768]{1,0:T(8,128)S(1)}, u32[]{:S(2)}, u32[]{:S(2)}) collective-permute-start(f32[96,768]{1,0:T(8,128)S(1)} %all_gather.3), channel_id=1, source_target_pairs={{2,0},{3,1},{4,2},{5,3},{6,4},{7,5},{8,6},{9,7},{10,8},{11,9},{12,... | collective-permute-start | bytes 884744 | tf_op jit(solution)/shard_map/ppermute | solution.py:65
  68.6 9.1 %copy-start.4 = (f32[96,768]{1,0:T(8,128)}, f32[96,768]{1,0:T(8,128)S(1)}, u32[]{:S(2)}) copy-start(f32[96,768]{1,0:T(8,128)S(1)} %collective-permute-done.1) | copy-start | bytes 884740
  76.5 1.1 copy-start.6
  77.7 7.7 %collective-permute-start.3 = (f32[4,96,768]{2,1,0:T(8,128)}, f32[4,96,768]{2,1,0:T(8,128)}, u32[]{:S(2)}, u32[]{:S(2)}) collective-permute-start(f32[4,96,768]{2,1,0:T(8,128)} %pad_maximum_fusion), channel_id=1, source_target_pairs={{0,1},{1,0},{2,3},{3,2},{4,5},{5,4},{6,7},{7,6},{8,9},{9,8},{10,11... | collective-permute-start | bytes 3538952 | tf_op jit(solution)/shard_map/ppermute | solution.py:70
  82.6 2.8 %copy-start.5 = (f32[96,768]{1,0:T(8,128)S(1)}, f32[96,768]{1,0:T(8,128)}, u32[]{:S(2)}) copy-start(f32[96,768]{1,0:T(8,128)} %copy-done.4) | copy-start | bytes 884740
  82.6 2.8 %copy-start.7 = (f32[96,768]{1,0:T(8,128)S(1)}, f32[96,768]{1,0:T(8,128)}, u32[]{:S(2)}) copy-start(f32[96,768]{1,0:T(8,128)} %copy-done.6) | copy-start | bytes 884740
  91.0 0.9 copy-start.1
  93.0 24.8 %all-to-all-start.2 = ((f32[16,48,384]{2,1,0:T(8,128)}), f32[16,48,384]{2,1,0:T(8,128)}, u32[]{:S(2)}, u32[]{:S(2)}) async-start(f32[16,48,384]{2,1,0:T(8,128)} %bitcast.128), calls=%async_computation.2 | async-start | bytes 2359296 | tf_op jit(solution)/shard_map/all_to_all | solution.py:90
  99.7 4.3 %copy-start.2 = (f32[1,4,4,2,8,768]{5,4,3,2,1,0:T(8,128)S(1)}, f32[1,4,4,2,8,768]{5,4,3,2,1,0:T(8,128)}, u32[]{:S(2)}) copy-start(f32[1,4,4,2,8,768]{5,4,3,2,1,0:T(8,128)} %copy-done.1) | copy-start | bytes 2359300
  100.7 0.9 copy-start.9
  102.6 0.6 copy-start.11
  119.1 5.3 %copy-start.8 = (f32[48,384]{1,0:T(8,128)}, f32[48,384]{1,0:T(8,128)S(1)}, u32[]{:S(2)}) copy-start(f32[48,384]{1,0:T(8,128)S(1)} %reduce_sum.18) | copy-start | bytes 221188
  119.1 6.1 %copy-start.3 = (f32[256,768]{1,0:T(8,128)S(1)}, f32[256,768]{1,0:T(8,128)}, u32[]{:S(2)}) copy-start(f32[256,768]{1,0:T(8,128)} %convolution_subtract_fusion.1) | copy-start | bytes 2359300
  119.1 5.2 %collective-permute-start.4 = (f32[24,384]{1,0:T(8,128)S(1)}, f32[24,384]{1,0:T(8,128)S(1)}, u32[]{:S(2)}, u32[]{:S(2)}) collective-permute-start(f32[24,384]{1,0:T(8,128)S(1)} %select_bitcast_fusion), channel_id=1, source_target_pairs={{0,1},{1,0},{2,3},{3,2},{4,5},{5,4},{6,7},{7,6},{8,9},{9,8},{10,11... | collective-permute-start | bytes 110600 | tf_op jit(solution)/shard_map/ppermute | solution.py:124
  124.4 1.5 copy-start.10
  124.4 1.5 copy-start.12
  124.4 1.5 copy-start.13
  124.4 1.4 collective-permute-start.5

commit v3 on v2

--- a/solution.py
+++ b/solution.py
@@ -2,6 +2,7 @@
 import jax.numpy as jnp
 from jax import lax
 from jax.sharding import PartitionSpec as P
+
 
 TILE = 128
 NSUPER = 3
@@ -47,6 +48,21 @@
     listed = lax.dynamic_slice_in_dim(tile_list, row * tiles, tiles, 1).astype(jnp.float32)
     mask = jnp.broadcast_to(listed[:, :, None], (NSUPER, tiles, TILE)).reshape(NSUPER, 1, height)
     local_panel = (jnp.swapaxes(sep_panels, 1, 2) * mask).reshape(slab, height)
+    swap = [(c, c ^ 1) for c in range(cols)]
+    turn = [
+        (r * cols + c, (c // cores) * cols + cores * r + c % cores)
+        for r in range(rows)
+        for c in range(cols)
+    ]
+    turned = lax.ppermute(local_panel, ("row", "col"), turn)
+    left, right = turned[:, :width], turned[:, width:]
+    kept = jnp.where(core == 0, left, right)
+    other = lax.ppermute(jnp.where(core == 0, right, left), "col", swap)
+    pieces = jnp.stack([jnp.where(core == 0, kept, other), jnp.where(core == 0, other, kept)])
+    col_panel = spread(pieces.reshape(cores * slab, width), "row")
+    col_panel = col_panel.reshape(rows, cores, NSUPER, nb_cols, width)
+    col_panel = [col_panel[:, :, k].reshape(nb, width) for k in range(NSUPER)]
+
     far_groups = [
         [cores * (first + NEAR * i) + c for i in range(far)]
         for first in range(NEAR)
@@ -57,7 +73,15 @@
     chain_rows, _ = lax.optimization_barrier((chain_rows, own))
     chain_rows = chain_rows.reshape(cols, npair * nb_rows, nb_cols)
     chain_rows = jnp.transpose(chain_rows, (1, 0, 2)).reshape(npair * nb_rows, nb)
-    chain_all = spread(chain_rows, "row").reshape(rows, npair, nb_rows, nb)
+    diag_cols = lax.dynamic_slice_in_dim(diag_inverse, col * nb_cols, nb_cols, 2)
+    extra = NSUPER * nb_rows * nb_cols
+    pad = -extra % (8 * nb)
+    diag_cols = jnp.pad(diag_cols.reshape(extra), (0, pad)).reshape(-1, nb)
+    chain_all = spread(jnp.concatenate([chain_rows, diag_cols], axis=0), "row")
+    diag_slab = chain_all[:, npair * nb_rows :].reshape(rows, extra + pad)[:, :extra]
+    diag_slab = diag_slab.reshape(rows, NSUPER, nb_rows, nb_cols)
+    diag_slab = [diag_slab[:, k].reshape(nb, nb_cols) for k in range(NSUPER)]
+    chain_all = chain_all[:, : npair * nb_rows].reshape(rows, npair, nb_rows, nb)
     chain = [chain_all[:, p].reshape(nb, nb) for p in range(npair)]
 
     def from_chip(block, step):
@@ -65,7 +89,6 @@
         return lax.ppermute(block, "col", moves)
 
     near = [own] + [from_chip(own, step) for step in (1, 2, -1)]
-    swap = [(c, c ^ 1) for c in range(cols)]
     mine = jnp.stack(near)
     theirs = lax.ppermute(mine, "col", swap)
     both = jnp.stack([jnp.where(core == 0, mine, theirs), jnp.where(core == 0, theirs, mine)])
@@ -92,51 +115,36 @@
     )
     new_rows = jnp.sum(incoming, axis=0).reshape(NSUPER, nb_rows, width)
 
+    exact = lax.Precision.HIGHEST
     solved = []
     for k in range(NSUPER):
-        acc = ordered[k]
+        acc = col_panel[k]
         for j in range(k):
             acc = acc - contract(chain[k * (k - 1) // 2 + j], solved[j], 0, 0)
         solved.append(acc)
-    solved = jnp.concatenate(solved, axis=0).T
-    place = col * nb_cols + lax.broadcasted_iota(jnp.int32, (nb_cols, nb), 0)
-    unit = (lax.broadcasted_iota(jnp.int32, (nb_cols, nb), 1) == place).astype(jnp.float32)
-    zero = jnp.zeros((nb_cols, nb), jnp.float32)
-    cc = [contract(unit, chain[p], 1, 1, lax.Precision.HIGHEST) for p in range(npair)]
+    solved = jnp.concatenate(solved, axis=0)
+    place = row * nb_rows + lax.broadcasted_iota(jnp.int32, (nb_rows, nb), 0)
+    unit = (lax.broadcasted_iota(jnp.int32, (nb_rows, nb), 1) == place).astype(jnp.float32)
+    zero = jnp.zeros((nb_rows, nb), jnp.float32)
+    cc = [contract(unit, chain[p], 1, 1, exact) for p in range(npair)]
     lead = [
-        jnp.concatenate([unit, -cc[0], contract(cc[2], chain[0], 1, 1) - cc[1]], axis=0),
+        jnp.concatenate([unit, -cc[0], contract(cc[2], chain[0], 1, 1, exact) - cc[1]], axis=0),
         jnp.concatenate([zero, unit, -cc[2]], axis=0),
         jnp.concatenate([zero, zero, unit], axis=0),
     ]
     base = []
     for k in range(NSUPER):
-        acc = contract(
-            lax.dynamic_slice_in_dim(lead[k], row * nb_rows, nb_rows, 1), diag_inverse[k], 1, 0
-        )
+        part_lead = lax.dynamic_slice_in_dim(lead[k], col * nb_cols, nb_cols, 1)
+        acc = contract(part_lead, diag_slab[k], 1, 1, exact)
         for j in range(k):
-            acc = acc - contract(base[j], chain[k * (k - 1) // 2 + j], 1, 0)
+            acc = acc - contract(base[j], chain[k * (k - 1) // 2 + j], 1, 0, exact)
         base.append(acc)
     base = jnp.concatenate(base, axis=1)
 
-    lower, upper = new_rows[:, :nb_cols], new_rows[:, nb_cols:]
-    kept = jnp.where(core == 0, lower, upper).reshape(slab, width)
-    sent = jnp.where(core == 0, upper, lower).reshape(slab, width)
-    other = lax.ppermute(sent, "col", swap)
-    wide = jnp.concatenate(
-        [jnp.where(core == 0, kept, other), jnp.where(core == 0, other, kept)], axis=1
-    )
-    turn = [
-        (r * cols + c, (c // cores) * cols + cores * r + c % cores)
-        for r in range(rows)
-        for c in range(cols)
-    ]
-    turned = lax.ppermute(wide, ("row", "col"), turn)
-
-    inner = (base - contract(turned, solved, 1, 0)).reshape(slab, NSUPER, rows, nb_rows)
-    packed = jnp.transpose(inner, (2, 0, 1, 3)).reshape(rows, 1, slab * NSUPER * nb_rows)
-    summed = jnp.sum(lax.all_to_all(packed, "row", 0, 0, tiled=True), axis=0)
-    whole = spread(summed, "col").reshape(cols, NSUPER, nb_cols, NSUPER, nb_rows)
-    state = jnp.transpose(whole, (3, 4, 1, 0, 2)).reshape(NSUPER, nb_rows, NSUPER * nb)
+    inner = base - contract(new_rows.reshape(NSUPER * nb_rows, width), solved, 1, 1)
+    share = NSUPER * nb_rows * NSUPER * nb // cols
+    summed = jnp.sum(lax.all_to_all(inner.reshape(cols, 1, share), "col", 0, 0, tiled=True), axis=0)
+    state = spread(summed, "col").reshape(NSUPER, nb_rows, NSUPER * nb)
     return (new_rows, state)
 
 
@@ -149,6 +157,7 @@
         P(),
     )
     out_specs = (P(None, "row", "col"), P(None, "row", None))
+
     return jax.shard_map(
         per_device, mesh=mesh, in_specs=in_specs, out_specs=out_specs, check_vma=False
     )

time: 184 us -> 198 us (1.076)
  local copies, waits for them, and re-layouts: 7.09 us -> 14.7 us
  waiting for transfers between devices: 26 us -> 31.4 us
  blocking collectives: 74.5 us -> 76.7 us
    all_to_all x2 -> x3, waiting for transfers between devices: 0.01 us -> 17.1 us  [spread(): return lax.all_to_all(copies, axis, 0, 0, tiled=True)]
    ppermute x3, waiting for transfers between devices: 13.1 us -> 0.01 us  [from_chip(): return lax.ppermute(block, 'col', moves)]
    all_to_all x2 -> x3, starting transfers between devices: 23.5 us -> 29.3 us  [spread(): return lax.all_to_all(copies, axis, 0, 0, tiled=True)]
    slice x0 -> x10, local copies, waits for them, and re-layouts: none -> 4.75 us  [the longest x4 2.59 us: per_device(): diag_slab = [diag_slab[:, k].reshape(nb, nb_cols) for k in range(NSUPER)]]
    all_gather x1, blocking collectives: 21 us -> 25.3 us  [per_device(): lax.all_gather(local_panel, 'col', axis=0, tiled=True, axis_index_groups=...]
    ppermute x3, starting transfers between devices: 12.6 us -> 8.87 us  [from_chip(): return lax.ppermute(block, 'col', moves)]
    all_to_all x1, blocking collectives: 24.1 us -> 20.8 us  [spread(): return lax.all_to_all(copies, axis, 0, 0, tiled=True)]
    ppermute x1, starting transfers between devices: 4.91 us -> 2.25 us  [per_device(): theirs = lax.ppermute(mine, 'col', swap)]
  transfers between devices with their start and end apart: 9 -> 10, of which waited for: 5 -> 4; matrix products, arithmetic and copies ran while one was open for 7% -> 15% of each run, Pallas kernels for 0% -> 0%
where the time goes in v3:
time: 198 us; the launch traced here: 197 us
  blocking collectives  76.7 us (39%)
  starting transfers between devices  51.5 us (26%)
  waiting for transfers between devices  31.4 us (16%)
  local copies, waits for them, and re-layouts  14.7 us (7%)
  matrix products  13 us (7%)
  other arithmetic  8.16 us (4%)
    all_to_all x1, blocking collectives, per_device(): lax.all_to_all(inner.reshape(cols, 1, share), 'col', 0, 0, tiled=True)  30.6 us
    all_to_all x3, starting transfers between devices, spread(): return lax.all_to_all(copies, axis, 0, 0, tiled=True)  29.3 us
    all_gather x1, blocking collectives, per_device(): lax.all_gather(local_panel, 'col', axis=0, tiled=True, axis_index_groups=...  25.3 us
    all_to_all x1, blocking collectives, spread(): return lax.all_to_all(copies, axis, 0, 0, tiled=True)  20.8 us
    all_to_all x3, waiting for transfers between devices, spread(): return lax.all_to_all(copies, axis, 0, 0, tiled=True)  17.1 us
    all_to_all x1, waiting for transfers between devices, per_device(): lax.all_to_all(outgoing.reshape(rows, NSUPER * nb_rows, width), 'row', 0,...  14 us
    dot_general x20, matrix products, contract(): lax.dot_general(left, right, (((left_dim,), (right_dim,)), ((), ())), pre...  13 us
    ppermute x3, starting transfers between devices, from_chip(): return lax.ppermute(block, 'col', moves)  8.87 us
  transfers between devices with their start and end apart: 10, of which 4 were waited for; matrix products, arithmetic and copies ran while one was open for 15% of the time, Pallas kernels for 0%

profile of v3, /device:TPU:1, one launch (start us, length us, event | category | flops | bytes accessed | tf_op | source)
XLA Modules:
  0.0 196.8 jit_solution(12628198402915811900)
XLA Ops:
  1.6 0.9 multiply_bitcast_fusion
  2.5 25.3 %all_gather.3 = f32[96,768]{1,0:T(8,128)S(1)} all-gather(f32[24,768]{1,0:T(8,128)S(1)} %multiply_bitcast_fusion), channel_id=1, replica_groups={{0,8,16,24},{1,9,17,25},{2,10,18,26},{3,11,19,27},{4,12,20,28},{5,13,21..., dimensions={0}, use_global_device_ids=true | all-gather | bytes 368640 | tf_op jit(solution)/shard_map/all_gather | solution.py:71
  27.8 2.9 %collective-permute-start.2 = (f32[96,768]{1,0:T(8,128)S(1)}, f32[96,768]{1,0:T(8,128)S(1)}, u32[]{:S(2)}, u32[]{:S(2)}) collective-permute-start(f32[96,768]{1,0:T(8,128)S(1)} %all_gather.3), channel_id=1, source_target_pairs={{30,0},{31,1},{0,2},{1,3},{2,4},{3,5},{4,6},{5,7},{6,8},{7,9},{8,1... | collective-permute-start | bytes 884744 | tf_op jit(solution)/shard_map/ppermute | solution.py:89
  30.7 4.1 %collective-permute-start.1 = (f32[96,768]{1,0:T(8,128)S(1)}, f32[96,768]{1,0:T(8,128)S(1)}, u32[]{:S(2)}, u32[]{:S(2)}) collective-permute-start(f32[96,768]{1,0:T(8,128)S(1)} %all_gather.3), channel_id=1, source_target_pairs={{4,0},{5,1},{6,2},{7,3},{8,4},{9,5},{10,6},{11,7},{12,8},{13,9},{1... | collective-permute-start | bytes 884744 | tf_op jit(solution)/shard_map/ppermute | solution.py:89
  34.8 1.9 collective-permute-start
  38.9 20.7 %all-to-all-start = ((f32[32,1,384]{2,1,0:T(1,128)}), f32[32,1,384]{2,1,0:T(1,128)S(1)}, u32[]{:S(2)}, u32[]{:S(2)}) async-start(f32[32,1,384]{2,1,0:T(1,128)} %broadcast_in_dim.18), calls=%async_computation | async-start | bytes 98304 | tf_op jit(solution)/shard_map/all_to_all | solution.py:25
  60.6 11.4 %all-to-all-done = f32[32,1,384]{2,1,0:T(1,128)S(1)} async-done(((f32[32,1,384]{2,1,0:T(1,128)}), f32[32,1,384]{2,1,0:T(1,128)S(1)}, u32[]{:S(2)}, u32[]{:S(2)}) %all-to-all-start) | async-done | bytes 49184 | tf_op jit(solution)/shard_map/all_to_all | solution.py:25
  72.4 1.0 broadcast_in_dim.38
  73.4 4.2 %all-to-all-start.1 = ((f32[16,56,256]{2,1,0:T(8,128)}), f32[16,56,256]{2,1,0:T(8,128)S(1)}, u32[]{:S(2)}, u32[]{:S(2)}) async-start(f32[16,56,256]{2,1,0:T(8,128)} %broadcast_in_dim.38), calls=%async_computation.1 | async-start | bytes 1835008 | tf_op jit(solution)/shard_map/all_to_all | solution.py:25
  77.7 3.7 %collective-permute-start.5 = (f32[24,384]{1,0:T(8,128)S(1)}, f32[24,384]{1,0:T(8,128)S(1)}, u32[]{:S(2)}, u32[]{:S(2)}) collective-permute-start(f32[24,384]{1,0:T(8,128)S(1)} %slice_select_fusion), channel_id=1, source_target_pairs={{0,1},{1,0},{2,3},{3,2},{4,5},{5,4},{6,7},{7,6},{8,9},{9,8},{10,11... | collective-permute-start | bytes 110600 | tf_op jit(solution)/shard_map/ppermute | solution.py:60
  82.3 1.3 pad_maximum_fusion
  83.6 2.3 %collective-permute-start.3 = (f32[4,96,768]{2,1,0:T(8,128)}, f32[4,96,768]{2,1,0:T(8,128)}, u32[]{:S(2)}, u32[]{:S(2)}) collective-permute-start(f32[4,96,768]{2,1,0:T(8,128)} %pad_maximum_fusion), channel_id=1, source_target_pairs={{0,1},{1,0},{2,3},{3,2},{4,5},{5,4},{6,7},{7,6},{8,9},{9,8},{10,11... | collective-permute-start | bytes 3538952 | tf_op jit(solution)/shard_map/ppermute | solution.py:93
  85.9 5.7 %all-to-all-done.1 = f32[16,56,256]{2,1,0:T(8,128)S(1)} async-done(((f32[16,56,256]{2,1,0:T(8,128)}), f32[16,56,256]{2,1,0:T(8,128)S(1)}, u32[]{:S(2)}, u32[]{:S(2)}) %all-to-all-start.1) | async-done | bytes 917536 | tf_op jit(solution)/shard_map/all_to_all | solution.py:25
  91.6 1.2 broadcast_in_dim.41
  92.9 4.3 %all-to-all-start.3 = ((f32[16,48,384]{2,1,0:T(8,128)}), f32[16,48,384]{2,1,0:T(8,128)S(1)}, u32[]{:S(2)}, u32[]{:S(2)}) async-start(f32[16,48,384]{2,1,0:T(8,128)} %broadcast_in_dim.41), calls=%async_computation.3 | async-start | bytes 2359296 | tf_op jit(solution)/shard_map/all_to_all | solution.py:25
  97.3 1.1 slice-done
  98.4 1.3 copy.67
  99.7 0.9 slice.113
  102.9 0.9 fusion.19
  103.8 0.9 copy.63
  105.4 0.9 copy.64
  107.1 0.9 convolution_subtract_fusion.6
  108.0 1.0 fusion.26
  109.0 1.0 fusion.22
  110.0 1.0 convolution_subtract_fusion.4
  111.4 1.5 broadcast_select_fusion.1
  117.8 1.1 pad_maximum_fusion.1
  118.9 6.7 %all-to-all-start.2 = ((f32[16,48,384]{2,1,0:T(8,128)}), f32[16,48,384]{2,1,0:T(8,128)}, u32[]{:S(2)}, u32[]{:S(2)}) async-start(f32[16,48,384]{2,1,0:T(8,128)} %bitcast.128), calls=%async_computation.2 | async-start | bytes 2359296 | tf_op jit(solution)/shard_map/all_to_all | solution.py:113
  128.0 14.0 %all-to-all-done.2 = f32[16,48,384]{2,1,0:T(8,128)} async-done(((f32[16,48,384]{2,1,0:T(8,128)}), f32[16,48,384]{2,1,0:T(8,128)}, u32[]{:S(2)}, u32[]{:S(2)}) %all-to-all-start.2) | async-done | bytes 1179680 | tf_op jit(solution)/shard_map/all_to_all | solution.py:113
  141.9 1.3 reduce_sum.18
  144.1 30.6 %all_to_all.30 = f32[32,1,1152]{2,1,0:T(1,128)S(1)} all-to-all(f32[32,1,1152]{2,1,0:T(1,128)S(1)} %reshape.229), channel_id=1, replica_groups=mesh['row'=16,'col'=32] {'col'}, dimensions={0} | all-to-all | bytes 294912 | tf_op jit(solution)/shard_map/all_to_all | solution.py:146
  174.9 20.8 %all_to_all.31 = f32[32,1,1152]{2,1,0:T(1,128)S(1)} all-to-all(f32[32,1,1152]{2,1,0:T(1,128)S(1)} %broadcast_in_dim.42), channel_id=1, replica_groups=mesh['row'=16,'col'=32] {'col'}, dimensions={0} | all-to-all | bytes 294912 | tf_op jit(solution)/shard_map/all_to_all | solution.py:25
  (100 shorter events, 18.5 us)
Async XLA Ops:
  0.6 113.3 %copy-start = (f32[768,384]{1,0:T(8,128)S(1)}, f32[768,384]{1,0:T(8,128)}, u32[]{:S(2)}) copy-start(f32[768,384]{1,0:T(8,128)} %param.5) | copy-start | bytes 3538948
  27.8 54.5 %copy-start.2 = (f32[96,768]{1,0:T(8,128)}, f32[96,768]{1,0:T(8,128)S(1)}, u32[]{:S(2)}) copy-start(f32[96,768]{1,0:T(8,128)S(1)} %all_gather.3) | copy-start | bytes 884740
  27.8 54.4 %collective-permute-start.2 = (f32[96,768]{1,0:T(8,128)S(1)}, f32[96,768]{1,0:T(8,128)S(1)}, u32[]{:S(2)}, u32[]{:S(2)}) collective-permute-start(f32[96,768]{1,0:T(8,128)S(1)} %all_gather.3), channel_id=1, source_target_pairs={{30,0},{31,1},{0,2},{1,3},{2,4},{3,5},{4,6},{5,7},{6,8},{7,9},{8,1... | collective-permute-start | bytes 884744 | tf_op jit(solution)/shard_map/ppermute | solution.py:89
  30.7 51.6 %collective-permute-start.1 = (f32[96,768]{1,0:T(8,128)S(1)}, f32[96,768]{1,0:T(8,128)S(1)}, u32[]{:S(2)}, u32[]{:S(2)}) collective-permute-start(f32[96,768]{1,0:T(8,128)S(1)} %all_gather.3), channel_id=1, source_target_pairs={{4,0},{5,1},{6,2},{7,3},{8,4},{9,5},{10,6},{11,7},{12,8},{13,9},{1... | collective-permute-start | bytes 884744 | tf_op jit(solution)/shard_map/ppermute | solution.py:89
  34.8 47.5 %collective-permute-start = (f32[96,768]{1,0:T(8,128)S(1)}, f32[96,768]{1,0:T(8,128)S(1)}, u32[]{:S(2)}, u32[]{:S(2)}) collective-permute-start(f32[96,768]{1,0:T(8,128)S(1)} %all_gather.3), channel_id=1, source_target_pairs={{2,0},{3,1},{4,2},{5,3},{6,4},{7,5},{8,6},{9,7},{10,8},{11,9},{12,... | collective-permute-start | bytes 884744 | tf_op jit(solution)/shard_map/ppermute | solution.py:89
  36.7 40.9 %collective-permute-start.4 = (f32[24,768]{1,0:T(8,128)S(1)}, f32[24,768]{1,0:T(8,128)S(1)}, u32[]{:S(2)}, u32[]{:S(2)}) collective-permute-start(f32[24,768]{1,0:T(8,128)S(1)} %multiply_bitcast_fusion), channel_id=1, source_target_pairs={{0,0},{1,1},{2,32},{3,33},{4,64},{5,65},{6,96},{7,97},{8,128},{9,1... | collective-permute-start | bytes 221192 | tf_op jit(solution)/shard_map/ppermute | solution.py:57
  38.9 33.1 %all-to-all-start = ((f32[32,1,384]{2,1,0:T(1,128)}), f32[32,1,384]{2,1,0:T(1,128)S(1)}, u32[]{:S(2)}, u32[]{:S(2)}) async-start(f32[32,1,384]{2,1,0:T(1,128)} %broadcast_in_dim.18), calls=%async_computation | async-start | bytes 98304 | tf_op jit(solution)/shard_map/all_to_all | solution.py:25
  60.6 41.8 %copy-start.16 = (s32[16]{0:T(128)}, s32[16]{0:T(128)S(1)}, u32[]{:S(2)}) copy-start(s32[16]{0:T(128)S(1)} %iota_add_fusion) | copy-start | bytes 196
  73.4 18.2 %all-to-all-start.1 = ((f32[16,56,256]{2,1,0:T(8,128)}), f32[16,56,256]{2,1,0:T(8,128)S(1)}, u32[]{:S(2)}, u32[]{:S(2)}) async-start(f32[16,56,256]{2,1,0:T(8,128)} %broadcast_in_dim.38), calls=%async_computation.1 | async-start | bytes 1835008 | tf_op jit(solution)/shard_map/all_to_all | solution.py:25
  77.7 4.6 %collective-permute-start.5 = (f32[24,384]{1,0:T(8,128)S(1)}, f32[24,384]{1,0:T(8,128)S(1)}, u32[]{:S(2)}, u32[]{:S(2)}) collective-permute-start(f32[24,384]{1,0:T(8,128)S(1)} %slice_select_fusion), channel_id=1, source_target_pairs={{0,1},{1,0},{2,3},{3,2},{4,5},{5,4},{6,7},{7,6},{8,9},{9,8},{10,11... | collective-permute-start | bytes 110600 | tf_op jit(solution)/shard_map/ppermute | solution.py:60
  82.3 1.3 copy-start.4
  82.3 1.3 copy-start.6
  82.3 1.3 copy-start.8
  83.6 27.7 %collective-permute-start.3 = (f32[4,96,768]{2,1,0:T(8,128)}, f32[4,96,768]{2,1,0:T(8,128)}, u32[]{:S(2)}, u32[]{:S(2)}) collective-permute-start(f32[4,96,768]{2,1,0:T(8,128)} %pad_maximum_fusion), channel_id=1, source_target_pairs={{0,1},{1,0},{2,3},{3,2},{4,5},{5,4},{6,7},{7,6},{8,9},{9,8},{10,11... | collective-permute-start | bytes 3538952 | tf_op jit(solution)/shard_map/ppermute | solution.py:93
  91.6 1.3 copy-start.1
  92.9 26.0 %all-to-all-start.3 = ((f32[16,48,384]{2,1,0:T(8,128)}), f32[16,48,384]{2,1,0:T(8,128)S(1)}, u32[]{:S(2)}, u32[]{:S(2)}) async-start(f32[16,48,384]{2,1,0:T(8,128)} %broadcast_in_dim.41), calls=%async_computation.3 | async-start | bytes 2359296 | tf_op jit(solution)/shard_map/all_to_all | solution.py:25
  97.2 1.1 slice-start
  97.2 1.2 slice-start.1
  102.4 8.9 %copy-start.3 = (f32[96,768]{1,0:T(8,128)S(1)}, f32[96,768]{1,0:T(8,128)}, u32[]{:S(2)}) copy-start(f32[96,768]{1,0:T(8,128)} %copy-done.2) | copy-start | bytes 884740
  107.0 4.3 %copy-start.5 = (f32[96,768]{1,0:T(8,128)S(1)}, f32[96,768]{1,0:T(8,128)}, u32[]{:S(2)}) copy-start(f32[96,768]{1,0:T(8,128)} %copy-done.4) | copy-start | bytes 884740
  107.1 4.3 %copy-start.7 = (f32[96,768]{1,0:T(8,128)S(1)}, f32[96,768]{1,0:T(8,128)}, u32[]{:S(2)}) copy-start(f32[96,768]{1,0:T(8,128)} %copy-done.6) | copy-start | bytes 884740
  107.1 4.3 %copy-start.9 = (f32[96,768]{1,0:T(8,128)S(1)}, f32[96,768]{1,0:T(8,128)}, u32[]{:S(2)}) copy-start(f32[96,768]{1,0:T(8,128)} %copy-done.8) | copy-start | bytes 884740
  109.0 2.3 %copy-start.10 = (f32[48,256]{1,0:T(8,128)}, f32[48,256]{1,0:T(8,128)S(1)}, u32[]{:S(2)}) copy-start(f32[48,256]{1,0:T(8,128)S(1)} %fusion.26) | copy-start | bytes 147460
  111.3 14.3 %copy-start.12 = (f32[48,256]{1,0:T(8,128)}, f32[48,256]{1,0:T(8,128)S(1)}, u32[]{:S(2)}) copy-start(f32[48,256]{1,0:T(8,128)S(1)} %convolution_subtract_fusion.5) | copy-start | bytes 147460
  118.9 23.0 %all-to-all-start.2 = ((f32[16,48,384]{2,1,0:T(8,128)}), f32[16,48,384]{2,1,0:T(8,128)}, u32[]{:S(2)}, u32[]{:S(2)}) async-start(f32[16,48,384]{2,1,0:T(8,128)} %bitcast.128), calls=%async_computation.2 | async-start | bytes 2359296 | tf_op jit(solution)/shard_map/all_to_all | solution.py:113
  127.5 15.8 %copy-start.11 = (f32[48,256]{1,0:T(8,128)S(1)}, f32[48,256]{1,0:T(8,128)}, u32[]{:S(2)}) copy-start(f32[48,256]{1,0:T(8,128)} %copy-done.10) | copy-start | bytes 147460
  127.5 15.8 %copy-start.13 = (f32[48,256]{1,0:T(8,128)S(1)}, f32[48,256]{1,0:T(8,128)}, u32[]{:S(2)}) copy-start(f32[48,256]{1,0:T(8,128)} %copy-done.12) | copy-start | bytes 147460
  127.5 15.8 %copy-start.15 = (f32[48,256]{1,0:T(8,128)S(1)}, f32[48,256]{1,0:T(8,128)}, u32[]{:S(2)}) copy-start(f32[48,256]{1,0:T(8,128)} %convolution_subtract_fusion.3) | copy-start | bytes 147460
  143.3 31.5 %copy-start.14 = (f32[48,384]{1,0:T(8,128)}, f32[48,384]{1,0:T(8,128)S(1)}, u32[]{:S(2)}) copy-start(f32[48,384]{1,0:T(8,128)S(1)} %reduce_sum.18) | copy-start | bytes 221188

commit v4 on v3

v4 whole, which is shorter than its diff:
```python
import jax
import jax.numpy as jnp
from jax import lax
from jax.sharding import PartitionSpec as P


TILE = 128
NSUPER = 3
NEAR = 4
LANES = 128


def contract(left, right, left_dim, right_dim, precision=lax.Precision.HIGH):
    return lax.dot_general(
        left,
        right,
        (((left_dim,), (right_dim,)), ((), ())),
        precision=precision,
        preferred_element_type=jnp.float32,
    )


def exchange(blocks, axis, groups=None):
    return lax.all_to_all(blocks, axis, 0, 0, tiled=True, axis_index_groups=groups)


def spread(block, axis, groups=None):
    count = len(groups[0]) if groups else lax.axis_size(axis)
    return exchange(jnp.broadcast_to(block[None], (count,) + block.shape), axis, groups)


def per_device(inverse_sep, sep_panels, chain_panels, diag_inverse, tile_list):
    rows = lax.axis_size("row")
    cols = lax.axis_size("col")
    row = lax.axis_index("row")
    col = lax.axis_index("col")
    height, width = inverse_sep.shape
    nb_cols = sep_panels.shape[2]
    nb_rows = chain_panels.shape[1]
    nb = nb_cols * cols
    cores = cols // rows
    chips = cols // cores
    far = chips // NEAR
    core = col % cores
    chip = col // cores
    tiles = height // TILE
    npair = chain_panels.shape[0]
    slab = NSUPER * nb_cols
    own_rows = NSUPER * nb_rows
    far_groups = [
        [cores * (first + NEAR * i) + c for i in range(far)]
        for first in range(NEAR)
        for c in range(cores)
    ]
    near_groups = [
        [cores * (NEAR * i + j) + c for j in range(NEAR) for c in range(cores)] for i in range(far)
    ]
    swap = [(c, c ^ 1) for c in range(cols)]
    turn = [
        (r * cols + c, (c // cores) * cols + cores * r + c % cores)
        for r in range(rows)
        for c in range(cols)
    ]

    listed = lax.dynamic_slice_in_dim(tile_list, row * tiles, tiles, 1).astype(jnp.float32)
    mask = jnp.broadcast_to(listed[:, :, None], (NSUPER, tiles, TILE)).reshape(NSUPER, 1, height)
    local_panel = (jnp.swapaxes(sep_panels, 1, 2) * mask).reshape(slab, height)
    turned = lax.ppermute(local_panel, ("row", "col"), turn)

    chain_size = npair * nb_rows * nb_cols
    chain_lines = chain_size // LANES
    chain_flat = chain_panels.reshape(chain_lines, LANES)
    chain_flat = jnp.pad(chain_flat, ((0, slab - chain_lines), (0, 0)))
    own = lax.all_gather(
        jnp.concatenate([local_panel, chain_flat], axis=1),
        "col",
        axis=0,
        tiled=True,
        axis_index_groups=far_groups,
    )
    chain_own = own[:, height:].reshape(far, slab, LANES)[:, :chain_lines]
    own = own[:, :height]

    chain_rows = spread(chain_own.reshape(1, far * chain_size), "col", near_groups)
    chain_rows = chain_rows.reshape(NEAR, cores, far, npair * nb_rows, nb_cols)
    chain_rows = jnp.transpose(chain_rows, (3, 2, 0, 1, 4)).reshape(npair * nb_rows, nb)
    diag_cols = lax.dynamic_slice_in_dim(diag_inverse, col * nb_cols, nb_cols, 2)
    diag_cols = jnp.concatenate([diag_cols[k] for k in range(NSUPER)], axis=1)
    diag_cols = jnp.pad(diag_cols, ((0, 0), (0, LANES - slab)))

    left, right = turned[:, :width], turned[:, width:]
    kept = jnp.where(core == 0, left, right)
    other = lax.ppermute(jnp.where(core == 0, right, left), "col", swap)
    pieces = [jnp.where(core == 0, kept, other), jnp.where(core == 0, other, kept)]
    pieces = jnp.concatenate(pieces, axis=0)

    def lines(block):
        tiles = range(0, block.shape[1], LANES)
        return jnp.concatenate([block[:, t : t + LANES] for t in tiles], axis=0)

    sides = [lines(chain_rows), diag_cols, lines(pieces)]
    sides_all = spread(jnp.concatenate(sides, axis=0), "row")
    cut = [sides[0].shape[0], sides[0].shape[0] + sides[1].shape[0]]
    chain_all = sides_all[:, : cut[0]].reshape(rows, nb // LANES, npair, nb_rows, LANES)
    chain = [
        jnp.concatenate(
            [chain_all[:, t, p].reshape(nb, LANES) for t in range(nb // LANES)], axis=1
        )
        for p in range(npair)
    ]
    late_sides = sides_all[:, cut[0] :]

    def from_chip(block, step):
        moves = [((c + cores * step) % cols, c) for c in range(cols)]
        return lax.ppermute(block, "col", moves)

    near = [own] + [from_chip(own, step) for step in (1, 2, -1)]
    mine = jnp.stack(near)
    theirs = lax.ppermute(mine, "col", swap)
    both = jnp.stack([jnp.where(core == 0, mine, theirs), jnp.where(core == 0, theirs, mine)])
    both = both.reshape(cores, NEAR, far, NSUPER, nb_cols, height)
    turnover = chip % NEAR
    places = []
    for place in range(NEAR):
        choice = both[:, place]
        for t in range(1, NEAR):
            choice = jnp.where(turnover == t, both[:, (place - t) % NEAR], choice)
        places.append(choice)
    ordered = jnp.stack(places)
    ordered = jnp.transpose(ordered, (3, 2, 0, 1, 4, 5)).reshape(NSUPER, nb, height)

    part = []
    for k in range(NSUPER):
        acc = contract(ordered[k], inverse_sep, 1, 0)
        for j in range(k):
            acc = acc + contract(chain[k * (k - 1) // 2 + j], part[j], 0, 0)
        part.append(-acc)
    outgoing = jnp.stack([x.reshape(rows, nb_rows, width) for x in part], axis=1)
    incoming = exchange(outgoing.reshape(rows, own_rows, width), "row")
    new_rows = jnp.sum(incoming, axis=0)

    col_panel = late_sides[:, nb_rows:].reshape(rows, width // LANES, cores, NSUPER, nb_cols, LANES)
    col_panel = [
        jnp.concatenate(
            [col_panel[:, t, :, k].reshape(nb, LANES) for t in range(width // LANES)], axis=1
        )
        for k in range(NSUPER)
    ]
    solved = []
    for k in range(NSUPER):
        acc = col_panel[k]
        for j in range(k):
            acc = acc - contract(chain[k * (k - 1) // 2 + j], solved[j], 0, 0)
        solved.append(acc)
    solved = jnp.concatenate(solved, axis=0)
    exact = lax.Precision.HIGHEST
    place = row * nb_rows + lax.broadcasted_iota(jnp.int32, (nb_rows, nb), 0)
    unit = (lax.broadcasted_iota(jnp.int32, (nb_rows, nb), 1) == place).astype(jnp.float32)
    zero = jnp.zeros((nb_rows, nb), jnp.float32)
    cc = [contract(unit, chain[p], 1, 1, exact) for p in range(npair)]
    lead = [
        jnp.concatenate([unit, -cc[0], contract(cc[2], chain[0], 1, 1, exact) - cc[1]], axis=0),
        jnp.concatenate([zero, unit, -cc[2]], axis=0),
        jnp.concatenate([zero, zero, unit], axis=0),
    ]
    diag_all = late_sides[:, :nb_rows].reshape(nb, LANES)
    source = lax.broadcasted_iota(jnp.int32, (nb, LANES), 0) - col * nb_cols
    target = lax.broadcasted_iota(jnp.int32, (nb, LANES), 1)
    inside = (source >= 0) & (source < nb_cols)
    base = []
    for k in range(NSUPER):
        pick = (inside & (target == source + k * nb_cols)).astype(jnp.float32)
        acc = contract(contract(lead[k], pick, 1, 0, exact), diag_all, 1, 1, exact)
        for j in range(k):
            acc = acc - contract(base[j], chain[k * (k - 1) // 2 + j], 1, 0, exact)
        base.append(acc)
    base = jnp.concatenate(base, axis=1)

    inner = base - contract(new_rows, solved, 1, 1)
    share = own_rows * NSUPER * nb // (NEAR * cores)
    near_sum = jnp.sum(exchange(inner.reshape(NEAR * cores, 1, share), "col", near_groups), axis=0)
    far_sum = jnp.sum(spread(near_sum, "col", far_groups), axis=0)
    state = spread(far_sum, "col", near_groups)
    return (
        new_rows.reshape(NSUPER, nb_rows, width),
        state.reshape(NSUPER, nb_rows, NSUPER * nb),
    )


def solution(mesh):
    in_specs = (
        P("row", "col"),
        P(None, "row", "col"),
        P(None, "row", "col"),
        P(None, "row", None),
        P(),
    )
    out_specs = (P(None, "row", "col"), P(None, "row", None))

    return jax.shard_map(
        per_device, mesh=mesh, in_specs=in_specs, out_specs=out_specs, check_vma=False
    )
```

time: 198 us -> 194 us (0.980)
  waiting for transfers between devices: 31.4 us -> 51.4 us
  starting transfers between devices: 51.5 us -> 39.3 us
  blocking collectives: 76.7 us -> 70.6 us
  local copies, waits for them, and re-layouts: 14.7 us -> 9.7 us
    all_to_all x4 -> x3, waiting for transfers between devices: 31.1 us -> 50.2 us  [exchange(): lax.all_to_all(blocks, axis, 0, 0, tiled=True, axis_index_groups=groups)]
    all_to_all x4 -> x3, starting transfers between devices: 36 us -> 25.5 us  [exchange(): lax.all_to_all(blocks, axis, 0, 0, tiled=True, axis_index_groups=groups)]
    all_to_all x2 -> x3, blocking collectives: 51.4 us -> 44.2 us  [exchange(): lax.all_to_all(blocks, axis, 0, 0, tiled=True, axis_index_groups=groups)]
    slice x11 -> x8, local copies, waits for them, and re-layouts: 4.8 us -> 0.4 us  [the longest x1 0.11 us: per_device(): col_panel[:, t, :, k].reshape(nb, LANES)]
    dot_general x20 -> x23, matrix products: 13 us -> 11.5 us  [contract(): lax.dot_general(left, right, (((left_dim,), (right_dim,)), ((), ())), pre...]
  transfers between devices with their start and end apart: 10 -> 9, of which waited for: 4 -> 4; matrix products, arithmetic and copies ran while one was open for 15% -> 8% of each run, Pallas kernels for 0% -> 0%
where the time goes in v4:
time: 194 us; the launch traced here: 193 us
  blocking collectives  70.6 us (36%)
  waiting for transfers between devices  51.4 us (26%)
  starting transfers between devices  39.3 us (20%)
  matrix products  11.5 us (6%)
  local copies, waits for them, and re-layouts  9.7 us (5%)
  other arithmetic  9.26 us (5%)
    all_to_all x3, waiting for transfers between devices, exchange(): lax.all_to_all(blocks, axis, 0, 0, tiled=True, axis_index_groups=groups)  50.2 us
    all_to_all x3, blocking collectives, exchange(): lax.all_to_all(blocks, axis, 0, 0, tiled=True, axis_index_groups=groups)  44.2 us
    all_gather x1, blocking collectives, per_device(): lax.all_gather(jnp.concatenate([local_panel, chain_flat], axis=1), 'col',...  26.4 us
    all_to_all x3, starting transfers between devices, exchange(): lax.all_to_all(blocks, axis, 0, 0, tiled=True, axis_index_groups=groups)  25.5 us
    dot_general x23, matrix products, contract(): lax.dot_general(left, right, (((left_dim,), (right_dim,)), ((), ())), pre...  11.5 us
    ppermute x3, starting transfers between devices, from_chip(): return lax.ppermute(block, 'col', moves)  8.5 us
  transfers between devices with their start and end apart: 9, of which 4 were waited for; matrix products, arithmetic and copies ran while one was open for 8% of the time, Pallas kernels for 0%

profile of v4, /device:TPU:1, one launch (start us, length us, event | category | flops | bytes accessed | tf_op | source)
XLA Modules:
  0.0 193.3 jit_solution(1015881602273143912)
XLA Ops:
  0.7 0.9 copy.75
  1.6 0.8 dynamic-slice_convert_fusion
  2.5 0.9 multiply_bitcast_fusion
  3.4 26.4 %all_gather.3 = f32[96,896]{1,0:T(8,128)S(1)} all-gather(f32[24,896]{1,0:T(8,128)S(1)} %select_maximum_fusion), channel_id=1, replica_groups={{0,8,16,24},{1,9,17,25},{2,10,18,26},{3,11,19,27},{4,12,20,28},{5,13,21..., dimensions={0}, use_global_device_ids=true | all-gather | bytes 430080 | tf_op jit(solution)/shard_map/all_gather | solution.py:74
  30.6 2.8 %collective-permute-start.2 = (f32[96,768]{1,0:T(8,128)}, f32[96,768]{1,0:T(8,128)S(1)}, u32[]{:S(2)}, u32[]{:S(2)}) collective-permute-start(f32[96,768]{1,0:T(8,128)} %get-tuple-element.31), channel_id=1, source_target_pairs={{30,0},{31,1},{0,2},{1,3},{2,4},{3,5},{4,6},{5,7},{6,8},{7,9},{8,1... | collective-permute-start | bytes 884744 | tf_op jit(solution)/shard_map/ppermute | solution.py:115
  33.4 3.7 %collective-permute-start.1 = (f32[96,768]{1,0:T(8,128)}, f32[96,768]{1,0:T(8,128)S(1)}, u32[]{:S(2)}, u32[]{:S(2)}) collective-permute-start(f32[96,768]{1,0:T(8,128)} %get-tuple-element.31), channel_id=1, source_target_pairs={{4,0},{5,1},{6,2},{7,3},{8,4},{9,5},{10,6},{11,7},{12,8},{13,9},{1... | collective-permute-start | bytes 884744 | tf_op jit(solution)/shard_map/ppermute | solution.py:115
  37.1 2.0 %collective-permute-start = (f32[96,768]{1,0:T(8,128)}, f32[96,768]{1,0:T(8,128)S(1)}, u32[]{:S(2)}, u32[]{:S(2)}) collective-permute-start(f32[96,768]{1,0:T(8,128)} %get-tuple-element.31), channel_id=1, source_target_pairs={{2,0},{3,1},{4,2},{5,3},{6,4},{7,5},{8,6},{9,7},{10,8},{11,9},{12,... | collective-permute-start | bytes 884744 | tf_op jit(solution)/shard_map/ppermute | solution.py:115
  40.4 12.6 %all-to-all-start = ((f32[8,1,1536]{2,1,0:T(1,128)}), f32[8,1,1536]{2,1,0:T(1,128)S(1)}, u32[]{:S(2)}, u32[]{:S(2)}) async-start(f32[8,1,1536]{2,1,0:T(1,128)} %broadcast_in_dim.16), calls=%async_computation | async-start | bytes 98304 | tf_op jit(solution)/shard_map/all_to_all | solution.py:24
  53.2 1.9 collective-permute-start.5
  55.1 1.2 collective-permute-done.5
  56.3 13.6 %all-to-all-done = f32[8,1,1536]{2,1,0:T(1,128)S(1)} async-done(((f32[8,1,1536]{2,1,0:T(1,128)}), f32[8,1,1536]{2,1,0:T(1,128)S(1)}, u32[]{:S(2)}, u32[]{:S(2)}) %all-to-all-start) | async-done | bytes 49184 | tf_op jit(solution)/shard_map/all_to_all | solution.py:24
  70.8 1.3 pad_maximum_fusion
  72.1 2.7 %collective-permute-start.3 = (f32[4,96,768]{2,1,0:T(8,128)}, f32[4,96,768]{2,1,0:T(8,128)}, u32[]{:S(2)}, u32[]{:S(2)}) collective-permute-start(f32[4,96,768]{2,1,0:T(8,128)} %pad_maximum_fusion), channel_id=1, source_target_pairs={{0,1},{1,0},{2,3},{3,2},{4,5},{5,4},{6,7},{7,6},{8,9},{9,8},{10,11... | collective-permute-start | bytes 3538952 | tf_op jit(solution)/shard_map/ppermute | solution.py:119
  75.0 1.6 broadcast_in_dim.17
  76.6 8.6 %all-to-all-start.1 = ((f32[16,256,128]{2,1,0:T(8,128)}), f32[16,256,128]{2,1,0:T(8,128)S(1)}, u32[]{:S(2)}, u32[]{:S(2)}) async-start(f32[16,256,128]{2,1,0:T(8,128)} %broadcast_in_dim.17), calls=%async_computation.1 | async-start | bytes 4194304 | tf_op jit(solution)/shard_map/all_to_all | solution.py:24
  86.4 0.9 fusion.30
  87.3 1.8 broadcast_select_fusion.1
  90.1 1.0 copy.80
  91.0 1.0 copy.88
  92.0 1.6 convolution_negate_fusion
  93.6 24.4 %all-to-all-done.1 = f32[16,256,128]{2,1,0:T(8,128)S(1)} async-done(((f32[16,256,128]{2,1,0:T(8,128)}), f32[16,256,128]{2,1,0:T(8,128)S(1)}, u32[]{:S(2)}, u32[]{:S(2)}) %all-to-all-start.1) | async-done | bytes 2097184 | tf_op jit(solution)/shard_map/all_to_all | solution.py:24
  118.2 0.9 convolution_negate_fusion.1
  119.5 0.8 fusion.2
  120.4 0.9 fusion.90
  122.1 0.8 fusion.1
  123.0 1.1 pad_maximum_fusion.1
  124.1 4.4 %all-to-all-start.2 = ((f32[16,48,384]{2,1,0:T(8,128)}), f32[16,48,384]{2,1,0:T(8,128)}, u32[]{:S(2)}, u32[]{:S(2)}) async-start(f32[16,48,384]{2,1,0:T(8,128)} %bitcast.102), calls=%async_computation.2 | async-start | bytes 2359296 | tf_op jit(solution)/shard_map/all_to_all | solution.py:24
  133.4 12.2 %all-to-all-done.2 = f32[16,48,384]{2,1,0:T(8,128)} async-done(((f32[16,48,384]{2,1,0:T(8,128)}), f32[16,48,384]{2,1,0:T(8,128)}, u32[]{:S(2)}, u32[]{:S(2)}) %all-to-all-start.2) | async-done | bytes 1179680 | tf_op jit(solution)/shard_map/all_to_all | solution.py:24
  145.6 1.3 reduce_sum.27
  147.8 12.3 %all_to_all.30 = f32[8,1,4608]{2,1,0:T(1,128)S(1)} all-to-all(f32[8,1,4608]{2,1,0:T(1,128)S(1)} %reshape.229), channel_id=1, replica_groups={{0,1,2,3,4,5,6,7},{8,9,10,11,12,13,14,15},{16,17,18,19,20,21,22,23},{24..., dimensions={0} | all-to-all | bytes 294912 | tf_op jit(solution)/shard_map/all_to_all | solution.py:24
  160.2 20.9 %all_to_all.31 = f32[4,1,4608]{2,1,0:T(1,128)S(1)} all-to-all(f32[4,1,4608]{2,1,0:T(1,128)S(1)} %broadcast_in_dim.19), channel_id=1, replica_groups={{0,8,16,24},{1,9,17,25},{2,10,18,26},{3,11,19,27},{4,12,20,28},{5,13,21..., dimensions={0} | all-to-all | bytes 147456 | tf_op jit(solution)/shard_map/all_to_all | solution.py:24
  181.3 11.0 %all_to_all.32 = f32[8,1,4608]{2,1,0:T(1,128)S(1)} all-to-all(f32[8,1,4608]{2,1,0:T(1,128)S(1)} %broadcast_in_dim.40), channel_id=1, replica_groups={{0,1,2,3,4,5,6,7},{8,9,10,11,12,13,14,15},{16,17,18,19,20,21,22,23},{24..., dimensions={0} | all-to-all | bytes 294912 | tf_op jit(solution)/shard_map/all_to_all | solution.py:24
  (145 shorter events, 13.8 us)
Async XLA Ops:
  0.6 91.4 %copy-start = (f32[768,384]{1,0:T(8,128)S(1)}, f32[768,384]{1,0:T(8,128)}, u32[]{:S(2)}) copy-start(f32[768,384]{1,0:T(8,128)} %param.5) | copy-start | bytes 3538948
  0.6 52.4 %copy-start.28 = (f32[3,16,256]{2,1,0:T(8,128)S(1)}, f32[3,16,256]{2,1,0:T(8,128)}, u32[]{:S(2)}) copy-start(f32[3,16,256]{2,1,0:T(8,128)} %param.8) | copy-start | bytes 147460
  30.5 40.2 %copy-start.12 = (f32[1,96,768]{2,1,0:T(8,128)}, f32[1,96,768]{2,1,0:T(8,128)S(1)}, u32[]{:S(2)}) copy-start(f32[1,96,768]{2,1,0:T(8,128)S(1)} %get-tuple-element.30) | copy-start | bytes 884740
  30.6 40.2 %collective-permute-start.2 = (f32[96,768]{1,0:T(8,128)}, f32[96,768]{1,0:T(8,128)S(1)}, u32[]{:S(2)}, u32[]{:S(2)}) collective-permute-start(f32[96,768]{1,0:T(8,128)} %get-tuple-element.31), channel_id=1, source_target_pairs={{30,0},{31,1},{0,2},{1,3},{2,4},{3,5},{4,6},{5,7},{6,8},{7,9},{8,1... | collective-permute-start | bytes 884744 | tf_op jit(solution)/shard_map/ppermute | solution.py:115
  33.4 37.4 %collective-permute-start.1 = (f32[96,768]{1,0:T(8,128)}, f32[96,768]{1,0:T(8,128)S(1)}, u32[]{:S(2)}, u32[]{:S(2)}) collective-permute-start(f32[96,768]{1,0:T(8,128)} %get-tuple-element.31), channel_id=1, source_target_pairs={{4,0},{5,1},{6,2},{7,3},{8,4},{9,5},{10,6},{11,7},{12,8},{13,9},{1... | collective-permute-start | bytes 884744 | tf_op jit(solution)/shard_map/ppermute | solution.py:115
  37.1 33.7 %collective-permute-start = (f32[96,768]{1,0:T(8,128)}, f32[96,768]{1,0:T(8,128)S(1)}, u32[]{:S(2)}, u32[]{:S(2)}) collective-permute-start(f32[96,768]{1,0:T(8,128)} %get-tuple-element.31), channel_id=1, source_target_pairs={{2,0},{3,1},{4,2},{5,3},{6,4},{7,5},{8,6},{9,7},{10,8},{11,9},{12,... | collective-permute-start | bytes 884744 | tf_op jit(solution)/shard_map/ppermute | solution.py:115
  39.1 14.1 %collective-permute-start.4 = (f32[24,768]{1,0:T(8,128)S(1)}, f32[24,768]{1,0:T(8,128)S(1)}, u32[]{:S(2)}, u32[]{:S(2)}) collective-permute-start(f32[24,768]{1,0:T(8,128)S(1)} %multiply_bitcast_fusion), channel_id=1, source_target_pairs={{0,0},{1,1},{2,32},{3,33},{4,64},{5,65},{6,96},{7,97},{8,128},{9,1... | collective-permute-start | bytes 221192 | tf_op jit(solution)/shard_map/ppermute | solution.py:68
  40.4 29.4 %all-to-all-start = ((f32[8,1,1536]{2,1,0:T(1,128)}), f32[8,1,1536]{2,1,0:T(1,128)S(1)}, u32[]{:S(2)}, u32[]{:S(2)}) async-start(f32[8,1,1536]{2,1,0:T(1,128)} %broadcast_in_dim.16), calls=%async_computation | async-start | bytes 98304 | tf_op jit(solution)/shard_map/all_to_all | solution.py:24
  53.0 65.2 %copy-start.29 = (s32[16]{0:T(128)}, s32[16]{0:T(128)S(1)}, u32[]{:S(2)}) copy-start(s32[16]{0:T(128)S(1)} %iota_add_fusion) | copy-start | bytes 196
  53.1 33.3 %copy-start.26 = (f32[16,256]{1,0:T(8,128)}, f32[16,256]{1,0:T(8,128)S(1)}, u32[]{:S(2)}) copy-start(f32[16,256]{1,0:T(8,128)S(1)} %fusion.59) | copy-start | bytes 49156
  53.2 3.1 %collective-permute-start.5 = (f32[24,384]{1,0:T(8,128)S(1)}, f32[24,384]{1,0:T(8,128)S(1)}, u32[]{:S(2)}, u32[]{:S(2)}) collective-permute-start(f32[24,384]{1,0:T(8,128)S(1)} %slice_select_fusion), channel_id=1, source_target_pairs={{0,1},{1,0},{2,3},{3,2},{4,5},{5,4},{6,7},{7,6},{8,9},{9,8},{10,11... | collective-permute-start | bytes 110600 | tf_op jit(solution)/shard_map/ppermute | solution.py:93
  72.1 15.2 %collective-permute-start.3 = (f32[4,96,768]{2,1,0:T(8,128)}, f32[4,96,768]{2,1,0:T(8,128)}, u32[]{:S(2)}, u32[]{:S(2)}) collective-permute-start(f32[4,96,768]{2,1,0:T(8,128)} %pad_maximum_fusion), channel_id=1, source_target_pairs={{0,1},{1,0},{2,3},{3,2},{4,5},{5,4},{6,7},{7,6},{8,9},{9,8},{10,11... | collective-permute-start | bytes 3538952 | tf_op jit(solution)/shard_map/ppermute | solution.py:119
  76.6 41.4 %all-to-all-start.1 = ((f32[16,256,128]{2,1,0:T(8,128)}), f32[16,256,128]{2,1,0:T(8,128)S(1)}, u32[]{:S(2)}, u32[]{:S(2)}) async-start(f32[16,256,128]{2,1,0:T(8,128)} %broadcast_in_dim.17), calls=%async_computation.1 | async-start | bytes 4194304 | tf_op jit(solution)/shard_map/all_to_all | solution.py:24
  85.2 3.9 %copy-start.35 = (pred[256]{0:T(512)(128)(4,1)}, pred[256]{0:T(512)(128)(4,1)S(1)}, u32[]{:S(2)}) copy-start(pred[256]{0:T(512)(128)(4,1)S(1)} %compare_and_fusion) | copy-start | bytes 772
  118.2 3.1 %copy-start.2 = (f32[16,1,1,16,128]{4,3,2,1,0:T(8,128)}, f32[16,1,1,16,128]{4,3,2,1,0:T(8,128)S(1)}, u32[]{:S(2)}) copy-start(f32[16,1,1,16,128]{4,3,2,1,0:T(8,128)S(1)} %get-tuple-element.25) | copy-start | bytes 393220
  118.2 3.1 %copy-start.4 = (f32[16,1,1,16,128]{4,3,2,1,0:T(8,128)}, f32[16,1,1,16,128]{4,3,2,1,0:T(8,128)S(1)}, u32[]{:S(2)}) copy-start(f32[16,1,1,16,128]{4,3,2,1,0:T(8,128)S(1)} %get-tuple-element.26) | copy-start | bytes 393220
  118.2 3.5 %copy-start.6 = (f32[16,1,1,16,128]{4,3,2,1,0:T(8,128)}, f32[16,1,1,16,128]{4,3,2,1,0:T(8,128)S(1)}, u32[]{:S(2)}) copy-start(f32[16,1,1,16,128]{4,3,2,1,0:T(8,128)S(1)} %get-tuple-element.24) | copy-start | bytes 393220
  118.2 3.5 %copy-start.8 = (f32[16,1,1,16,128]{4,3,2,1,0:T(8,128)}, f32[16,1,1,16,128]{4,3,2,1,0:T(8,128)S(1)}, u32[]{:S(2)}) copy-start(f32[16,1,1,16,128]{4,3,2,1,0:T(8,128)S(1)} %get-tuple-element.27) | copy-start | bytes 393220
  120.4 1.8 copy-start.10
  124.1 21.5 %all-to-all-start.2 = ((f32[16,48,384]{2,1,0:T(8,128)}), f32[16,48,384]{2,1,0:T(8,128)}, u32[]{:S(2)}, u32[]{:S(2)}) async-start(f32[16,48,384]{2,1,0:T(8,128)} %bitcast.102), calls=%async_computation.2 | async-start | bytes 2359296 | tf_op jit(solution)/shard_map/all_to_all | solution.py:24
  128.6 1.5 copy-start.25
  128.6 1.5 copy-start.27
  128.6 1.5 copy-start.33
  128.7 2.9 %copy-start.16 = (f32[16,1,2,1,8,128]{5,4,3,2,1,0:T(8,128)}, f32[16,1,2,1,8,128]{5,4,3,2,1,0:T(8,128)S(1)}, u32[]{:S(2)}) copy-start(f32[16,1,2,1,8,128]{5,4,3,2,1,0:T(8,128)S(1)} %get-tuple-element.21) | copy-start | bytes 393220
  128.8 2.9 %copy-start.18 = (f32[16,1,2,1,8,128]{5,4,3,2,1,0:T(8,128)}, f32[16,1,2,1,8,128]{5,4,3,2,1,0:T(8,128)S(1)}, u32[]{:S(2)}) copy-start(f32[16,1,2,1,8,128]{5,4,3,2,1,0:T(8,128)S(1)} %get-tuple-element.22) | copy-start | bytes 393220
  128.8 2.9 %copy-start.20 = (f32[16,1,2,1,8,128]{5,4,3,2,1,0:T(8,128)}, f32[16,1,2,1,8,128]{5,4,3,2,1,0:T(8,128)S(1)}, u32[]{:S(2)}) copy-start(f32[16,1,2,1,8,128]{5,4,3,2,1,0:T(8,128)S(1)} %get-tuple-element.23) | copy-start | bytes 393220
  128.8 2.1 %copy-start.24 = (f32[16,256]{1,0:T(8,128)S(1)}, f32[16,256]{1,0:T(8,128)}, u32[]{:S(2)}) copy-start(f32[16,256]{1,0:T(8,128)} %get-tuple-element.39) | copy-start | bytes 49156
  128.8 2.1 %copy-start.32 = (s32[256]{0:T(256)S(1)}, s32[256]{0:T(256)}, u32[]{:S(2)}) copy-start(s32[256]{0:T(256)} %get-tuple-element.42) | copy-start | bytes 3076
  128.8 2.1 %copy-start.34 = (f32[48]{0:T(128)S(1)}, f32[48]{0:T(128)}, u32[]{:S(2)}) copy-start(f32[48]{0:T(128)} %pad.28.clone) | copy-start | bytes 580
  132.9 14.0 %copy-start.17 = (f32[16,1,2,1,8,128]{5,4,3,2,1,0:T(8,128)S(1)}, f32[16,1,2,1,8,128]{5,4,3,2,1,0:T(8,128)}, u32[]{:S(2)}) copy-start(f32[16,1,2,1,8,128]{5,4,3,2,1,0:T(8,128)} %copy-done.16) | copy-start | bytes 393220
  132.9 14.0 %copy-start.19 = (f32[16,1,2,1,8,128]{5,4,3,2,1,0:T(8,128)S(1)}, f32[16,1,2,1,8,128]{5,4,3,2,1,0:T(8,128)}, u32[]{:S(2)}) copy-start(f32[16,1,2,1,8,128]{5,4,3,2,1,0:T(8,128)} %copy-done.18) | copy-start | bytes 393220
  132.9 14.0 %copy-start.21 = (f32[16,1,2,1,8,128]{5,4,3,2,1,0:T(8,128)S(1)}, f32[16,1,2,1,8,128]{5,4,3,2,1,0:T(8,128)}, u32[]{:S(2)}) copy-start(f32[16,1,2,1,8,128]{5,4,3,2,1,0:T(8,128)} %copy-done.20) | copy-start | bytes 393220
  (14 other events, 15.4 us)

commit v5 on v4

--- a/solution.py
+++ b/solution.py
@@ -98,17 +98,18 @@
         tiles = range(0, block.shape[1], LANES)
         return jnp.concatenate([block[:, t : t + LANES] for t in tiles], axis=0)
 
-    sides = [lines(chain_rows), diag_cols, lines(pieces)]
-    sides_all = spread(jnp.concatenate(sides, axis=0), "row")
-    cut = [sides[0].shape[0], sides[0].shape[0] + sides[1].shape[0]]
-    chain_all = sides_all[:, : cut[0]].reshape(rows, nb // LANES, npair, nb_rows, LANES)
+    chain_lines = lines(chain_rows)
+    chain_all = spread(jnp.concatenate([chain_lines, diag_cols], axis=0), "row")
+    col_panel = spread(pieces, "row").reshape(rows, cores, NSUPER, nb_cols, width)
+    diag_all = chain_all[:, chain_lines.shape[0] :].reshape(nb, LANES)
+    chain_all = chain_all[:, : chain_lines.shape[0]]
+    chain_all = chain_all.reshape(rows, nb // LANES, npair, nb_rows, LANES)
     chain = [
         jnp.concatenate(
             [chain_all[:, t, p].reshape(nb, LANES) for t in range(nb // LANES)], axis=1
         )
         for p in range(npair)
     ]
-    late_sides = sides_all[:, cut[0] :]
 
     def from_chip(block, step):
         moves = [((c + cores * step) % cols, c) for c in range(cols)]
@@ -139,13 +140,7 @@
     incoming = exchange(outgoing.reshape(rows, own_rows, width), "row")
     new_rows = jnp.sum(incoming, axis=0)
 
-    col_panel = late_sides[:, nb_rows:].reshape(rows, width // LANES, cores, NSUPER, nb_cols, LANES)
-    col_panel = [
-        jnp.concatenate(
-            [col_panel[:, t, :, k].reshape(nb, LANES) for t in range(width // LANES)], axis=1
-        )
-        for k in range(NSUPER)
-    ]
+    col_panel = [col_panel[:, :, k].reshape(nb, width) for k in range(NSUPER)]
     solved = []
     for k in range(NSUPER):
         acc = col_panel[k]
@@ -163,7 +158,6 @@
         jnp.concatenate([zero, unit, -cc[2]], axis=0),
         jnp.concatenate([zero, zero, unit], axis=0),
     ]
-    diag_all = late_sides[:, :nb_rows].reshape(nb, LANES)
     source = lax.broadcasted_iota(jnp.int32, (nb, LANES), 0) - col * nb_cols
     target = lax.broadcasted_iota(jnp.int32, (nb, LANES), 1)
     inside = (source >= 0) & (source < nb_cols)

time: 194 us -> 182 us (0.938)
  waiting for transfers between devices: 51.4 us -> 38.7 us
  starting transfers between devices: 39.3 us -> 42.3 us
  matrix products: 11.5 us -> 13.7 us
  blocking collectives: 70.6 us -> 68.5 us
    all_to_all x3 -> x4, waiting for transfers between devices: 50.2 us -> 37.9 us  [exchange(): lax.all_to_all(blocks, axis, 0, 0, tiled=True, axis_index_groups=groups)]
    all_to_all x3 -> x4, starting transfers between devices: 25.5 us -> 27.9 us  [exchange(): lax.all_to_all(blocks, axis, 0, 0, tiled=True, axis_index_groups=groups)]
    dot_general x23, matrix products: 11.5 us -> 13.7 us  [contract(): lax.dot_general(left, right, (((left_dim,), (right_dim,)), ((), ())), pre...]
    all_to_all x3, blocking collectives: 44.2 us -> 42.1 us  [exchange(): lax.all_to_all(blocks, axis, 0, 0, tiled=True, axis_index_groups=groups)]
  transfers between devices with their start and end apart: 9 -> 10, of which waited for: 4 -> 5; matrix products, arithmetic and copies ran while one was open for 8% -> 12% of each run, Pallas kernels for 0% -> 0%
where the time goes in v5:
time: 182 us; the launch traced here: 181 us
  blocking collectives  68.5 us (38%)
  starting transfers between devices  42.3 us (23%)
  waiting for transfers between devices  38.7 us (21%)
  matrix products  13.7 us (8%)
  local copies, waits for them, and re-layouts  8.36 us (5%)
  other arithmetic  8.32 us (5%)
    all_to_all x3, blocking collectives, exchange(): lax.all_to_all(blocks, axis, 0, 0, tiled=True, axis_index_groups=groups)  42.1 us
    all_to_all x4, waiting for transfers between devices, exchange(): lax.all_to_all(blocks, axis, 0, 0, tiled=True, axis_index_groups=groups)  37.9 us
    all_to_all x4, starting transfers between devices, exchange(): lax.all_to_all(blocks, axis, 0, 0, tiled=True, axis_index_groups=groups)  27.9 us
    all_gather x1, blocking collectives, per_device(): lax.all_gather(jnp.concatenate([local_panel, chain_flat], axis=1), 'col',...  26.4 us
    dot_general x23, matrix products, contract(): lax.dot_general(left, right, (((left_dim,), (right_dim,)), ((), ())), pre...  13.7 us
    ppermute x3, starting transfers between devices, from_chip(): return lax.ppermute(block, 'col', moves)  8.51 us
  transfers between devices with their start and end apart: 10, of which 5 were waited for; matrix products, arithmetic and copies ran while one was open for 12% of the time, Pallas kernels for 0%

profile of v5, /device:TPU:1, one launch (start us, length us, event | category | flops | bytes accessed | tf_op | source)
XLA Modules:
  0.0 181.2 jit_solution(16708167996629389698)
XLA Ops:
  0.7 0.9 copy.60
  2.5 0.9 multiply_bitcast_fusion
  3.4 26.4 %all_gather.3 = f32[96,896]{1,0:T(8,128)S(1)} all-gather(f32[24,896]{1,0:T(8,128)S(1)} %select_maximum_fusion), channel_id=1, replica_groups={{0,8,16,24},{1,9,17,25},{2,10,18,26},{3,11,19,27},{4,12,20,28},{5,13,21..., dimensions={0}, use_global_device_ids=true | all-gather | bytes 430080 | tf_op jit(solution)/shard_map/all_gather | solution.py:74
  30.5 2.8 %collective-permute-start.2 = (f32[96,768]{1,0:T(8,128)}, f32[96,768]{1,0:T(8,128)}, u32[]{:S(2)}, u32[]{:S(2)}) collective-permute-start(f32[96,768]{1,0:T(8,128)} %get-tuple-element.25), channel_id=1, source_target_pairs={{30,0},{31,1},{0,2},{1,3},{2,4},{3,5},{4,6},{5,7},{6,8},{7,9},{8,1... | collective-permute-start | bytes 884744 | tf_op jit(solution)/shard_map/ppermute | solution.py:116
  33.4 3.7 %collective-permute-start.1 = (f32[96,768]{1,0:T(8,128)}, f32[96,768]{1,0:T(8,128)}, u32[]{:S(2)}, u32[]{:S(2)}) collective-permute-start(f32[96,768]{1,0:T(8,128)} %get-tuple-element.25), channel_id=1, source_target_pairs={{4,0},{5,1},{6,2},{7,3},{8,4},{9,5},{10,6},{11,7},{12,8},{13,9},{1... | collective-permute-start | bytes 884744 | tf_op jit(solution)/shard_map/ppermute | solution.py:116
  37.1 2.0 %collective-permute-start = (f32[96,768]{1,0:T(8,128)}, f32[96,768]{1,0:T(8,128)}, u32[]{:S(2)}, u32[]{:S(2)}) collective-permute-start(f32[96,768]{1,0:T(8,128)} %get-tuple-element.25), channel_id=1, source_target_pairs={{2,0},{3,1},{4,2},{5,3},{6,4},{7,5},{8,6},{9,7},{10,8},{11,9},{12,... | collective-permute-start | bytes 884744 | tf_op jit(solution)/shard_map/ppermute | solution.py:116
  40.4 12.6 %all-to-all-start = ((f32[8,1,1536]{2,1,0:T(1,128)}), f32[8,1,1536]{2,1,0:T(1,128)S(1)}, u32[]{:S(2)}, u32[]{:S(2)}) async-start(f32[8,1,1536]{2,1,0:T(1,128)} %broadcast_in_dim.18), calls=%async_computation | async-start | bytes 98304 | tf_op jit(solution)/shard_map/all_to_all | solution.py:24
  53.4 16.5 %all-to-all-done = f32[8,1,1536]{2,1,0:T(1,128)S(1)} async-done(((f32[8,1,1536]{2,1,0:T(1,128)}), f32[8,1,1536]{2,1,0:T(1,128)S(1)}, u32[]{:S(2)}, u32[]{:S(2)}) %all-to-all-start) | async-done | bytes 49184 | tf_op jit(solution)/shard_map/all_to_all | solution.py:24
  70.9 1.0 broadcast_in_dim.19
  71.9 6.2 %all-to-all-start.1 = ((f32[16,112,128]{2,1,0:T(8,128)}), f32[16,112,128]{2,1,0:T(8,128)S(1)}, u32[]{:S(2)}, u32[]{:S(2)}) async-start(f32[16,112,128]{2,1,0:T(8,128)} %broadcast_in_dim.19), calls=%async_computation.1 | async-start | bytes 1835008 | tf_op jit(solution)/shard_map/all_to_all | solution.py:24
  78.5 2.9 %collective-permute-start.5 = (f32[24,384]{1,0:T(8,128)S(1)}, f32[24,384]{1,0:T(8,128)S(1)}, u32[]{:S(2)}, u32[]{:S(2)}) collective-permute-start(f32[24,384]{1,0:T(8,128)S(1)} %slice_select_fusion), channel_id=1, source_target_pairs={{0,1},{1,0},{2,3},{3,2},{4,5},{5,4},{6,7},{7,6},{8,9},{9,8},{10,11... | collective-permute-start | bytes 110600 | tf_op jit(solution)/shard_map/ppermute | solution.py:93
  82.3 2.2 %pad_maximum_fusion = f32[4,96,768]{2,1,0:T(8,128)} fusion(f32[1,96,768]{2,1,0:T(8,128)} %bitcast.5, f32[1,96,768]{2,1,0:T(8,128)} %bitcast.4, f32[1,96,768]{2,1,0:T(8,128)} %bitcast.3, f32[1,96,768]{2,1,0:T(8,128)S(1)} %get-tuple-element.24), kind=kLoop, calls=%fused_computation.16 | loop fusion | flops 884736 | bytes 2359296 | tf_op jit(solution)/shard_map/stack | solution.py:119
  84.6 2.2 %collective-permute-start.3 = (f32[4,96,768]{2,1,0:T(8,128)}, f32[4,96,768]{2,1,0:T(8,128)}, u32[]{:S(2)}, u32[]{:S(2)}) collective-permute-start(f32[4,96,768]{2,1,0:T(8,128)} %pad_maximum_fusion), channel_id=1, source_target_pairs={{0,1},{1,0},{2,3},{3,2},{4,5},{5,4},{6,7},{7,6},{8,9},{9,8},{10,11... | collective-permute-start | bytes 3538952 | tf_op jit(solution)/shard_map/ppermute | solution.py:120
  86.8 5.9 %all-to-all-done.1 = f32[16,112,128]{2,1,0:T(8,128)S(1)} async-done(((f32[16,112,128]{2,1,0:T(8,128)}), f32[16,112,128]{2,1,0:T(8,128)S(1)}, u32[]{:S(2)}, u32[]{:S(2)}) %all-to-all-start.1) | async-done | bytes 917536 | tf_op jit(solution)/shard_map/all_to_all | solution.py:24
  92.7 1.1 broadcast_in_dim.21
  93.8 4.0 %all-to-all-start.3 = ((f32[16,48,384]{2,1,0:T(8,128)}), f32[16,48,384]{2,1,0:T(8,128)S(1)}, u32[]{:S(2)}, u32[]{:S(2)}) async-start(f32[16,48,384]{2,1,0:T(8,128)} %broadcast_in_dim.21), calls=%async_computation.3 | async-start | bytes 2359296 | tf_op jit(solution)/shard_map/all_to_all | solution.py:24
  100.3 0.9 convolution_subtract_fusion.4
  101.4 0.9 convolution_subtract_fusion.5
  102.3 1.7 broadcast_select_fusion.1
  105.0 0.8 convolution_negate_fusion
  106.9 0.8 fusion.2
  108.1 0.8 fusion.1
  109.0 1.1 pad_maximum_fusion.1
  110.1 4.1 %all-to-all-done.3 = f32[16,48,384]{2,1,0:T(8,128)S(1)} async-done(((f32[16,48,384]{2,1,0:T(8,128)}), f32[16,48,384]{2,1,0:T(8,128)S(1)}, u32[]{:S(2)}, u32[]{:S(2)}) %all-to-all-start.3) | async-done | bytes 1179680 | tf_op jit(solution)/shard_map/all_to_all | solution.py:24
  114.2 5.1 %all-to-all-start.2 = ((f32[16,48,384]{2,1,0:T(8,128)}), f32[16,48,384]{2,1,0:T(8,128)S(1)}, u32[]{:S(2)}, u32[]{:S(2)}) async-start(f32[16,48,384]{2,1,0:T(8,128)} %bitcast.35), calls=%async_computation.2 | async-start | bytes 2359296 | tf_op jit(solution)/shard_map/all_to_all | solution.py:24
  119.4 1.9 %convolution_subtract_fusion.3 = f32[48,256]{1,0:T(8,128)} fusion(f32[48,256]{1,0:T(8,128)} %convolution_subtract_fusion.4, f32[48,256]{1,0:T(8,128)} %convolution_subtract_fusion.5, f32[256,128]{1,0:T(8,128)} %bitcast.111, f32[256,128]{1,0:T(8,128)} %bitcast.115), kind=kOutput, calls=%fused_computation.25 | convolution fusion | flops 37826560 | bytes 409600 | tf_op jit(solution)/shard_map/dot_general | solution.py:14
  123.2 1.2 convolution_subtract_fusion
  124.4 11.4 %all-to-all-done.2 = f32[16,48,384]{2,1,0:T(8,128)S(1)} async-done(((f32[16,48,384]{2,1,0:T(8,128)}), f32[16,48,384]{2,1,0:T(8,128)S(1)}, u32[]{:S(2)}, u32[]{:S(2)}) %all-to-all-start.2) | async-done | bytes 1179680 | tf_op jit(solution)/shard_map/all_to_all | solution.py:24
  135.9 1.7 fusion.9
  137.7 11.8 %all_to_all.35 = f32[8,1,4608]{2,1,0:T(1,128)S(1)} all-to-all(f32[8,1,4608]{2,1,0:T(1,128)S(1)} %reshape.230), channel_id=1, replica_groups={{0,1,2,3,4,5,6,7},{8,9,10,11,12,13,14,15},{16,17,18,19,20,21,22,23},{24..., dimensions={0} | all-to-all | bytes 294912 | tf_op jit(solution)/shard_map/all_to_all | solution.py:24
  149.7 19.2 %all_to_all.36 = f32[4,1,4608]{2,1,0:T(1,128)S(1)} all-to-all(f32[4,1,4608]{2,1,0:T(1,128)S(1)} %broadcast_in_dim.22), channel_id=1, replica_groups={{0,8,16,24},{1,9,17,25},{2,10,18,26},{3,11,19,27},{4,12,20,28},{5,13,21..., dimensions={0} | all-to-all | bytes 147456 | tf_op jit(solution)/shard_map/all_to_all | solution.py:24
  169.1 11.0 %all_to_all.37 = f32[8,1,4608]{2,1,0:T(1,128)S(1)} all-to-all(f32[8,1,4608]{2,1,0:T(1,128)S(1)} %broadcast_in_dim.23), channel_id=1, replica_groups={{0,1,2,3,4,5,6,7},{8,9,10,11,12,13,14,15},{16,17,18,19,20,21,22,23},{24..., dimensions={0} | all-to-all | bytes 294912 | tf_op jit(solution)/shard_map/all_to_all | solution.py:24
  (118 shorter events, 14.0 us)
Async XLA Ops:
  0.6 104.3 %copy-start = (f32[768,384]{1,0:T(8,128)S(1)}, f32[768,384]{1,0:T(8,128)}, u32[]{:S(2)}) copy-start(f32[768,384]{1,0:T(8,128)} %param.5) | copy-start | bytes 3538948
  0.6 52.4 %copy-start.22 = (f32[3,16,256]{2,1,0:T(8,128)S(1)}, f32[3,16,256]{2,1,0:T(8,128)}, u32[]{:S(2)}) copy-start(f32[3,16,256]{2,1,0:T(8,128)} %param.8) | copy-start | bytes 147460
  30.5 51.8 %copy-start.15 = (f32[1,96,768]{2,1,0:T(8,128)}, f32[1,96,768]{2,1,0:T(8,128)S(1)}, u32[]{:S(2)}) copy-start(f32[1,96,768]{2,1,0:T(8,128)S(1)} %get-tuple-element.24) | copy-start | bytes 884740
  30.5 51.7 %collective-permute-start.2 = (f32[96,768]{1,0:T(8,128)}, f32[96,768]{1,0:T(8,128)}, u32[]{:S(2)}, u32[]{:S(2)}) collective-permute-start(f32[96,768]{1,0:T(8,128)} %get-tuple-element.25), channel_id=1, source_target_pairs={{30,0},{31,1},{0,2},{1,3},{2,4},{3,5},{4,6},{5,7},{6,8},{7,9},{8,1... | collective-permute-start | bytes 884744 | tf_op jit(solution)/shard_map/ppermute | solution.py:116
  33.4 48.9 %collective-permute-start.1 = (f32[96,768]{1,0:T(8,128)}, f32[96,768]{1,0:T(8,128)}, u32[]{:S(2)}, u32[]{:S(2)}) collective-permute-start(f32[96,768]{1,0:T(8,128)} %get-tuple-element.25), channel_id=1, source_target_pairs={{4,0},{5,1},{6,2},{7,3},{8,4},{9,5},{10,6},{11,7},{12,8},{13,9},{1... | collective-permute-start | bytes 884744 | tf_op jit(solution)/shard_map/ppermute | solution.py:116
  37.1 45.2 %collective-permute-start = (f32[96,768]{1,0:T(8,128)}, f32[96,768]{1,0:T(8,128)}, u32[]{:S(2)}, u32[]{:S(2)}) collective-permute-start(f32[96,768]{1,0:T(8,128)} %get-tuple-element.25), channel_id=1, source_target_pairs={{2,0},{3,1},{4,2},{5,3},{6,4},{7,5},{8,6},{9,7},{10,8},{11,9},{12,... | collective-permute-start | bytes 884744 | tf_op jit(solution)/shard_map/ppermute | solution.py:116
  39.1 39.4 %collective-permute-start.4 = (f32[24,768]{1,0:T(8,128)S(1)}, f32[24,768]{1,0:T(8,128)S(1)}, u32[]{:S(2)}, u32[]{:S(2)}) collective-permute-start(f32[24,768]{1,0:T(8,128)S(1)} %multiply_bitcast_fusion), channel_id=1, source_target_pairs={{0,0},{1,1},{2,32},{3,33},{4,64},{5,65},{6,96},{7,97},{8,128},{9,1... | collective-permute-start | bytes 221192 | tf_op jit(solution)/shard_map/ppermute | solution.py:68
  40.4 29.4 %all-to-all-start = ((f32[8,1,1536]{2,1,0:T(1,128)}), f32[8,1,1536]{2,1,0:T(1,128)S(1)}, u32[]{:S(2)}, u32[]{:S(2)}) async-start(f32[8,1,1536]{2,1,0:T(1,128)} %broadcast_in_dim.18), calls=%async_computation | async-start | bytes 98304 | tf_op jit(solution)/shard_map/all_to_all | solution.py:24
  71.9 20.8 %all-to-all-start.1 = ((f32[16,112,128]{2,1,0:T(8,128)}), f32[16,112,128]{2,1,0:T(8,128)S(1)}, u32[]{:S(2)}, u32[]{:S(2)}) async-start(f32[16,112,128]{2,1,0:T(8,128)} %broadcast_in_dim.19), calls=%async_computation.1 | async-start | bytes 1835008 | tf_op jit(solution)/shard_map/all_to_all | solution.py:24
  78.5 3.8 %collective-permute-start.5 = (f32[24,384]{1,0:T(8,128)S(1)}, f32[24,384]{1,0:T(8,128)S(1)}, u32[]{:S(2)}, u32[]{:S(2)}) collective-permute-start(f32[24,384]{1,0:T(8,128)S(1)} %slice_select_fusion), channel_id=1, source_target_pairs={{0,1},{1,0},{2,3},{3,2},{4,5},{5,4},{6,7},{7,6},{8,9},{9,8},{10,11... | collective-permute-start | bytes 110600 | tf_op jit(solution)/shard_map/ppermute | solution.py:93
  84.6 17.7 %collective-permute-start.3 = (f32[4,96,768]{2,1,0:T(8,128)}, f32[4,96,768]{2,1,0:T(8,128)}, u32[]{:S(2)}, u32[]{:S(2)}) collective-permute-start(f32[4,96,768]{2,1,0:T(8,128)} %pad_maximum_fusion), channel_id=1, source_target_pairs={{0,1},{1,0},{2,3},{3,2},{4,5},{5,4},{6,7},{7,6},{8,9},{9,8},{10,11... | collective-permute-start | bytes 3538952 | tf_op jit(solution)/shard_map/ppermute | solution.py:120
  93.8 20.4 %all-to-all-start.3 = ((f32[16,48,384]{2,1,0:T(8,128)}), f32[16,48,384]{2,1,0:T(8,128)S(1)}, u32[]{:S(2)}, u32[]{:S(2)}) async-start(f32[16,48,384]{2,1,0:T(8,128)} %broadcast_in_dim.21), calls=%async_computation.3 | async-start | bytes 2359296 | tf_op jit(solution)/shard_map/all_to_all | solution.py:24
  98.0 7.8 %copy-start.1 = (f32[16,1,1,16,128]{4,3,2,1,0:T(8,128)}, f32[16,1,1,16,128]{4,3,2,1,0:T(8,128)S(1)}, u32[]{:S(2)}) copy-start(f32[16,1,1,16,128]{4,3,2,1,0:T(8,128)S(1)} %get-tuple-element.22) | copy-start | bytes 393220
  98.0 7.8 %copy-start.3 = (f32[16,1,1,16,128]{4,3,2,1,0:T(8,128)}, f32[16,1,1,16,128]{4,3,2,1,0:T(8,128)S(1)}, u32[]{:S(2)}) copy-start(f32[16,1,1,16,128]{4,3,2,1,0:T(8,128)S(1)} %get-tuple-element.23) | copy-start | bytes 393220
  98.0 8.4 %copy-start.11 = (f32[16,1,1,16,128]{4,3,2,1,0:T(8,128)}, f32[16,1,1,16,128]{4,3,2,1,0:T(8,128)S(1)}, u32[]{:S(2)}) copy-start(f32[16,1,1,16,128]{4,3,2,1,0:T(8,128)S(1)} %get-tuple-element.18) | copy-start | bytes 393220
  98.0 8.4 %copy-start.13 = (f32[16,1,1,16,128]{4,3,2,1,0:T(8,128)}, f32[16,1,1,16,128]{4,3,2,1,0:T(8,128)S(1)}, u32[]{:S(2)}) copy-start(f32[16,1,1,16,128]{4,3,2,1,0:T(8,128)S(1)} %get-tuple-element.21) | copy-start | bytes 393220
  98.0 9.7 %copy-start.7 = (f32[16,1,1,16,128]{4,3,2,1,0:T(8,128)}, f32[16,1,1,16,128]{4,3,2,1,0:T(8,128)S(1)}, u32[]{:S(2)}) copy-start(f32[16,1,1,16,128]{4,3,2,1,0:T(8,128)S(1)} %get-tuple-element.19) | copy-start | bytes 393220
  98.0 9.7 %copy-start.9 = (f32[16,1,1,16,128]{4,3,2,1,0:T(8,128)}, f32[16,1,1,16,128]{4,3,2,1,0:T(8,128)S(1)}, u32[]{:S(2)}) copy-start(f32[16,1,1,16,128]{4,3,2,1,0:T(8,128)S(1)} %get-tuple-element.20) | copy-start | bytes 393220
  98.8 3.4 %copy-start.16 = (f32[1,96,768]{2,1,0:T(8,128)S(1)}, f32[1,96,768]{2,1,0:T(8,128)}, u32[]{:S(2)}) copy-start(f32[1,96,768]{2,1,0:T(8,128)} %copy-done.15) | copy-start | bytes 884740
  100.3 3.7 %copy-start.17 = (f32[48,256]{1,0:T(8,128)}, f32[48,256]{1,0:T(8,128)S(1)}, u32[]{:S(2)}) copy-start(f32[48,256]{1,0:T(8,128)S(1)} %fusion.82) | copy-start | bytes 147460
  114.2 21.5 %all-to-all-start.2 = ((f32[16,48,384]{2,1,0:T(8,128)}), f32[16,48,384]{2,1,0:T(8,128)S(1)}, u32[]{:S(2)}, u32[]{:S(2)}) async-start(f32[16,48,384]{2,1,0:T(8,128)} %bitcast.35), calls=%async_computation.2 | async-start | bytes 2359296 | tf_op jit(solution)/shard_map/all_to_all | solution.py:24
  121.2 1.0 copy-start.14
  121.3 1.7 copy-start.5
  121.4 1.3 copy-start.2
  121.4 1.3 copy-start.4
  122.2 0.9 copy-start.8
  122.2 1.0 copy-start.10
  123.2 12.6 %copy-start.18 = (f32[48,256]{1,0:T(8,128)S(1)}, f32[48,256]{1,0:T(8,128)}, u32[]{:S(2)}) copy-start(f32[48,256]{1,0:T(8,128)} %copy-done.17) | copy-start | bytes 147460
  123.2 12.7 %copy-start.19 = (f32[48,256]{1,0:T(8,128)S(1)}, f32[48,256]{1,0:T(8,128)}, u32[]{:S(2)}) copy-start(f32[48,256]{1,0:T(8,128)} %convolution_subtract_fusion.5) | copy-start | bytes 147460
  124.4 11.5 %copy-start.6 = (f32[16,2,1,8,384]{4,3,2,1,0:T(8,128)S(1)}, f32[16,2,1,8,384]{4,3,2,1,0:T(8,128)}, u32[]{:S(2)}) copy-start(f32[16,2,1,8,384]{4,3,2,1,0:T(8,128)} %copy-done.5) | copy-start | bytes 1179652
  124.4 11.5 %copy-start.21 = (f32[48,256]{1,0:T(8,128)S(1)}, f32[48,256]{1,0:T(8,128)}, u32[]{:S(2)}) copy-start(f32[48,256]{1,0:T(8,128)} %convolution_subtract_fusion.3) | copy-start | bytes 147460
  135.9 13.8 %copy-start.20 = (f32[48,384]{1,0:T(8,128)}, f32[48,384]{1,0:T(8,128)S(1)}, u32[]{:S(2)}) copy-start(f32[48,384]{1,0:T(8,128)S(1)} %reduce_sum.27) | copy-start | bytes 221188
  (1 other events, 0.9 us)

commit v6 on v5

v6 whole, which is shorter than its diff:
```python
import jax
import jax.numpy as jnp
from jax import lax
from jax.sharding import PartitionSpec as P


TILE = 128
NSUPER = 3
NEAR = 4


def contract(left, right, left_dim, right_dim, precision=lax.Precision.HIGH):
    return lax.dot_general(
        left,
        right,
        (((left_dim,), (right_dim,)), ((), ())),
        precision=precision,
        preferred_element_type=jnp.float32,
    )


def exchange(blocks, axis, groups=None):
    return lax.all_to_all(blocks, axis, 0, 0, tiled=True, axis_index_groups=groups)


def spread(block, axis, groups=None):
    count = len(groups[0]) if groups else lax.axis_size(axis)
    return exchange(jnp.broadcast_to(block[None], (count,) + block.shape), axis, groups)


def per_device(inverse_sep, sep_panels, chain_panels, diag_inverse, tile_list):
    rows = lax.axis_size("row")
    cols = lax.axis_size("col")
    row = lax.axis_index("row")
    col = lax.axis_index("col")
    height, width = inverse_sep.shape
    nb_cols = sep_panels.shape[2]
    nb_rows = chain_panels.shape[1]
    nb = nb_cols * cols
    cores = cols // rows
    chips = cols // cores
    far = chips // NEAR
    core = col % cores
    chip = col // cores
    tiles = height // TILE
    npair = chain_panels.shape[0]
    slab = NSUPER * nb_cols
    own_rows = NSUPER * nb_rows
    far_groups = [
        [cores * (first + NEAR * i) + c for i in range(far)]
        for first in range(NEAR)
        for c in range(cores)
    ]
    near_groups = [
        [cores * (NEAR * i + j) + c for j in range(NEAR) for c in range(cores)] for i in range(far)
    ]
    swap = [(c, c ^ 1) for c in range(cols)]
    turn = [
        (r * cols + c, (c // cores) * cols + cores * r + c % cores)
        for r in range(rows)
        for c in range(cols)
    ]

    listed = lax.dynamic_slice_in_dim(tile_list, row * tiles, tiles, 1).astype(jnp.float32)
    mask = jnp.broadcast_to(listed[:, :, None], (NSUPER, tiles, TILE)).reshape(NSUPER, 1, height)
    local_panel = (jnp.swapaxes(sep_panels, 1, 2) * mask).reshape(slab, height)
    diag_cols = lax.dynamic_slice_in_dim(diag_inverse, col * nb_cols, nb_cols, 2)
    small = jnp.concatenate([chain_panels, diag_cols], axis=0)
    small_rows = (npair + NSUPER) * nb_cols
    small = jnp.swapaxes(small, 1, 2).reshape(1, small_rows * nb_rows)
    small = spread(small, "row").reshape(rows, small_rows, nb_rows)
    small = jnp.transpose(small, (1, 0, 2)).reshape(small_rows, nb)
    chain_cols, diag_cols = small[: npair * nb_cols], small[npair * nb_cols :]
    turned = lax.ppermute(local_panel, ("row", "col"), turn)

    own = lax.all_gather(
        jnp.concatenate([local_panel, chain_cols], axis=1),
        "col",
        axis=0,
        tiled=True,
        axis_index_groups=far_groups,
    )

    left, right = turned[:, :width], turned[:, width:]
    kept = jnp.where(core == 0, left, right)
    other = lax.ppermute(jnp.where(core == 0, right, left), "col", swap)
    pieces = [jnp.where(core == 0, kept, other), jnp.where(core == 0, other, kept)]
    col_panel = spread(jnp.concatenate(pieces, axis=0), "row")
    col_panel = col_panel.reshape(rows, cores, NSUPER, nb_cols, width)

    def from_chip(block, step):
        moves = [((c + cores * step) % cols, c) for c in range(cols)]
        return lax.ppermute(block, "col", moves)

    near = [own] + [from_chip(own, step) for step in (1, 2, -1)]
    mine = jnp.stack(near)
    theirs = lax.ppermute(mine, "col", swap)
    both = jnp.stack([jnp.where(core == 0, mine, theirs), jnp.where(core == 0, theirs, mine)])
    both = both.reshape(cores, NEAR, far, NSUPER, nb_cols, height + nb)
    turnover = chip % NEAR
    places = []
    for place in range(NEAR):
        choice = both[:, place]
        for t in range(1, NEAR):
            choice = jnp.where(turnover == t, both[:, (place - t) % NEAR], choice)
        places.append(choice)
    ordered = jnp.stack(places)
    ordered = jnp.transpose(ordered, (3, 2, 0, 1, 4, 5)).reshape(NSUPER, nb, height + nb)
    panel = [ordered[k, :, :height] for k in range(NSUPER)]
    chain = [ordered[p, :, height:] for p in range(npair)]

    part = []
    for k in range(NSUPER):
        acc = contract(panel[k], inverse_sep, 1, 0)
        for j in range(k):
            acc = acc + contract(chain[k * (k - 1) // 2 + j], part[j], 1, 0)
        part.append(-acc)
    outgoing = jnp.stack([x.reshape(rows, nb_rows, width) for x in part], axis=1)
    incoming = exchange(outgoing.reshape(rows, own_rows, width), "row")
    new_rows = jnp.sum(incoming, axis=0)

    col_panel = [col_panel[:, :, k].reshape(nb, width) for k in range(NSUPER)]
    solved = []
    for k in range(NSUPER):
        acc = col_panel[k]
        for j in range(k):
            acc = acc - contract(chain[k * (k - 1) // 2 + j], solved[j], 1, 0)
        solved.append(acc)
    solved = jnp.concatenate(solved, axis=0)
    exact = lax.Precision.HIGHEST
    place = row * nb_rows + lax.broadcasted_iota(jnp.int32, (nb_rows, nb), 0)
    unit = (lax.broadcasted_iota(jnp.int32, (nb_rows, nb), 1) == place).astype(jnp.float32)
    zero = jnp.zeros((nb_rows, nb), jnp.float32)
    cc = [lax.dynamic_slice_in_dim(chain[p], row * nb_rows, nb_rows, 0) for p in range(npair)]
    lead = [
        jnp.concatenate([unit, -cc[0], contract(cc[2], chain[0], 1, 0, exact) - cc[1]], axis=0),
        jnp.concatenate([zero, unit, -cc[2]], axis=0),
        jnp.concatenate([zero, zero, unit], axis=0),
    ]
    base = []
    for k in range(NSUPER):
        part_lead = lax.dynamic_slice_in_dim(lead[k], col * nb_cols, nb_cols, 1)
        acc = contract(part_lead, diag_cols[k * nb_cols : (k + 1) * nb_cols], 1, 0, exact)
        for j in range(k):
            acc = acc - contract(base[j], chain[k * (k - 1) // 2 + j], 1, 1, exact)
        base.append(acc)
    base = jnp.concatenate(base, axis=1)

    inner = base - contract(new_rows, solved, 1, 1)
    share = own_rows * NSUPER * nb // (NEAR * cores)
    near_sum = jnp.sum(exchange(inner.reshape(NEAR * cores, 1, share), "col", near_groups), axis=0)
    far_sum = jnp.sum(spread(near_sum, "col", far_groups), axis=0)
    state = spread(far_sum, "col", near_groups)
    return (
        new_rows.reshape(NSUPER, nb_rows, width),
        state.reshape(NSUPER, nb_rows, NSUPER * nb),
    )


def solution(mesh):
    in_specs = (
        P("row", "col"),
        P(None, "row", "col"),
        P(None, "row", "col"),
        P(None, "row", None),
        P(),
    )
    out_specs = (P(None, "row", "col"), P(None, "row", None))

    return jax.shard_map(
        per_device, mesh=mesh, in_specs=in_specs, out_specs=out_specs, check_vma=False
    )
```

time: 182 us -> 195 us (1.071)
  starting transfers between devices: 42.3 us -> 47.4 us
  local copies, waits for them, and re-layouts: 8.36 us -> 11.4 us
  matrix products: 13.7 us -> 16.1 us
    ppermute x3, waiting for transfers between devices: 0.01 us -> 15.4 us  [from_chip(): return lax.ppermute(block, 'col', moves)]
    all_to_all x4 -> x3, waiting for transfers between devices: 37.9 us -> 24.2 us  [exchange(): lax.all_to_all(blocks, axis, 0, 0, tiled=True, axis_index_groups=groups)]
    ppermute x1, starting transfers between devices: 2.25 us -> 8.74 us  [per_device(): theirs = lax.ppermute(mine, 'col', swap)]
    all_to_all x4 -> x3, starting transfers between devices: 27.9 us -> 22.9 us  [exchange(): lax.all_to_all(blocks, axis, 0, 0, tiled=True, axis_index_groups=groups)]
    slice x11, local copies, waits for them, and re-layouts: 0.69 us -> 4.09 us  [the longest x7 3.83 us: per_device(): diag_cols[k * nb_cols:(k + 1) * nb_cols]]
    ppermute x1, starting transfers between devices: 2.94 us -> 6.27 us  [per_device(): other = lax.ppermute(jnp.where(core == 0, right, left), 'col', swap)]
    dot_general x23 -> x17, matrix products: 13.7 us -> 16.1 us  [contract(): lax.dot_general(left, right, (((left_dim,), (right_dim,)), ((), ())), pre...]
  transfers between devices with their start and end apart: 10 -> 9, of which waited for: 5 -> 4; matrix products, arithmetic and copies ran while one was open for 12% -> 10% of each run, Pallas kernels for 0% -> 0%
where the time goes in v6:
time: 195 us; the launch traced here: 194 us
  blocking collectives  70.1 us (36%)
  starting transfers between devices  47.4 us (24%)
  waiting for transfers between devices  39.6 us (20%)
  matrix products  16.1 us (8%)
  local copies, waits for them, and re-layouts  11.4 us (6%)
  other arithmetic  8.3 us (4%)
    all_to_all x3, blocking collectives, exchange(): lax.all_to_all(blocks, axis, 0, 0, tiled=True, axis_index_groups=groups)  43.5 us
    all_gather x1, blocking collectives, per_device(): lax.all_gather(jnp.concatenate([local_panel, chain_cols], axis=1), 'col',...  26.6 us
    all_to_all x3, waiting for transfers between devices, exchange(): lax.all_to_all(blocks, axis, 0, 0, tiled=True, axis_index_groups=groups)  24.2 us
    all_to_all x3, starting transfers between devices, exchange(): lax.all_to_all(blocks, axis, 0, 0, tiled=True, axis_index_groups=groups)  22.9 us
    dot_general x17, matrix products, contract(): lax.dot_general(left, right, (((left_dim,), (right_dim,)), ((), ())), pre...  16.1 us
    ppermute x3, waiting for transfers between devices, from_chip(): return lax.ppermute(block, 'col', moves)  15.4 us
    ppermute x3, starting transfers between devices, from_chip(): return lax.ppermute(block, 'col', moves)  8.91 us
    ppermute x1, starting transfers between devices, per_device(): theirs = lax.ppermute(mine, 'col', swap)  8.74 us
  transfers between devices with their start and end apart: 9, of which 4 were waited for; matrix products, arithmetic and copies ran while one was open for 10% of the time, Pallas kernels for 0%

profile of v6, /device:TPU:1, one launch (start us, length us, event | category | flops | bytes accessed | tf_op | source)
XLA Modules:
  0.0 194.2 jit_solution(3859573017695370937)
XLA Ops:
  0.7 0.9 copy.58
  3.2 7.6 %all-to-all-start = ((f32[16,1,768]{2,1,0:T(1,128)}), f32[16,1,768]{2,1,0:T(1,128)S(1)}, u32[]{:S(2)}, u32[]{:S(2)}) async-start(f32[16,1,768]{2,1,0:T(1,128)} %broadcast_in_dim.16), calls=%async_computation | async-start | bytes 98304 | tf_op jit(solution)/shard_map/all_to_all | solution.py:23
  11.6 0.9 multiply_bitcast_fusion
  12.5 4.7 %all-to-all-done = f32[16,1,768]{2,1,0:T(1,128)S(1)} async-done(((f32[16,1,768]{2,1,0:T(1,128)}), f32[16,1,768]{2,1,0:T(1,128)S(1)}, u32[]{:S(2)}, u32[]{:S(2)}) %all-to-all-start) | async-done | bytes 49184 | tf_op jit(solution)/shard_map/all_to_all | solution.py:23
  18.3 26.6 %all_gather.3 = f32[96,1024]{1,0:T(8,128)S(1)} all-gather(f32[24,1024]{1,0:T(8,128)S(1)} %pad_maximum_fusion.3), channel_id=1, replica_groups={{0,8,16,24},{1,9,17,25},{2,10,18,26},{3,11,19,27},{4,12,20,28},{5,13,21..., dimensions={0}, use_global_device_ids=true | all-gather | bytes 491520 | tf_op jit(solution)/shard_map/all_gather | solution.py:76
  44.9 3.9 %collective-permute-start = (f32[96,1024]{1,0:T(8,128)S(1)}, f32[96,1024]{1,0:T(8,128)S(1)}, u32[]{:S(2)}, u32[]{:S(2)}) collective-permute-start(f32[96,1024]{1,0:T(8,128)S(1)} %all_gather.3), channel_id=1, source_target_pairs={{2,0},{3,1},{4,2},{5,3},{6,4},{7,5},{8,6},{9,7},{10,8},{11,9},{12,... | collective-permute-start | bytes 1179656 | tf_op jit(solution)/shard_map/ppermute | solution.py:93
  48.8 1.9 collective-permute-start.1
  50.7 3.1 %collective-permute-start.2 = (f32[96,1024]{1,0:T(8,128)S(1)}, f32[96,1024]{1,0:T(8,128)S(1)}, u32[]{:S(2)}, u32[]{:S(2)}) collective-permute-start(f32[96,1024]{1,0:T(8,128)S(1)} %all_gather.3), channel_id=1, source_target_pairs={{30,0},{31,1},{0,2},{1,3},{2,4},{3,5},{4,6},{5,7},{6,8},{7,9},{8,1... | collective-permute-start | bytes 1179656 | tf_op jit(solution)/shard_map/ppermute | solution.py:93
  54.5 6.3 %collective-permute-start.5 = (f32[24,384]{1,0:T(8,128)S(1)}, f32[24,384]{1,0:T(8,128)S(1)}, u32[]{:S(2)}, u32[]{:S(2)}) collective-permute-start(f32[24,384]{1,0:T(8,128)S(1)} %slice_select_fusion), channel_id=1, source_target_pairs={{0,1},{1,0},{2,3},{3,2},{4,5},{5,4},{6,7},{7,6},{8,9},{9,8},{10,11... | collective-permute-start | bytes 110600 | tf_op jit(solution)/shard_map/ppermute | solution.py:86
  60.8 15.4 %collective-permute-done.1 = f32[96,1024]{1,0:T(8,128)S(1)} collective-permute-done((f32[96,1024]{1,0:T(8,128)S(1)}, f32[96,1024]{1,0:T(8,128)S(1)}, u32[]{:S(2)}, u32[]{:S(2)}) %collective-permute-start.1) | collective-permute-done | bytes 393248 | tf_op jit(solution)/shard_map/ppermute | solution.py:93
  76.2 1.3 pad_maximum_fusion
  77.6 8.7 %collective-permute-start.3 = (f32[4,96,1024]{2,1,0:T(8,128)}, f32[4,96,1024]{2,1,0:T(8,128)}, u32[]{:S(2)}, u32[]{:S(2)}) collective-permute-start(f32[4,96,1024]{2,1,0:T(8,128)} %pad_maximum_fusion), channel_id=1, source_target_pairs={{0,1},{1,0},{2,3},{3,2},{4,5},{5,4},{6,7},{7,6},{8,9},{9,8},{10,11... | collective-permute-start | bytes 4718600 | tf_op jit(solution)/shard_map/ppermute | solution.py:97
  86.4 1.1 broadcast_in_dim.18
  87.5 10.2 %all-to-all-start.2 = ((f32[16,48,384]{2,1,0:T(8,128)}), f32[16,48,384]{2,1,0:T(8,128)S(1)}, u32[]{:S(2)}, u32[]{:S(2)}) async-start(f32[16,48,384]{2,1,0:T(8,128)} %broadcast_in_dim.18), calls=%async_computation.2 | async-start | bytes 2359296 | tf_op jit(solution)/shard_map/all_to_all | solution.py:23
  101.2 0.9 copy.70
  102.2 0.9 fusion.32
  103.0 12.3 %all-to-all-done.2 = f32[16,48,384]{2,1,0:T(8,128)S(1)} async-done(((f32[16,48,384]{2,1,0:T(8,128)}), f32[16,48,384]{2,1,0:T(8,128)S(1)}, u32[]{:S(2)}, u32[]{:S(2)}) %all-to-all-start.2) | async-done | bytes 1179680 | tf_op jit(solution)/shard_map/all_to_all | solution.py:23
  115.3 1.0 fusion.69
  116.4 2.0 %broadcast_select_fusion.1 = (f32[4,96,1024]{2,1,0:T(8,128)S(1)}, f32[4,96,1024]{2,1,0:T(8,128)S(1)}) fusion(f32[4,96,1024]{2,1,0:T(8,128)} %collective-permute-done.3, pred[]{:T(512)S(6)} %eq.14, f32[1,96,1024]{2,1,0:T(8,128)} %bitcast.139, f32[1,96,1024]{2,1,0:T(8,128)} %bitcast.137, f32[1,96,1024]{2,1,0:T(8,128)S(1)} %bitcast.135, ...), kind=kLoop, calls=%fused_computation.45 | loop fusion | flops 1966080 | bytes 6291457 | tf_op jit(solution)/shard_map/jit(_where)/select_n | solution.py:98
  124.0 1.1 pad_maximum_fusion.1
  125.1 5.1 %all-to-all-start.1 = ((f32[16,48,384]{2,1,0:T(8,128)}), f32[16,48,384]{2,1,0:T(8,128)S(1)}, u32[]{:S(2)}, u32[]{:S(2)}) async-start(f32[16,48,384]{2,1,0:T(8,128)} %bitcast.28), calls=%async_computation.1 | async-start | bytes 2359296 | tf_op jit(solution)/shard_map/all_to_all | solution.py:23
  130.8 1.3 convolution_subtract_fusion.5
  132.1 1.3 convolution_subtract_fusion.4
  133.4 1.9 convolution_subtract_fusion.3
  135.4 1.3 convolution_subtract_fusion.2
  136.7 1.3 convolution_subtract_fusion.1
  138.1 2.1 %convolution_subtract_fusion = f32[256,384]{1,0:T(8,128)} fusion(f32[256,384]{1,0:T(8,128)S(1)} %convolution_subtract_fusion.1, f32[256,384]{1,0:T(8,128)S(1)} %convolution_subtract_fusion.2, f32[3,256,1024]{2,1,0:T(8,128)} %bitcast.123), kind=kOutput, calls=%fused_computation.14 | convolution fusion | flops 151093248 | bytes 1441792 | tf_op jit(solution)/shard_map/dot_general | solution.py:13
  140.2 7.2 %all-to-all-done.1 = f32[16,48,384]{2,1,0:T(8,128)S(1)} async-done(((f32[16,48,384]{2,1,0:T(8,128)}), f32[16,48,384]{2,1,0:T(8,128)S(1)}, u32[]{:S(2)}, u32[]{:S(2)}) %all-to-all-start.1) | async-done | bytes 1179680 | tf_op jit(solution)/shard_map/all_to_all | solution.py:23
  147.5 1.7 fusion.9
  149.3 13.0 %all_to_all.30 = f32[8,1,4608]{2,1,0:T(1,128)S(1)} all-to-all(f32[8,1,4608]{2,1,0:T(1,128)S(1)} %reshape.216), channel_id=1, replica_groups={{0,1,2,3,4,5,6,7},{8,9,10,11,12,13,14,15},{16,17,18,19,20,21,22,23},{24..., dimensions={0} | all-to-all | bytes 294912 | tf_op jit(solution)/shard_map/all_to_all | solution.py:23
  162.5 19.5 %all_to_all.31 = f32[4,1,4608]{2,1,0:T(1,128)S(1)} all-to-all(f32[4,1,4608]{2,1,0:T(1,128)S(1)} %broadcast_in_dim.19), channel_id=1, replica_groups={{0,8,16,24},{1,9,17,25},{2,10,18,26},{3,11,19,27},{4,12,20,28},{5,13,21..., dimensions={0} | all-to-all | bytes 147456 | tf_op jit(solution)/shard_map/all_to_all | solution.py:23
  182.1 11.0 %all_to_all.32 = f32[8,1,4608]{2,1,0:T(1,128)S(1)} all-to-all(f32[8,1,4608]{2,1,0:T(1,128)S(1)} %broadcast_in_dim.40), channel_id=1, replica_groups={{0,1,2,3,4,5,6,7},{8,9,10,11,12,13,14,15},{16,17,18,19,20,21,22,23},{24..., dimensions={0} | all-to-all | bytes 294912 | tf_op jit(solution)/shard_map/all_to_all | solution.py:23
  (93 shorter events, 15.5 us)
Async XLA Ops:
  0.6 119.4 %copy-start = (f32[768,384]{1,0:T(8,128)S(1)}, f32[768,384]{1,0:T(8,128)}, u32[]{:S(2)}) copy-start(f32[768,384]{1,0:T(8,128)} %param.5) | copy-start | bytes 3538948
  3.2 14.0 %all-to-all-start = ((f32[16,1,768]{2,1,0:T(1,128)}), f32[16,1,768]{2,1,0:T(1,128)S(1)}, u32[]{:S(2)}, u32[]{:S(2)}) async-start(f32[16,1,768]{2,1,0:T(1,128)} %broadcast_in_dim.16), calls=%async_computation | async-start | bytes 98304 | tf_op jit(solution)/shard_map/all_to_all | solution.py:23
  17.5 0.8 copy-start.4
  44.9 15.9 %collective-permute-start = (f32[96,1024]{1,0:T(8,128)S(1)}, f32[96,1024]{1,0:T(8,128)S(1)}, u32[]{:S(2)}, u32[]{:S(2)}) collective-permute-start(f32[96,1024]{1,0:T(8,128)S(1)} %all_gather.3), channel_id=1, source_target_pairs={{2,0},{3,1},{4,2},{5,3},{6,4},{7,5},{8,6},{9,7},{10,8},{11,9},{12,... | collective-permute-start | bytes 1179656 | tf_op jit(solution)/shard_map/ppermute | solution.py:93
  48.8 27.4 %collective-permute-start.1 = (f32[96,1024]{1,0:T(8,128)S(1)}, f32[96,1024]{1,0:T(8,128)S(1)}, u32[]{:S(2)}, u32[]{:S(2)}) collective-permute-start(f32[96,1024]{1,0:T(8,128)S(1)} %all_gather.3), channel_id=1, source_target_pairs={{4,0},{5,1},{6,2},{7,3},{8,4},{9,5},{10,6},{11,7},{12,8},{13,9},{1... | collective-permute-start | bytes 1179656 | tf_op jit(solution)/shard_map/ppermute | solution.py:93
  50.7 25.5 %collective-permute-start.2 = (f32[96,1024]{1,0:T(8,128)S(1)}, f32[96,1024]{1,0:T(8,128)S(1)}, u32[]{:S(2)}, u32[]{:S(2)}) collective-permute-start(f32[96,1024]{1,0:T(8,128)S(1)} %all_gather.3), channel_id=1, source_target_pairs={{30,0},{31,1},{0,2},{1,3},{2,4},{3,5},{4,6},{5,7},{6,8},{7,9},{8,1... | collective-permute-start | bytes 1179656 | tf_op jit(solution)/shard_map/ppermute | solution.py:93
  53.8 0.7 collective-permute-start.4
  54.5 31.9 %collective-permute-start.5 = (f32[24,384]{1,0:T(8,128)S(1)}, f32[24,384]{1,0:T(8,128)S(1)}, u32[]{:S(2)}, u32[]{:S(2)}) collective-permute-start(f32[24,384]{1,0:T(8,128)S(1)} %slice_select_fusion), channel_id=1, source_target_pairs={{0,1},{1,0},{2,3},{3,2},{4,5},{5,4},{6,7},{7,6},{8,9},{9,8},{10,11... | collective-permute-start | bytes 110600 | tf_op jit(solution)/shard_map/ppermute | solution.py:86
  76.2 1.4 copy-start.2
  76.2 1.4 copy-start.3
  77.6 38.7 %collective-permute-start.3 = (f32[4,96,1024]{2,1,0:T(8,128)}, f32[4,96,1024]{2,1,0:T(8,128)}, u32[]{:S(2)}, u32[]{:S(2)}) collective-permute-start(f32[4,96,1024]{2,1,0:T(8,128)} %pad_maximum_fusion), channel_id=1, source_target_pairs={{0,1},{1,0},{2,3},{3,2},{4,5},{5,4},{6,7},{7,6},{8,9},{9,8},{10,11... | collective-permute-start | bytes 4718600 | tf_op jit(solution)/shard_map/ppermute | solution.py:97
  86.4 11.9 %copy-start.5 = (f32[16,48,16]{2,1,0:T(8,128)S(1)}, f32[16,48,16]{2,1,0:T(8,128)}, u32[]{:S(2)}) copy-start(f32[16,48,16]{2,1,0:T(8,128)} %copy-done.4) | copy-start | bytes 147460
  87.5 27.8 %all-to-all-start.2 = ((f32[16,48,384]{2,1,0:T(8,128)}), f32[16,48,384]{2,1,0:T(8,128)S(1)}, u32[]{:S(2)}, u32[]{:S(2)}) async-start(f32[16,48,384]{2,1,0:T(8,128)} %broadcast_in_dim.18), calls=%async_computation.2 | async-start | bytes 2359296 | tf_op jit(solution)/shard_map/all_to_all | solution.py:23
  119.9 3.2 %copy-start.1 = (f32[3,4,4,2,8,1024]{5,4,3,2,1,0:T(8,128)}, f32[3,4,4,2,8,1024]{5,4,3,2,1,0:T(8,128)S(1)}, u32[]{:S(2)}) copy-start(f32[3,4,4,2,8,1024]{5,4,3,2,1,0:T(8,128)S(1)} %copy.64) | copy-start | bytes 9437188
  125.1 5.2 %copy-start.16 = (f32[8,256]{1,0:T(8,128)S(1)}, f32[8,256]{1,0:T(8,128)}, u32[]{:S(2)}) copy-start(f32[8,256]{1,0:T(8,128)} %slice.99) | copy-start | bytes 24580
  125.1 5.4 %copy-start.15 = (f32[8,256]{1,0:T(8,128)S(1)}, f32[8,256]{1,0:T(8,128)}, u32[]{:S(2)}) copy-start(f32[8,256]{1,0:T(8,128)} %slice.101) | copy-start | bytes 24580
  125.1 5.4 %copy-start.17 = (f32[48]{0:T(128)S(1)}, f32[48]{0:T(128)}, u32[]{:S(2)}) copy-start(f32[48]{0:T(128)} %pad.9.clone) | copy-start | bytes 580
  125.1 7.0 %copy-start.12 = (f32[48,256]{1,0:T(8,128)S(1)}, f32[48,256]{1,0:T(8,128)}, u32[]{:S(2)}) copy-start(f32[48,256]{1,0:T(8,128)} %fusion.32) | copy-start | bytes 147460
  125.1 10.3 %copy-start.7 = (f32[16,2,1,8,384]{4,3,2,1,0:T(8,128)S(1)}, f32[16,2,1,8,384]{4,3,2,1,0:T(8,128)}, u32[]{:S(2)}) copy-start(f32[16,2,1,8,384]{4,3,2,1,0:T(8,128)} %get-tuple-element.15) | copy-start | bytes 1179652
  125.1 22.3 %all-to-all-start.1 = ((f32[16,48,384]{2,1,0:T(8,128)}), f32[16,48,384]{2,1,0:T(8,128)S(1)}, u32[]{:S(2)}, u32[]{:S(2)}) async-start(f32[16,48,384]{2,1,0:T(8,128)} %bitcast.28), calls=%async_computation.1 | async-start | bytes 2359296 | tf_op jit(solution)/shard_map/all_to_all | solution.py:23
  130.2 6.5 %copy-start.6 = (f32[16,2,1,8,384]{4,3,2,1,0:T(8,128)S(1)}, f32[16,2,1,8,384]{4,3,2,1,0:T(8,128)}, u32[]{:S(2)}) copy-start(f32[16,2,1,8,384]{4,3,2,1,0:T(8,128)} %get-tuple-element.16) | copy-start | bytes 1179652
  130.5 4.8 %copy-start.8 = (f32[48,256]{1,0:T(8,128)}, f32[48,256]{1,0:T(8,128)S(1)}, u32[]{:S(2)}) copy-start(f32[48,256]{1,0:T(8,128)S(1)} %fusion.39) | copy-start | bytes 147460
  132.1 3.3 %copy-start.10 = (f32[48,256]{1,0:T(8,128)}, f32[48,256]{1,0:T(8,128)S(1)}, u32[]{:S(2)}) copy-start(f32[48,256]{1,0:T(8,128)S(1)} %convolution_subtract_fusion.5) | copy-start | bytes 147460
  138.0 9.4 %copy-start.9 = (f32[48,256]{1,0:T(8,128)S(1)}, f32[48,256]{1,0:T(8,128)}, u32[]{:S(2)}) copy-start(f32[48,256]{1,0:T(8,128)} %copy-done.8) | copy-start | bytes 147460
  138.1 9.4 %copy-start.11 = (f32[48,256]{1,0:T(8,128)S(1)}, f32[48,256]{1,0:T(8,128)}, u32[]{:S(2)}) copy-start(f32[48,256]{1,0:T(8,128)} %copy-done.10) | copy-start | bytes 147460
  138.1 9.4 %copy-start.14 = (f32[48,256]{1,0:T(8,128)S(1)}, f32[48,256]{1,0:T(8,128)}, u32[]{:S(2)}) copy-start(f32[48,256]{1,0:T(8,128)} %convolution_subtract_fusion.3) | copy-start | bytes 147460
  147.5 45.7 %copy-start.13 = (f32[48,384]{1,0:T(8,128)}, f32[48,384]{1,0:T(8,128)S(1)}, u32[]{:S(2)}) copy-start(f32[48,384]{1,0:T(8,128)S(1)} %reduce_sum.27) | copy-start | bytes 221188

commit v7 on v6

--- a/solution.py
+++ b/solution.py
@@ -70,6 +70,7 @@
     small = jnp.swapaxes(small, 1, 2).reshape(1, small_rows * nb_rows)
     small = spread(small, "row").reshape(rows, small_rows, nb_rows)
     small = jnp.transpose(small, (1, 0, 2)).reshape(small_rows, nb)
+    small = lax.optimization_barrier(small)
     chain_cols, diag_cols = small[: npair * nb_cols], small[npair * nb_cols :]
     turned = lax.ppermute(local_panel, ("row", "col"), turn)
 
@@ -119,15 +120,10 @@
     incoming = exchange(outgoing.reshape(rows, own_rows, width), "row")
     new_rows = jnp.sum(incoming, axis=0)
 
-    col_panel = [col_panel[:, :, k].reshape(nb, width) for k in range(NSUPER)]
-    solved = []
-    for k in range(NSUPER):
-        acc = col_panel[k]
-        for j in range(k):
-            acc = acc - contract(chain[k * (k - 1) // 2 + j], solved[j], 1, 0)
-        solved.append(acc)
-    solved = jnp.concatenate(solved, axis=0)
     exact = lax.Precision.HIGHEST
+    col_panel = jnp.concatenate(
+        [col_panel[:, :, k].reshape(nb, width) for k in range(NSUPER)], axis=0
+    )
     place = row * nb_rows + lax.broadcasted_iota(jnp.int32, (nb_rows, nb), 0)
     unit = (lax.broadcasted_iota(jnp.int32, (nb_rows, nb), 1) == place).astype(jnp.float32)
     zero = jnp.zeros((nb_rows, nb), jnp.float32)
@@ -140,17 +136,23 @@
     base = []
     for k in range(NSUPER):
         part_lead = lax.dynamic_slice_in_dim(lead[k], col * nb_cols, nb_cols, 1)
-        acc = contract(part_lead, diag_cols[k * nb_cols : (k + 1) * nb_cols], 1, 0, exact)
-        for j in range(k):
-            acc = acc - contract(base[j], chain[k * (k - 1) // 2 + j], 1, 1, exact)
-        base.append(acc)
+        diag_part = diag_cols[k * nb_cols : (k + 1) * nb_cols]
+        base.append(contract(part_lead, diag_part, 1, 0, exact))
     base = jnp.concatenate(base, axis=1)
 
-    inner = base - contract(new_rows, solved, 1, 1)
-    share = own_rows * NSUPER * nb // (NEAR * cores)
-    near_sum = jnp.sum(exchange(inner.reshape(NEAR * cores, 1, share), "col", near_groups), axis=0)
+    inner = base - contract(new_rows, col_panel, 1, 1)
+    members = NEAR * cores
+    share = own_rows * NSUPER * nb // members
+    near_sum = jnp.sum(exchange(inner.reshape(members, 1, share), "col", near_groups), axis=0)
     far_sum = jnp.sum(spread(near_sum, "col", far_groups), axis=0)
-    state = spread(far_sum, "col", near_groups)
+    far_sum = far_sum.reshape(own_rows // members, NSUPER, nb)
+    final = []
+    for k in range(NSUPER):
+        acc = far_sum[:, k]
+        for j in range(k):
+            acc = acc - contract(final[j], chain[k * (k - 1) // 2 + j], 1, 1)
+        final.append(acc)
+    state = spread(jnp.stack(final, axis=1).reshape(1, share), "col", near_groups)
     return (
         new_rows.reshape(NSUPER, nb_rows, width),
         state.reshape(NSUPER, nb_rows, NSUPER * nb),

time: 195 us -> 198 us (1.015)
  waiting for transfers between devices: 39.6 us -> 51.3 us
  matrix products: 16.1 us -> 10.9 us
  local copies, waits for them, and re-layouts: 11.4 us -> 8.16 us
    all_to_all x3, waiting for transfers between devices: 24.2 us -> 35.9 us  [exchange(): lax.all_to_all(blocks, axis, 0, 0, tiled=True, axis_index_groups=groups)]
    dot_general x17 -> x14, matrix products: 16.1 us -> 10.9 us  [contract(): lax.dot_general(left, right, (((left_dim,), (right_dim,)), ((), ())), pre...]
    slice x8 -> x2, local copies, waits for them, and re-layouts: 4.86 us -> 1.1 us  [the longest x1 1.08 us: per_device(): col_panel[:, :, k].reshape(nb, width)]
  transfers between devices with their start and end apart: 9 -> 9, of which waited for: 4 -> 4; matrix products, arithmetic and copies ran while one was open for 10% -> 4% of each run, Pallas kernels for 0% -> 0%
where the time goes in v7:
time: 198 us; the launch traced here: 197 us
  blocking collectives  70.1 us (35%)
  waiting for transfers between devices  51.3 us (26%)
  starting transfers between devices  47.3 us (24%)
  matrix products  10.9 us (6%)
  other arithmetic  8.19 us (4%)
  local copies, waits for them, and re-layouts  8.16 us (4%)
    all_to_all x3, blocking collectives, exchange(): lax.all_to_all(blocks, axis, 0, 0, tiled=True, axis_index_groups=groups)  43.5 us
    all_to_all x3, waiting for transfers between devices, exchange(): lax.all_to_all(blocks, axis, 0, 0, tiled=True, axis_index_groups=groups)  35.9 us
    all_gather x1, blocking collectives, per_device(): lax.all_gather(jnp.concatenate([local_panel, chain_cols], axis=1), 'col',...  26.6 us
    all_to_all x3, starting transfers between devices, exchange(): lax.all_to_all(blocks, axis, 0, 0, tiled=True, axis_index_groups=groups)  22.7 us
    ppermute x3, waiting for transfers between devices, from_chip(): return lax.ppermute(block, 'col', moves)  15.4 us
    dot_general x14, matrix products, contract(): lax.dot_general(left, right, (((left_dim,), (right_dim,)), ((), ())), pre...  10.9 us
    ppermute x3, starting transfers between devices, from_chip(): return lax.ppermute(block, 'col', moves)  8.91 us
    ppermute x1, starting transfers between devices, per_device(): theirs = lax.ppermute(mine, 'col', swap)  8.74 us
  transfers between devices with their start and end apart: 9, of which 4 were waited for; matrix products, arithmetic and copies ran while one was open for 4% of the time, Pallas kernels for 0%

profile of v7, /device:TPU:1, one launch (start us, length us, event | category | flops | bytes accessed | tf_op | source)
XLA Modules:
  0.0 197.2 jit_solution(4260204739561311153)
XLA Ops:
  0.7 0.9 copy.69
  3.2 7.6 %all-to-all-start = ((f32[16,1,768]{2,1,0:T(1,128)}), f32[16,1,768]{2,1,0:T(1,128)S(1)}, u32[]{:S(2)}, u32[]{:S(2)}) async-start(f32[16,1,768]{2,1,0:T(1,128)} %broadcast_in_dim.18), calls=%async_computation | async-start | bytes 98304 | tf_op jit(solution)/shard_map/all_to_all | solution.py:23
  11.6 0.9 multiply_bitcast_fusion
  12.5 4.7 %all-to-all-done = f32[16,1,768]{2,1,0:T(1,128)S(1)} async-done(((f32[16,1,768]{2,1,0:T(1,128)}), f32[16,1,768]{2,1,0:T(1,128)S(1)}, u32[]{:S(2)}, u32[]{:S(2)}) %all-to-all-start) | async-done | bytes 49184 | tf_op jit(solution)/shard_map/all_to_all | solution.py:23
  17.7 26.6 %all_gather.3 = f32[96,1024]{1,0:T(8,128)S(1)} all-gather(f32[24,1024]{1,0:T(8,128)S(1)} %pad_maximum_fusion.3), channel_id=1, replica_groups={{0,8,16,24},{1,9,17,25},{2,10,18,26},{3,11,19,27},{4,12,20,28},{5,13,21..., dimensions={0}, use_global_device_ids=true | all-gather | bytes 491520 | tf_op jit(solution)/shard_map/all_gather | solution.py:77
  44.3 3.9 %collective-permute-start = (f32[96,1024]{1,0:T(8,128)S(1)}, f32[96,1024]{1,0:T(8,128)S(1)}, u32[]{:S(2)}, u32[]{:S(2)}) collective-permute-start(f32[96,1024]{1,0:T(8,128)S(1)} %all_gather.3), channel_id=1, source_target_pairs={{2,0},{3,1},{4,2},{5,3},{6,4},{7,5},{8,6},{9,7},{10,8},{11,9},{12,... | collective-permute-start | bytes 1179656 | tf_op jit(solution)/shard_map/ppermute | solution.py:94
  48.2 1.9 collective-permute-start.1
  50.2 3.1 %collective-permute-start.2 = (f32[96,1024]{1,0:T(8,128)S(1)}, f32[96,1024]{1,0:T(8,128)S(1)}, u32[]{:S(2)}, u32[]{:S(2)}) collective-permute-start(f32[96,1024]{1,0:T(8,128)S(1)} %all_gather.3), channel_id=1, source_target_pairs={{30,0},{31,1},{0,2},{1,3},{2,4},{3,5},{4,6},{5,7},{6,8},{7,9},{8,1... | collective-permute-start | bytes 1179656 | tf_op jit(solution)/shard_map/ppermute | solution.py:94
  54.0 6.3 %collective-permute-start.5 = (f32[24,384]{1,0:T(8,128)S(1)}, f32[24,384]{1,0:T(8,128)S(1)}, u32[]{:S(2)}, u32[]{:S(2)}) collective-permute-start(f32[24,384]{1,0:T(8,128)S(1)} %slice_select_fusion), channel_id=1, source_target_pairs={{0,1},{1,0},{2,3},{3,2},{4,5},{5,4},{6,7},{7,6},{8,9},{9,8},{10,11... | collective-permute-start | bytes 110600 | tf_op jit(solution)/shard_map/ppermute | solution.py:87
  60.3 15.4 %collective-permute-done.1 = f32[96,1024]{1,0:T(8,128)S(1)} collective-permute-done((f32[96,1024]{1,0:T(8,128)S(1)}, f32[96,1024]{1,0:T(8,128)S(1)}, u32[]{:S(2)}, u32[]{:S(2)}) %collective-permute-start.1) | collective-permute-done | bytes 393248 | tf_op jit(solution)/shard_map/ppermute | solution.py:94
  75.6 1.3 pad_maximum_fusion
  77.0 8.7 %collective-permute-start.3 = (f32[4,96,1024]{2,1,0:T(8,128)}, f32[4,96,1024]{2,1,0:T(8,128)}, u32[]{:S(2)}, u32[]{:S(2)}) collective-permute-start(f32[4,96,1024]{2,1,0:T(8,128)} %pad_maximum_fusion), channel_id=1, source_target_pairs={{0,1},{1,0},{2,3},{3,2},{4,5},{5,4},{6,7},{7,6},{8,9},{9,8},{10,11... | collective-permute-start | bytes 4718600 | tf_op jit(solution)/shard_map/ppermute | solution.py:98
  85.8 1.1 broadcast_in_dim.39
  86.9 10.2 %all-to-all-start.2 = ((f32[16,48,384]{2,1,0:T(8,128)}), f32[16,48,384]{2,1,0:T(8,128)S(1)}, u32[]{:S(2)}, u32[]{:S(2)}) async-start(f32[16,48,384]{2,1,0:T(8,128)} %broadcast_in_dim.39), calls=%async_computation.2 | async-start | bytes 2359296 | tf_op jit(solution)/shard_map/all_to_all | solution.py:23
  97.6 17.2 %all-to-all-done.2 = f32[16,48,384]{2,1,0:T(8,128)S(1)} async-done(((f32[16,48,384]{2,1,0:T(8,128)}), f32[16,48,384]{2,1,0:T(8,128)S(1)}, u32[]{:S(2)}, u32[]{:S(2)}) %all-to-all-start.2) | async-done | bytes 1179680 | tf_op jit(solution)/shard_map/all_to_all | solution.py:23
  114.8 1.1 fusion.71
  116.3 1.8 broadcast_select_fusion.1
  119.7 0.8 convolution_negate_fusion
  121.3 0.8 fusion.2
  122.5 0.8 fusion.1
  123.4 1.1 pad_maximum_fusion.1
  124.5 5.0 %all-to-all-start.1 = ((f32[16,48,384]{2,1,0:T(8,128)}), f32[16,48,384]{2,1,0:T(8,128)S(1)}, u32[]{:S(2)}, u32[]{:S(2)}) async-start(f32[16,48,384]{2,1,0:T(8,128)} %bitcast.29), calls=%async_computation.1 | async-start | bytes 2359296 | tf_op jit(solution)/shard_map/all_to_all | solution.py:23
  129.5 1.2 fusion.70
  130.8 1.2 convolution_subtract_fusion
  132.6 14.0 %all-to-all-done.1 = f32[16,48,384]{2,1,0:T(8,128)S(1)} async-done(((f32[16,48,384]{2,1,0:T(8,128)}), f32[16,48,384]{2,1,0:T(8,128)S(1)}, u32[]{:S(2)}, u32[]{:S(2)}) %all-to-all-start.1) | async-done | bytes 1179680 | tf_op jit(solution)/shard_map/all_to_all | solution.py:23
  146.8 1.6 fusion.9
  148.6 13.0 %all_to_all.30 = f32[8,1,4608]{2,1,0:T(1,128)S(1)} all-to-all(f32[8,1,4608]{2,1,0:T(1,128)S(1)} %reshape.218), channel_id=1, replica_groups={{0,1,2,3,4,5,6,7},{8,9,10,11,12,13,14,15},{16,17,18,19,20,21,22,23},{24..., dimensions={0} | all-to-all | bytes 294912 | tf_op jit(solution)/shard_map/all_to_all | solution.py:23
  161.7 19.5 %all_to_all.31 = f32[4,1,4608]{2,1,0:T(1,128)S(1)} all-to-all(f32[4,1,4608]{2,1,0:T(1,128)S(1)} %broadcast_in_dim.40), channel_id=1, replica_groups={{0,8,16,24},{1,9,17,25},{2,10,18,26},{3,11,19,27},{4,12,20,28},{5,13,21..., dimensions={0} | all-to-all | bytes 147456 | tf_op jit(solution)/shard_map/all_to_all | solution.py:23
  181.4 1.1 convolution_subtract_fusion.3
  182.5 1.2 convolution_subtract_fusion.2
  183.7 1.2 fusion.12
  185.1 11.0 %all_to_all.32 = f32[8,1,4608]{2,1,0:T(1,128)S(1)} all-to-all(f32[8,1,4608]{2,1,0:T(1,128)S(1)} %broadcast_in_dim.42), channel_id=1, replica_groups={{0,1,2,3,4,5,6,7},{8,9,10,11,12,13,14,15},{16,17,18,19,20,21,22,23},{24..., dimensions={0} | all-to-all | bytes 294912 | tf_op jit(solution)/shard_map/all_to_all | solution.py:23
  (70 shorter events, 9.7 us)
Async XLA Ops:
  0.6 119.1 %copy-start = (f32[768,384]{1,0:T(8,128)S(1)}, f32[768,384]{1,0:T(8,128)}, u32[]{:S(2)}) copy-start(f32[768,384]{1,0:T(8,128)} %param.5) | copy-start | bytes 3538948
  3.2 14.0 %all-to-all-start = ((f32[16,1,768]{2,1,0:T(1,128)}), f32[16,1,768]{2,1,0:T(1,128)S(1)}, u32[]{:S(2)}, u32[]{:S(2)}) async-start(f32[16,1,768]{2,1,0:T(1,128)} %broadcast_in_dim.18), calls=%async_computation | async-start | bytes 98304 | tf_op jit(solution)/shard_map/all_to_all | solution.py:23
  44.3 15.9 %collective-permute-start = (f32[96,1024]{1,0:T(8,128)S(1)}, f32[96,1024]{1,0:T(8,128)S(1)}, u32[]{:S(2)}, u32[]{:S(2)}) collective-permute-start(f32[96,1024]{1,0:T(8,128)S(1)} %all_gather.3), channel_id=1, source_target_pairs={{2,0},{3,1},{4,2},{5,3},{6,4},{7,5},{8,6},{9,7},{10,8},{11,9},{12,... | collective-permute-start | bytes 1179656 | tf_op jit(solution)/shard_map/ppermute | solution.py:94
  48.2 27.4 %collective-permute-start.1 = (f32[96,1024]{1,0:T(8,128)S(1)}, f32[96,1024]{1,0:T(8,128)S(1)}, u32[]{:S(2)}, u32[]{:S(2)}) collective-permute-start(f32[96,1024]{1,0:T(8,128)S(1)} %all_gather.3), channel_id=1, source_target_pairs={{4,0},{5,1},{6,2},{7,3},{8,4},{9,5},{10,6},{11,7},{12,8},{13,9},{1... | collective-permute-start | bytes 1179656 | tf_op jit(solution)/shard_map/ppermute | solution.py:94
  50.2 25.5 %collective-permute-start.2 = (f32[96,1024]{1,0:T(8,128)S(1)}, f32[96,1024]{1,0:T(8,128)S(1)}, u32[]{:S(2)}, u32[]{:S(2)}) collective-permute-start(f32[96,1024]{1,0:T(8,128)S(1)} %all_gather.3), channel_id=1, source_target_pairs={{30,0},{31,1},{0,2},{1,3},{2,4},{3,5},{4,6},{5,7},{6,8},{7,9},{8,1... | collective-permute-start | bytes 1179656 | tf_op jit(solution)/shard_map/ppermute | solution.py:94
  53.3 0.7 collective-permute-start.4
  54.0 31.8 %collective-permute-start.5 = (f32[24,384]{1,0:T(8,128)S(1)}, f32[24,384]{1,0:T(8,128)S(1)}, u32[]{:S(2)}, u32[]{:S(2)}) collective-permute-start(f32[24,384]{1,0:T(8,128)S(1)} %slice_select_fusion), channel_id=1, source_target_pairs={{0,1},{1,0},{2,3},{3,2},{4,5},{5,4},{6,7},{7,6},{8,9},{9,8},{10,11... | collective-permute-start | bytes 110600 | tf_op jit(solution)/shard_map/ppermute | solution.py:87
  75.6 1.3 copy-start.2
  75.6 1.4 copy-start.4
  77.0 38.8 %collective-permute-start.3 = (f32[4,96,1024]{2,1,0:T(8,128)}, f32[4,96,1024]{2,1,0:T(8,128)}, u32[]{:S(2)}, u32[]{:S(2)}) collective-permute-start(f32[4,96,1024]{2,1,0:T(8,128)} %pad_maximum_fusion), channel_id=1, source_target_pairs={{0,1},{1,0},{2,3},{3,2},{4,5},{5,4},{6,7},{7,6},{8,9},{9,8},{10,11... | collective-permute-start | bytes 4718600 | tf_op jit(solution)/shard_map/ppermute | solution.py:98
  86.9 27.8 %all-to-all-start.2 = ((f32[16,48,384]{2,1,0:T(8,128)}), f32[16,48,384]{2,1,0:T(8,128)S(1)}, u32[]{:S(2)}, u32[]{:S(2)}) async-start(f32[16,48,384]{2,1,0:T(8,128)} %broadcast_in_dim.39), calls=%async_computation.2 | async-start | bytes 2359296 | tf_op jit(solution)/shard_map/all_to_all | solution.py:23
  114.8 1.2 copy-start.3
  114.8 1.5 copy-start.5
  119.7 2.8 %copy-start.1 = (f32[3,4,4,2,8,1024]{5,4,3,2,1,0:T(8,128)}, f32[3,4,4,2,8,1024]{5,4,3,2,1,0:T(8,128)S(1)}, u32[]{:S(2)}) copy-start(f32[3,4,4,2,8,1024]{5,4,3,2,1,0:T(8,128)S(1)} %copy.76) | copy-start | bytes 9437188
  124.5 22.2 %all-to-all-start.1 = ((f32[16,48,384]{2,1,0:T(8,128)}), f32[16,48,384]{2,1,0:T(8,128)S(1)}, u32[]{:S(2)}, u32[]{:S(2)}) async-start(f32[16,48,384]{2,1,0:T(8,128)} %bitcast.29), calls=%async_computation.1 | async-start | bytes 2359296 | tf_op jit(solution)/shard_map/all_to_all | solution.py:23
  129.5 17.3 %copy-start.6 = (f32[16,2,1,8,384]{4,3,2,1,0:T(8,128)S(1)}, f32[16,2,1,8,384]{4,3,2,1,0:T(8,128)}, u32[]{:S(2)}) copy-start(f32[16,2,1,8,384]{4,3,2,1,0:T(8,128)} %get-tuple-element.15) | copy-start | bytes 1179652
  129.5 17.3 %copy-start.7 = (f32[16,2,1,8,384]{4,3,2,1,0:T(8,128)S(1)}, f32[16,2,1,8,384]{4,3,2,1,0:T(8,128)}, u32[]{:S(2)}) copy-start(f32[16,2,1,8,384]{4,3,2,1,0:T(8,128)} %get-tuple-element.16) | copy-start | bytes 1179652
  146.7 35.8 %copy-start.8 = (f32[48,384]{1,0:T(8,128)}, f32[48,384]{1,0:T(8,128)S(1)}, u32[]{:S(2)}) copy-start(f32[48,384]{1,0:T(8,128)S(1)} %reduce_sum.27) | copy-start | bytes 221188

commit v8 on v6

--- a/solution.py
+++ b/solution.py
@@ -70,6 +70,7 @@
     small = jnp.swapaxes(small, 1, 2).reshape(1, small_rows * nb_rows)
     small = spread(small, "row").reshape(rows, small_rows, nb_rows)
     small = jnp.transpose(small, (1, 0, 2)).reshape(small_rows, nb)
+    small = lax.optimization_barrier(small)
     chain_cols, diag_cols = small[: npair * nb_cols], small[npair * nb_cols :]
     turned = lax.ppermute(local_panel, ("row", "col"), turn)
 
@@ -88,26 +89,27 @@
     col_panel = spread(jnp.concatenate(pieces, axis=0), "row")
     col_panel = col_panel.reshape(rows, cores, NSUPER, nb_cols, width)
 
-    def from_chip(block, step):
-        moves = [((c + cores * step) % cols, c) for c in range(cols)]
+    def from_chip(block, steps):
+        moves = [((c + cores * steps[c % cores]) % cols, c) for c in range(cols)]
         return lax.ppermute(block, "col", moves)
 
-    near = [own] + [from_chip(own, step) for step in (1, 2, -1)]
-    mine = jnp.stack(near)
-    theirs = lax.ppermute(mine, "col", swap)
-    both = jnp.stack([jnp.where(core == 0, mine, theirs), jnp.where(core == 0, theirs, mine)])
-    both = both.reshape(cores, NEAR, far, NSUPER, nb_cols, height + nb)
-    turnover = chip % NEAR
-    places = []
-    for place in range(NEAR):
-        choice = both[:, place]
-        for t in range(1, NEAR):
-            choice = jnp.where(turnover == t, both[:, (place - t) % NEAR], choice)
-        places.append(choice)
-    ordered = jnp.stack(places)
-    ordered = jnp.transpose(ordered, (3, 2, 0, 1, 4, 5)).reshape(NSUPER, nb, height + nb)
-    panel = [ordered[k, :, :height] for k in range(NSUPER)]
-    chain = [ordered[p, :, height:] for p in range(npair)]
+    lines = jnp.zeros((far, NSUPER, NEAR, cores, nb_cols, height + nb), jnp.float32)
+
+    def place(lines, block, step, from_core):
+        block = block.reshape(far, NSUPER, 1, 1, nb_cols, height + nb)
+        start = (0, 0, (chip + step) % NEAR, from_core, 0, 0)
+        return lax.dynamic_update_slice(lines, block, start)
+
+    near = [from_chip(own, steps) for steps in ((1, 1), (-1, -1), (2, -2))]
+    theirs = lax.ppermute(own, "col", swap)
+    lines = place(lines, own, 0, core)
+    lines = place(lines, theirs, 0, 1 - core)
+    for block, step in zip(near, (1, -1, 2)):
+        theirs = lax.ppermute(block, "col", swap)
+        lines = place(lines, block, step, core)
+        lines = place(lines, theirs, step, 1 - core)
+    panel = [lines[:, k, ..., :height].reshape(nb, height) for k in range(NSUPER)]
+    chain = [lines[:, p, ..., height:].reshape(nb, nb) for p in range(npair)]
 
     part = []
     for k in range(NSUPER):
@@ -119,6 +121,7 @@
     incoming = exchange(outgoing.reshape(rows, own_rows, width), "row")
     new_rows = jnp.sum(incoming, axis=0)
 
+    exact = lax.Precision.HIGHEST
     col_panel = [col_panel[:, :, k].reshape(nb, width) for k in range(NSUPER)]
     solved = []
     for k in range(NSUPER):
@@ -127,9 +130,8 @@
             acc = acc - contract(chain[k * (k - 1) // 2 + j], solved[j], 1, 0)
         solved.append(acc)
     solved = jnp.concatenate(solved, axis=0)
-    exact = lax.Precision.HIGHEST
-    place = row * nb_rows + lax.broadcasted_iota(jnp.int32, (nb_rows, nb), 0)
-    unit = (lax.broadcasted_iota(jnp.int32, (nb_rows, nb), 1) == place).astype(jnp.float32)
+    spot = row * nb_rows + lax.broadcasted_iota(jnp.int32, (nb_rows, nb), 0)
+    unit = (lax.broadcasted_iota(jnp.int32, (nb_rows, nb), 1) == spot).astype(jnp.float32)
     zero = jnp.zeros((nb_rows, nb), jnp.float32)
     cc = [lax.dynamic_slice_in_dim(chain[p], row * nb_rows, nb_rows, 0) for p in range(npair)]
     lead = [
@@ -140,7 +142,8 @@
     base = []
     for k in range(NSUPER):
         part_lead = lax.dynamic_slice_in_dim(lead[k], col * nb_cols, nb_cols, 1)
-        acc = contract(part_lead, diag_cols[k * nb_cols : (k + 1) * nb_cols], 1, 0, exact)
+        diag_part = diag_cols[k * nb_cols : (k + 1) * nb_cols]
+        acc = contract(part_lead, diag_part, 1, 0, exact)
         for j in range(k):
             acc = acc - contract(base[j], chain[k * (k - 1) // 2 + j], 1, 1, exact)
         base.append(acc)

time: 195 us -> 182 us (0.933)
  waiting for transfers between devices: 39.6 us -> 22.4 us
  starting transfers between devices: 47.4 us -> 56.4 us
  local copies, waits for them, and re-layouts: 11.4 us -> 19.3 us
  matrix products: 16.1 us -> 9.04 us
  other arithmetic: 8.3 us -> 4.9 us
    ppermute x3, waiting for transfers between devices: 15.4 us -> 0.01 us  [from_chip(): return lax.ppermute(block, 'col', moves)]
    dynamic_update_slice x0 -> x8, local copies, waits for them, and re-layouts: none -> 9.19 us  [place(): return lax.dynamic_update_slice(lines, block, start)]
    ppermute x3, starting transfers between devices: 8.91 us -> 16.6 us  [from_chip(): return lax.ppermute(block, 'col', moves)]
    dot_general x17, matrix products: 16.1 us -> 9.04 us  [contract(): lax.dot_general(left, right, (((left_dim,), (right_dim,)), ((), ())), pre...]
    ppermute x1 -> x4, starting transfers between devices: 8.74 us -> 13.4 us  [the longest x1 6.71 us: per_device(): theirs = lax.ppermute(own, 'col', swap)]
    ppermute x1, starting transfers between devices: 6.27 us -> 1.92 us  [per_device(): other = lax.ppermute(jnp.where(core == 0, right, left), 'col', swap)]
    select_n x3 -> x0, other arithmetic: 3.03 us -> none  [the longest x1 1.98 us: per_device(): jnp.where(core == 0, mine, theirs)]
    all_to_all x3, waiting for transfers between devices: 24.2 us -> 21.5 us  [exchange(): lax.all_to_all(blocks, axis, 0, 0, tiled=True, axis_index_groups=groups)]
  transfers between devices with their start and end apart: 9 -> 12, of which waited for: 4 -> 3; matrix products, arithmetic and copies ran while one was open for 10% -> 15% of each run, Pallas kernels for 0% -> 0%
where the time goes in v8:
time: 182 us; the launch traced here: 181 us
  blocking collectives  68.2 us (37%)
  starting transfers between devices  56.4 us (31%)
  waiting for transfers between devices  22.4 us (12%)
  local copies, waits for them, and re-layouts  19.3 us (11%)
  matrix products  9.04 us (5%)
  other arithmetic  4.9 us (3%)
    all_to_all x3, blocking collectives, exchange(): lax.all_to_all(blocks, axis, 0, 0, tiled=True, axis_index_groups=groups)  41.2 us
    all_gather x1, blocking collectives, per_device(): lax.all_gather(jnp.concatenate([local_panel, chain_cols], axis=1), 'col',...  27 us
    all_to_all x3, starting transfers between devices, exchange(): lax.all_to_all(blocks, axis, 0, 0, tiled=True, axis_index_groups=groups)  23.8 us
    all_to_all x3, waiting for transfers between devices, exchange(): lax.all_to_all(blocks, axis, 0, 0, tiled=True, axis_index_groups=groups)  21.5 us
    ppermute x3, starting transfers between devices, from_chip(): return lax.ppermute(block, 'col', moves)  16.6 us
    dynamic_update_slice x8, local copies, waits for them, and re-layouts, place(): return lax.dynamic_update_slice(lines, block, start)  9.19 us
    dot_general x17, matrix products, contract(): lax.dot_general(left, right, (((left_dim,), (right_dim,)), ((), ())), pre...  9.04 us
    ppermute x1, starting transfers between devices, per_device(): theirs = lax.ppermute(own, 'col', swap)  6.71 us
  transfers between devices with their start and end apart: 12, of which 3 were waited for; matrix products, arithmetic and copies ran while one was open for 15% of the time, Pallas kernels for 0%

profile of v8, /device:TPU:1, one launch (start us, length us, event | category | flops | bytes accessed | tf_op | source)
XLA Modules:
  0.0 181.4 jit_solution(16533188434253471381)
XLA Ops:
  0.7 0.9 copy.62
  3.2 7.6 %all-to-all-start = ((f32[16,1,768]{2,1,0:T(1,128)}), f32[16,1,768]{2,1,0:T(1,128)S(1)}, u32[]{:S(2)}, u32[]{:S(2)}) async-start(f32[16,1,768]{2,1,0:T(1,128)} %broadcast_in_dim.19), calls=%async_computation | async-start | bytes 98304 | tf_op jit(solution)/shard_map/all_to_all | solution.py:23
  11.6 0.9 multiply_bitcast_fusion
  13.3 3.9 %all-to-all-done = f32[16,1,768]{2,1,0:T(1,128)S(1)} async-done(((f32[16,1,768]{2,1,0:T(1,128)}), f32[16,1,768]{2,1,0:T(1,128)S(1)}, u32[]{:S(2)}, u32[]{:S(2)}) %all-to-all-start) | async-done | bytes 49184 | tf_op jit(solution)/shard_map/all_to_all | solution.py:23
  17.7 27.0 %all_gather.3 = f32[96,1024]{1,0:T(8,128)S(1)} all-gather(f32[24,1024]{1,0:T(8,128)S(1)} %pad_maximum_fusion.1), channel_id=1, replica_groups={{0,8,16,24},{1,9,17,25},{2,10,18,26},{3,11,19,27},{4,12,20,28},{5,13,21..., dimensions={0}, use_global_device_ids=true | all-gather | bytes 491520 | tf_op jit(solution)/shard_map/all_gather | solution.py:77
  44.7 6.7 %collective-permute-start = (f32[96,1024]{1,0:T(8,128)S(1)}, f32[96,1024]{1,0:T(8,128)}, u32[]{:S(2)}, u32[]{:S(2)}) collective-permute-start(f32[96,1024]{1,0:T(8,128)S(1)} %all_gather.3), channel_id=1, source_target_pairs={{0,1},{1,0},{2,3},{3,2},{4,5},{5,4},{6,7},{7,6},{8,9},{9,8},{10,11... | collective-permute-start | bytes 1179656 | tf_op jit(solution)/shard_map/ppermute | solution.py:104
  51.4 7.6 %collective-permute-start.1 = (f32[96,1024]{1,0:T(8,128)S(1)}, f32[96,1024]{1,0:T(8,128)}, u32[]{:S(2)}, u32[]{:S(2)}) collective-permute-start(f32[96,1024]{1,0:T(8,128)S(1)} %all_gather.3), channel_id=1, source_target_pairs={{2,0},{3,1},{4,2},{5,3},{6,4},{7,5},{8,6},{9,7},{10,8},{11,9},{12,... | collective-permute-start | bytes 1179656 | tf_op jit(solution)/shard_map/ppermute | solution.py:94
  59.0 3.1 %collective-permute-start.3 = (f32[96,1024]{1,0:T(8,128)S(1)}, f32[96,1024]{1,0:T(8,128)}, u32[]{:S(2)}, u32[]{:S(2)}) collective-permute-start(f32[96,1024]{1,0:T(8,128)S(1)} %all_gather.3), channel_id=1, source_target_pairs={{30,0},{31,1},{0,2},{1,3},{2,4},{3,5},{4,6},{5,7},{6,8},{7,9},{8,1... | collective-permute-start | bytes 1179656 | tf_op jit(solution)/shard_map/ppermute | solution.py:94
  62.1 5.9 %collective-permute-start.5 = (f32[96,1024]{1,0:T(8,128)S(1)}, f32[96,1024]{1,0:T(8,128)S(1)}, u32[]{:S(2)}, u32[]{:S(2)}) collective-permute-start(f32[96,1024]{1,0:T(8,128)S(1)} %all_gather.3), channel_id=1, source_target_pairs={{4,0},{29,1},{6,2},{31,3},{8,4},{1,5},{10,6},{3,7},{12,8},{5,9},{1... | collective-permute-start | bytes 1179656 | tf_op jit(solution)/shard_map/ppermute | solution.py:94
  68.1 2.0 %broadcast_in_dim.16 = f32[4,3,4,2,8,1024]{5,4,3,2,0,1:T(8,128)} broadcast(f32[]{:T(128)} %constant.67.clone.1), dimensions={} | broadcast | bytes 3145732 | tf_op jit(solution)/shard_map/broadcast_in_dim | solution.py:96
  70.9 1.9 %collective-permute-start.8 = (f32[24,384]{1,0:T(8,128)S(1)}, f32[24,384]{1,0:T(8,128)S(1)}, u32[]{:S(2)}, u32[]{:S(2)}) collective-permute-start(f32[24,384]{1,0:T(8,128)S(1)} %slice_select_fusion), channel_id=1, source_target_pairs={{0,1},{1,0},{2,3},{3,2},{4,5},{5,4},{6,7},{7,6},{8,9},{9,8},{10,11... | collective-permute-start | bytes 110600 | tf_op jit(solution)/shard_map/ppermute | solution.py:87
  73.2 0.8 collective-permute-done.8
  74.0 1.1 broadcast_in_dim.42
  75.2 9.2 %all-to-all-start.2 = ((f32[16,48,384]{2,1,0:T(8,128)}), f32[16,48,384]{2,1,0:T(8,128)S(1)}, u32[]{:S(2)}, u32[]{:S(2)}) async-start(f32[16,48,384]{2,1,0:T(8,128)} %broadcast_in_dim.42), calls=%async_computation.2 | async-start | bytes 2359296 | tf_op jit(solution)/shard_map/all_to_all | solution.py:23
  84.4 2.3 %collective-permute-start.2 = (f32[96,1024]{1,0:T(8,128)}, f32[96,1024]{1,0:T(8,128)S(1)}, u32[]{:S(2)}, u32[]{:S(2)}) collective-permute-start(f32[96,1024]{1,0:T(8,128)} %collective-permute-done.1), channel_id=1, source_target_pairs={{0,1},{1,0},{2,3},{3,2},{4,5},{5,4},{6,7},{7,6},{8,9},{9,8},{10,11... | collective-permute-start | bytes 1179656 | tf_op jit(solution)/shard_map/ppermute | solution.py:108
  86.8 2.0 %collective-permute-start.4 = (f32[96,1024]{1,0:T(8,128)}, f32[96,1024]{1,0:T(8,128)S(1)}, u32[]{:S(2)}, u32[]{:S(2)}) collective-permute-start(f32[96,1024]{1,0:T(8,128)} %collective-permute-done.3), channel_id=1, source_target_pairs={{0,1},{1,0},{2,3},{3,2},{4,5},{5,4},{6,7},{7,6},{8,9},{9,8},{10,11... | collective-permute-start | bytes 1179656 | tf_op jit(solution)/shard_map/ppermute | solution.py:108
  88.8 2.4 %collective-permute-start.6 = (f32[96,1024]{1,0:T(8,128)S(1)}, f32[96,1024]{1,0:T(8,128)S(1)}, u32[]{:S(2)}, u32[]{:S(2)}) collective-permute-start(f32[96,1024]{1,0:T(8,128)S(1)} %collective-permute-done.5), channel_id=1, source_target_pairs={{0,1},{1,0},{2,3},{3,2},{4,5},{5,4},{6,7},{7,6},{8,9},{9,8},{10,11... | collective-permute-start | bytes 1179656 | tf_op jit(solution)/shard_map/ppermute | solution.py:108
  91.1 1.8 copy_dynamic-update-slice_fusion.6
  92.9 1.8 copy_dynamic-update-slice_fusion.5
  95.5 1.8 copy_dynamic-update-slice_fusion.3
  99.5 1.2 fusion.37
  100.7 1.8 fusion.36
  104.3 0.8 fusion.2
  106.4 1.1 pad_maximum_fusion
  109.0 7.0 %all-to-all-start.1 = ((f32[16,48,384]{2,1,0:T(8,128)}), f32[16,48,384]{2,1,0:T(8,128)}, u32[]{:S(2)}, u32[]{:S(2)}) async-start(f32[16,48,384]{2,1,0:T(8,128)} %bitcast.76), calls=%async_computation.1 | async-start | bytes 2359296 | tf_op jit(solution)/shard_map/all_to_all | solution.py:23
  115.9 1.0 convolution_subtract_fusion.3
  118.2 17.6 %all-to-all-done.1 = f32[16,48,384]{2,1,0:T(8,128)} async-done(((f32[16,48,384]{2,1,0:T(8,128)}), f32[16,48,384]{2,1,0:T(8,128)}, u32[]{:S(2)}, u32[]{:S(2)}) %all-to-all-start.1) | async-done | bytes 1179680 | tf_op jit(solution)/shard_map/all_to_all | solution.py:23
  135.8 1.3 reduce_sum.27
  137.2 1.5 fusion.9
  138.8 11.5 %all_to_all.30 = f32[8,1,4608]{2,1,0:T(1,128)S(1)} all-to-all(f32[8,1,4608]{2,1,0:T(1,128)S(1)} %reshape.85), channel_id=1, replica_groups={{0,1,2,3,4,5,6,7},{8,9,10,11,12,13,14,15},{16,17,18,19,20,21,22,23},{24..., dimensions={0} | all-to-all | bytes 294912 | tf_op jit(solution)/shard_map/all_to_all | solution.py:23
  150.5 18.7 %all_to_all.31 = f32[4,1,4608]{2,1,0:T(1,128)S(1)} all-to-all(f32[4,1,4608]{2,1,0:T(1,128)S(1)} %broadcast_in_dim.43), channel_id=1, replica_groups={{0,8,16,24},{1,9,17,25},{2,10,18,26},{3,11,19,27},{4,12,20,28},{5,13,21..., dimensions={0} | all-to-all | bytes 147456 | tf_op jit(solution)/shard_map/all_to_all | solution.py:23
  169.3 11.0 %all_to_all.32 = f32[8,1,4608]{2,1,0:T(1,128)S(1)} all-to-all(f32[8,1,4608]{2,1,0:T(1,128)S(1)} %broadcast_in_dim.44), channel_id=1, replica_groups={{0,1,2,3,4,5,6,7},{8,9,10,11,12,13,14,15},{16,17,18,19,20,21,22,23},{24..., dimensions={0} | all-to-all | bytes 294912 | tf_op jit(solution)/shard_map/all_to_all | solution.py:23
  (69 shorter events, 15.0 us)
Async XLA Ops:
  0.6 101.9 %copy-start = (f32[768,384]{1,0:T(8,128)S(1)}, f32[768,384]{1,0:T(8,128)}, u32[]{:S(2)}) copy-start(f32[768,384]{1,0:T(8,128)} %param.5) | copy-start | bytes 3538948
  3.2 14.0 %all-to-all-start = ((f32[16,1,768]{2,1,0:T(1,128)}), f32[16,1,768]{2,1,0:T(1,128)S(1)}, u32[]{:S(2)}, u32[]{:S(2)}) async-start(f32[16,1,768]{2,1,0:T(1,128)} %broadcast_in_dim.19), calls=%async_computation | async-start | bytes 98304 | tf_op jit(solution)/shard_map/all_to_all | solution.py:23
  12.5 58.4 %collective-permute-start.7 = (f32[24,768]{1,0:T(8,128)S(1)}, f32[24,768]{1,0:T(8,128)S(1)}, u32[]{:S(2)}, u32[]{:S(2)}) collective-permute-start(f32[24,768]{1,0:T(8,128)S(1)} %multiply_bitcast_fusion), channel_id=1, source_target_pairs={{0,0},{1,1},{2,32},{3,33},{4,64},{5,65},{6,96},{7,97},{8,128},{9,1... | collective-permute-start | bytes 221192 | tf_op jit(solution)/shard_map/ppermute | solution.py:75
  44.7 46.4 %collective-permute-start = (f32[96,1024]{1,0:T(8,128)S(1)}, f32[96,1024]{1,0:T(8,128)}, u32[]{:S(2)}, u32[]{:S(2)}) collective-permute-start(f32[96,1024]{1,0:T(8,128)S(1)} %all_gather.3), channel_id=1, source_target_pairs={{0,1},{1,0},{2,3},{3,2},{4,5},{5,4},{6,7},{7,6},{8,9},{9,8},{10,11... | collective-permute-start | bytes 1179656 | tf_op jit(solution)/shard_map/ppermute | solution.py:104
  51.4 33.0 %collective-permute-start.1 = (f32[96,1024]{1,0:T(8,128)S(1)}, f32[96,1024]{1,0:T(8,128)}, u32[]{:S(2)}, u32[]{:S(2)}) collective-permute-start(f32[96,1024]{1,0:T(8,128)S(1)} %all_gather.3), channel_id=1, source_target_pairs={{2,0},{3,1},{4,2},{5,3},{6,4},{7,5},{8,6},{9,7},{10,8},{11,9},{12,... | collective-permute-start | bytes 1179656 | tf_op jit(solution)/shard_map/ppermute | solution.py:94
  59.0 27.8 %collective-permute-start.3 = (f32[96,1024]{1,0:T(8,128)S(1)}, f32[96,1024]{1,0:T(8,128)}, u32[]{:S(2)}, u32[]{:S(2)}) collective-permute-start(f32[96,1024]{1,0:T(8,128)S(1)} %all_gather.3), channel_id=1, source_target_pairs={{30,0},{31,1},{0,2},{1,3},{2,4},{3,5},{4,6},{5,7},{6,8},{7,9},{8,1... | collective-permute-start | bytes 1179656 | tf_op jit(solution)/shard_map/ppermute | solution.py:94
  62.1 26.6 %collective-permute-start.5 = (f32[96,1024]{1,0:T(8,128)S(1)}, f32[96,1024]{1,0:T(8,128)S(1)}, u32[]{:S(2)}, u32[]{:S(2)}) collective-permute-start(f32[96,1024]{1,0:T(8,128)S(1)} %all_gather.3), channel_id=1, source_target_pairs={{4,0},{29,1},{6,2},{31,3},{8,4},{1,5},{10,6},{3,7},{12,8},{5,9},{1... | collective-permute-start | bytes 1179656 | tf_op jit(solution)/shard_map/ppermute | solution.py:94
  70.9 3.1 %collective-permute-start.8 = (f32[24,384]{1,0:T(8,128)S(1)}, f32[24,384]{1,0:T(8,128)S(1)}, u32[]{:S(2)}, u32[]{:S(2)}) collective-permute-start(f32[24,384]{1,0:T(8,128)S(1)} %slice_select_fusion), channel_id=1, source_target_pairs={{0,1},{1,0},{2,3},{3,2},{4,5},{5,4},{6,7},{7,6},{8,9},{9,8},{10,11... | collective-permute-start | bytes 110600 | tf_op jit(solution)/shard_map/ppermute | solution.py:87
  75.2 33.8 %all-to-all-start.2 = ((f32[16,48,384]{2,1,0:T(8,128)}), f32[16,48,384]{2,1,0:T(8,128)S(1)}, u32[]{:S(2)}, u32[]{:S(2)}) async-start(f32[16,48,384]{2,1,0:T(8,128)} %broadcast_in_dim.42), calls=%async_computation.2 | async-start | bytes 2359296 | tf_op jit(solution)/shard_map/all_to_all | solution.py:23
  84.4 10.3 %collective-permute-start.2 = (f32[96,1024]{1,0:T(8,128)}, f32[96,1024]{1,0:T(8,128)S(1)}, u32[]{:S(2)}, u32[]{:S(2)}) collective-permute-start(f32[96,1024]{1,0:T(8,128)} %collective-permute-done.1), channel_id=1, source_target_pairs={{0,1},{1,0},{2,3},{3,2},{4,5},{5,4},{6,7},{7,6},{8,9},{9,8},{10,11... | collective-permute-start | bytes 1179656 | tf_op jit(solution)/shard_map/ppermute | solution.py:108
  86.8 10.5 %collective-permute-start.4 = (f32[96,1024]{1,0:T(8,128)}, f32[96,1024]{1,0:T(8,128)S(1)}, u32[]{:S(2)}, u32[]{:S(2)}) collective-permute-start(f32[96,1024]{1,0:T(8,128)} %collective-permute-done.3), channel_id=1, source_target_pairs={{0,1},{1,0},{2,3},{3,2},{4,5},{5,4},{6,7},{7,6},{8,9},{9,8},{10,11... | collective-permute-start | bytes 1179656 | tf_op jit(solution)/shard_map/ppermute | solution.py:108
  88.8 10.0 %collective-permute-start.6 = (f32[96,1024]{1,0:T(8,128)S(1)}, f32[96,1024]{1,0:T(8,128)S(1)}, u32[]{:S(2)}, u32[]{:S(2)}) collective-permute-start(f32[96,1024]{1,0:T(8,128)S(1)} %collective-permute-done.5), channel_id=1, source_target_pairs={{0,1},{1,0},{2,3},{3,2},{4,5},{5,4},{6,7},{7,6},{8,9},{9,8},{10,11... | collective-permute-start | bytes 1179656 | tf_op jit(solution)/shard_map/ppermute | solution.py:108
  107.9 0.7 copy-start.1
  108.9 8.0 %copy-start.3 = (f32[48,256]{1,0:T(8,128)}, f32[48,256]{1,0:T(8,128)S(1)}, u32[]{:S(2)}) copy-start(f32[48,256]{1,0:T(8,128)S(1)} %convolution_subtract_fusion.5) | copy-start | bytes 147460
  109.0 26.9 %all-to-all-start.1 = ((f32[16,48,384]{2,1,0:T(8,128)}), f32[16,48,384]{2,1,0:T(8,128)}, u32[]{:S(2)}, u32[]{:S(2)}) async-start(f32[16,48,384]{2,1,0:T(8,128)} %bitcast.76), calls=%async_computation.1 | async-start | bytes 2359296 | tf_op jit(solution)/shard_map/all_to_all | solution.py:23
  117.0 20.1 %copy-start.2 = (f32[48,256]{1,0:T(8,128)S(1)}, f32[48,256]{1,0:T(8,128)}, u32[]{:S(2)}) copy-start(f32[48,256]{1,0:T(8,128)} %copy-done.1) | copy-start | bytes 147460
  137.2 44.3 %copy-start.4 = (f32[48,384]{1,0:T(8,128)}, f32[48,384]{1,0:T(8,128)S(1)}, u32[]{:S(2)}) copy-start(f32[48,384]{1,0:T(8,128)S(1)} %reduce_sum.27) | copy-start | bytes 221188

commit v9 on v6

--- a/solution.py
+++ b/solution.py
@@ -70,6 +70,7 @@
     small = jnp.swapaxes(small, 1, 2).reshape(1, small_rows * nb_rows)
     small = spread(small, "row").reshape(rows, small_rows, nb_rows)
     small = jnp.transpose(small, (1, 0, 2)).reshape(small_rows, nb)
+    small = lax.optimization_barrier(small)
     chain_cols, diag_cols = small[: npair * nb_cols], small[npair * nb_cols :]
     turned = lax.ppermute(local_panel, ("row", "col"), turn)
 
@@ -88,11 +89,11 @@
     col_panel = spread(jnp.concatenate(pieces, axis=0), "row")
     col_panel = col_panel.reshape(rows, cores, NSUPER, nb_cols, width)
 
-    def from_chip(block, step):
-        moves = [((c + cores * step) % cols, c) for c in range(cols)]
+    def from_chip(block, steps):
+        moves = [((c + cores * steps[c % cores]) % cols, c) for c in range(cols)]
         return lax.ppermute(block, "col", moves)
 
-    near = [own] + [from_chip(own, step) for step in (1, 2, -1)]
+    near = [own] + [from_chip(own, steps) for steps in ((1, 1), (2, -2), (-1, -1))]
     mine = jnp.stack(near)
     theirs = lax.ppermute(mine, "col", swap)
     both = jnp.stack([jnp.where(core == 0, mine, theirs), jnp.where(core == 0, theirs, mine)])
@@ -119,6 +120,7 @@
     incoming = exchange(outgoing.reshape(rows, own_rows, width), "row")
     new_rows = jnp.sum(incoming, axis=0)
 
+    exact = lax.Precision.HIGHEST
     col_panel = [col_panel[:, :, k].reshape(nb, width) for k in range(NSUPER)]
     solved = []
     for k in range(NSUPER):
@@ -127,9 +129,8 @@
             acc = acc - contract(chain[k * (k - 1) // 2 + j], solved[j], 1, 0)
         solved.append(acc)
     solved = jnp.concatenate(solved, axis=0)
-    exact = lax.Precision.HIGHEST
-    place = row * nb_rows + lax.broadcasted_iota(jnp.int32, (nb_rows, nb), 0)
-    unit = (lax.broadcasted_iota(jnp.int32, (nb_rows, nb), 1) == place).astype(jnp.float32)
+    spot = row * nb_rows + lax.broadcasted_iota(jnp.int32, (nb_rows, nb), 0)
+    unit = (lax.broadcasted_iota(jnp.int32, (nb_rows, nb), 1) == spot).astype(jnp.float32)
     zero = jnp.zeros((nb_rows, nb), jnp.float32)
     cc = [lax.dynamic_slice_in_dim(chain[p], row * nb_rows, nb_rows, 0) for p in range(npair)]
     lead = [
@@ -140,7 +141,8 @@
     base = []
     for k in range(NSUPER):
         part_lead = lax.dynamic_slice_in_dim(lead[k], col * nb_cols, nb_cols, 1)
-        acc = contract(part_lead, diag_cols[k * nb_cols : (k + 1) * nb_cols], 1, 0, exact)
+        diag_part = diag_cols[k * nb_cols : (k + 1) * nb_cols]
+        acc = contract(part_lead, diag_part, 1, 0, exact)
         for j in range(k):
             acc = acc - contract(base[j], chain[k * (k - 1) // 2 + j], 1, 1, exact)
         base.append(acc)

time: 195 us -> 190 us (0.974)
  local copies, waits for them, and re-layouts: 11.4 us -> 6.36 us
  blocking collectives: 70.1 us -> 65.7 us
  starting transfers between devices: 47.4 us -> 51.1 us
    all_to_all x3, waiting for transfers between devices: 24.2 us -> 32.4 us  [exchange(): lax.all_to_all(blocks, axis, 0, 0, tiled=True, axis_index_groups=groups)]
    ppermute x3, waiting for transfers between devices: 15.4 us -> 9.09 us  [from_chip(): return lax.ppermute(block, 'col', moves)]
    ppermute x1, starting transfers between devices: 8.74 us -> 13.7 us  [per_device(): theirs = lax.ppermute(mine, 'col', swap)]
    all_to_all x3, blocking collectives: 43.5 us -> 39 us  [exchange(): lax.all_to_all(blocks, axis, 0, 0, tiled=True, axis_index_groups=groups)]
    slice x7 -> x0, local copies, waits for them, and re-layouts: 3.83 us -> none  [per_device(): diag_cols[k * nb_cols:(k + 1) * nb_cols]]
  transfers between devices with their start and end apart: 9 -> 9, of which waited for: 4 -> 5; matrix products, arithmetic and copies ran while one was open for 10% -> 8% of each run, Pallas kernels for 0% -> 0%
where the time goes in v9:
time: 190 us; the launch traced here: 189 us
  blocking collectives  65.7 us (35%)
  starting transfers between devices  51.1 us (27%)
  waiting for transfers between devices  41.5 us (22%)
  matrix products  14.4 us (8%)
  other arithmetic  8.36 us (4%)
  local copies, waits for them, and re-layouts  6.36 us (3%)
    all_to_all x3, blocking collectives, exchange(): lax.all_to_all(blocks, axis, 0, 0, tiled=True, axis_index_groups=groups)  39 us
    all_to_all x3, waiting for transfers between devices, exchange(): lax.all_to_all(blocks, axis, 0, 0, tiled=True, axis_index_groups=groups)  32.4 us
    all_gather x1, blocking collectives, per_device(): lax.all_gather(jnp.concatenate([local_panel, chain_cols], axis=1), 'col',...  26.6 us
    all_to_all x3, starting transfers between devices, exchange(): lax.all_to_all(blocks, axis, 0, 0, tiled=True, axis_index_groups=groups)  21.5 us
    dot_general x17, matrix products, contract(): lax.dot_general(left, right, (((left_dim,), (right_dim,)), ((), ())), pre...  14.4 us
    ppermute x1, starting transfers between devices, per_device(): theirs = lax.ppermute(mine, 'col', swap)  13.7 us
    ppermute x3, waiting for transfers between devices, from_chip(): return lax.ppermute(block, 'col', moves)  9.09 us
    ppermute x3, starting transfers between devices, from_chip(): return lax.ppermute(block, 'col', moves)  7.74 us
  transfers between devices with their start and end apart: 9, of which 5 were waited for; matrix products, arithmetic and copies ran while one was open for 8% of the time, Pallas kernels for 0%

profile of v9, /device:TPU:1, one launch (start us, length us, event | category | flops | bytes accessed | tf_op | source)
XLA Modules:
  0.0 188.6 jit_solution(3495198286386101440)
XLA Ops:
  0.7 0.9 copy.53
  3.2 7.6 %all-to-all-start = ((f32[16,1,768]{2,1,0:T(1,128)}), f32[16,1,768]{2,1,0:T(1,128)S(1)}, u32[]{:S(2)}, u32[]{:S(2)}) async-start(f32[16,1,768]{2,1,0:T(1,128)} %broadcast_in_dim.16), calls=%async_computation | async-start | bytes 98304 | tf_op jit(solution)/shard_map/all_to_all | solution.py:23
  11.6 0.9 multiply_bitcast_fusion
  12.5 4.7 %all-to-all-done = f32[16,1,768]{2,1,0:T(1,128)S(1)} async-done(((f32[16,1,768]{2,1,0:T(1,128)}), f32[16,1,768]{2,1,0:T(1,128)S(1)}, u32[]{:S(2)}, u32[]{:S(2)}) %all-to-all-start) | async-done | bytes 49184 | tf_op jit(solution)/shard_map/all_to_all | solution.py:23
  17.7 26.6 %all_gather.3 = f32[96,1024]{1,0:T(8,128)S(1)} all-gather(f32[24,1024]{1,0:T(8,128)S(1)} %pad_maximum_fusion.3), channel_id=1, replica_groups={{0,8,16,24},{1,9,17,25},{2,10,18,26},{3,11,19,27},{4,12,20,28},{5,13,21..., dimensions={0}, use_global_device_ids=true | all-gather | bytes 491520 | tf_op jit(solution)/shard_map/all_gather | solution.py:77
  44.3 3.9 %collective-permute-start = (f32[96,1024]{1,0:T(8,128)S(1)}, f32[96,1024]{1,0:T(8,128)S(1)}, u32[]{:S(2)}, u32[]{:S(2)}) collective-permute-start(f32[96,1024]{1,0:T(8,128)S(1)} %all_gather.3), channel_id=1, source_target_pairs={{2,0},{3,1},{4,2},{5,3},{6,4},{7,5},{8,6},{9,7},{10,8},{11,9},{12,... | collective-permute-start | bytes 1179656 | tf_op jit(solution)/shard_map/ppermute | solution.py:94
  48.2 1.9 %collective-permute-start.1 = (f32[96,1024]{1,0:T(8,128)S(1)}, f32[96,1024]{1,0:T(8,128)S(1)}, u32[]{:S(2)}, u32[]{:S(2)}) collective-permute-start(f32[96,1024]{1,0:T(8,128)S(1)} %all_gather.3), channel_id=1, source_target_pairs={{4,0},{29,1},{6,2},{31,3},{8,4},{1,5},{10,6},{3,7},{12,8},{5,9},{1... | collective-permute-start | bytes 1179656 | tf_op jit(solution)/shard_map/ppermute | solution.py:94
  50.2 1.9 %collective-permute-start.2 = (f32[96,1024]{1,0:T(8,128)S(1)}, f32[96,1024]{1,0:T(8,128)S(1)}, u32[]{:S(2)}, u32[]{:S(2)}) collective-permute-start(f32[96,1024]{1,0:T(8,128)S(1)} %all_gather.3), channel_id=1, source_target_pairs={{30,0},{31,1},{0,2},{1,3},{2,4},{3,5},{4,6},{5,7},{6,8},{7,9},{8,1... | collective-permute-start | bytes 1179656 | tf_op jit(solution)/shard_map/ppermute | solution.py:94
  52.8 7.4 %collective-permute-start.5 = (f32[24,384]{1,0:T(8,128)S(1)}, f32[24,384]{1,0:T(8,128)S(1)}, u32[]{:S(2)}, u32[]{:S(2)}) collective-permute-start(f32[24,384]{1,0:T(8,128)S(1)} %slice_select_fusion), channel_id=1, source_target_pairs={{0,1},{1,0},{2,3},{3,2},{4,5},{5,4},{6,7},{7,6},{8,9},{9,8},{10,11... | collective-permute-start | bytes 110600 | tf_op jit(solution)/shard_map/ppermute | solution.py:87
  60.3 4.1 %collective-permute-done.1 = f32[96,1024]{1,0:T(8,128)S(1)} collective-permute-done((f32[96,1024]{1,0:T(8,128)S(1)}, f32[96,1024]{1,0:T(8,128)S(1)}, u32[]{:S(2)}, u32[]{:S(2)}) %collective-permute-start.1) | collective-permute-done | bytes 393248 | tf_op jit(solution)/shard_map/ppermute | solution.py:94
  64.4 4.9 %collective-permute-done.2 = f32[96,1024]{1,0:T(8,128)S(1)} collective-permute-done((f32[96,1024]{1,0:T(8,128)S(1)}, f32[96,1024]{1,0:T(8,128)S(1)}, u32[]{:S(2)}, u32[]{:S(2)}) %collective-permute-start.2) | collective-permute-done | bytes 393248 | tf_op jit(solution)/shard_map/ppermute | solution.py:94
  69.4 1.3 pad_maximum_fusion
  70.7 13.7 %collective-permute-start.3 = (f32[4,96,1024]{2,1,0:T(8,128)}, f32[4,96,1024]{2,1,0:T(8,128)}, u32[]{:S(2)}, u32[]{:S(2)}) collective-permute-start(f32[4,96,1024]{2,1,0:T(8,128)} %pad_maximum_fusion), channel_id=1, source_target_pairs={{0,1},{1,0},{2,3},{3,2},{4,5},{5,4},{6,7},{7,6},{8,9},{9,8},{10,11... | collective-permute-start | bytes 4718600 | tf_op jit(solution)/shard_map/ppermute | solution.py:98
  84.5 1.1 broadcast_in_dim.18
  85.6 10.1 %all-to-all-start.2 = ((f32[16,48,384]{2,1,0:T(8,128)}), f32[16,48,384]{2,1,0:T(8,128)S(1)}, u32[]{:S(2)}, u32[]{:S(2)}) async-start(f32[16,48,384]{2,1,0:T(8,128)} %broadcast_in_dim.18), calls=%async_computation.2 | async-start | bytes 2359296 | tf_op jit(solution)/shard_map/all_to_all | solution.py:23
  96.2 19.3 %all-to-all-done.2 = f32[16,48,384]{2,1,0:T(8,128)S(1)} async-done(((f32[16,48,384]{2,1,0:T(8,128)}), f32[16,48,384]{2,1,0:T(8,128)S(1)}, u32[]{:S(2)}, u32[]{:S(2)}) %all-to-all-start.2) | async-done | bytes 1179680 | tf_op jit(solution)/shard_map/all_to_all | solution.py:23
  115.4 1.0 fusion.72
  116.4 2.1 %broadcast_select_fusion.1 = (f32[4,96,1024]{2,1,0:T(8,128)S(1)}, f32[4,96,1024]{2,1,0:T(8,128)S(1)}) fusion(f32[4,96,1024]{2,1,0:T(8,128)} %collective-permute-done.3, pred[]{:T(512)S(6)} %eq.14, f32[1,96,1024]{2,1,0:T(8,128)} %bitcast.142, f32[1,96,1024]{2,1,0:T(8,128)} %bitcast.140, f32[1,96,1024]{2,1,0:T(8,128)} %bitcast.138, f32[1,96,1024]{2,1,0:T(8,128)S(1)} %bitcast.128), kind=kLoop, calls=%fused_computation.45 | loop fusion | flops 1966080 | bytes 6291457 | tf_op jit(solution)/shard_map/jit(_where)/select_n | solution.py:99
  123.3 0.8 fusion.1
  124.1 1.1 pad_maximum_fusion.1
  125.3 3.8 %all-to-all-start.1 = ((f32[16,48,384]{2,1,0:T(8,128)}), f32[16,48,384]{2,1,0:T(8,128)S(1)}, u32[]{:S(2)}, u32[]{:S(2)}) async-start(f32[16,48,384]{2,1,0:T(8,128)} %bitcast.29), calls=%async_computation.1 | async-start | bytes 2359296 | tf_op jit(solution)/shard_map/all_to_all | solution.py:23
  129.8 1.3 convolution_subtract_fusion.5
  131.1 1.3 convolution_subtract_fusion.4
  132.4 1.3 convolution_subtract_fusion.3
  133.7 1.3 convolution_subtract_fusion.2
  135.1 1.5 convolution_subtract_fusion.1
  136.6 1.3 convolution_subtract_fusion
  137.9 8.4 %all-to-all-done.1 = f32[16,48,384]{2,1,0:T(8,128)S(1)} async-done(((f32[16,48,384]{2,1,0:T(8,128)}), f32[16,48,384]{2,1,0:T(8,128)S(1)}, u32[]{:S(2)}, u32[]{:S(2)}) %all-to-all-start.1) | async-done | bytes 1179680 | tf_op jit(solution)/shard_map/all_to_all | solution.py:23
  146.4 1.7 fusion.9
  148.2 11.3 %all_to_all.30 = f32[8,1,4608]{2,1,0:T(1,128)S(1)} all-to-all(f32[8,1,4608]{2,1,0:T(1,128)S(1)} %reshape.214), channel_id=1, replica_groups={{0,1,2,3,4,5,6,7},{8,9,10,11,12,13,14,15},{16,17,18,19,20,21,22,23},{24..., dimensions={0} | all-to-all | bytes 294912 | tf_op jit(solution)/shard_map/all_to_all | solution.py:23
  159.7 16.7 %all_to_all.31 = f32[4,1,4608]{2,1,0:T(1,128)S(1)} all-to-all(f32[4,1,4608]{2,1,0:T(1,128)S(1)} %broadcast_in_dim.19), channel_id=1, replica_groups={{0,8,16,24},{1,9,17,25},{2,10,18,26},{3,11,19,27},{4,12,20,28},{5,13,21..., dimensions={0} | all-to-all | bytes 147456 | tf_op jit(solution)/shard_map/all_to_all | solution.py:23
  176.6 11.0 %all_to_all.32 = f32[8,1,4608]{2,1,0:T(1,128)S(1)} all-to-all(f32[8,1,4608]{2,1,0:T(1,128)S(1)} %broadcast_in_dim.40), channel_id=1, replica_groups={{0,1,2,3,4,5,6,7},{8,9,10,11,12,13,14,15},{16,17,18,19,20,21,22,23},{24..., dimensions={0} | all-to-all | bytes 294912 | tf_op jit(solution)/shard_map/all_to_all | solution.py:23
  (67 shorter events, 11.0 us)
Async XLA Ops:
  0.6 119.6 %copy-start = (f32[768,384]{1,0:T(8,128)S(1)}, f32[768,384]{1,0:T(8,128)}, u32[]{:S(2)}) copy-start(f32[768,384]{1,0:T(8,128)} %param.5) | copy-start | bytes 3538948
  3.2 14.0 %all-to-all-start = ((f32[16,1,768]{2,1,0:T(1,128)}), f32[16,1,768]{2,1,0:T(1,128)S(1)}, u32[]{:S(2)}, u32[]{:S(2)}) async-start(f32[16,1,768]{2,1,0:T(1,128)} %broadcast_in_dim.16), calls=%async_computation | async-start | bytes 98304 | tf_op jit(solution)/shard_map/all_to_all | solution.py:23
  44.3 15.9 %collective-permute-start = (f32[96,1024]{1,0:T(8,128)S(1)}, f32[96,1024]{1,0:T(8,128)S(1)}, u32[]{:S(2)}, u32[]{:S(2)}) collective-permute-start(f32[96,1024]{1,0:T(8,128)S(1)} %all_gather.3), channel_id=1, source_target_pairs={{2,0},{3,1},{4,2},{5,3},{6,4},{7,5},{8,6},{9,7},{10,8},{11,9},{12,... | collective-permute-start | bytes 1179656 | tf_op jit(solution)/shard_map/ppermute | solution.py:94
  48.2 16.2 %collective-permute-start.1 = (f32[96,1024]{1,0:T(8,128)S(1)}, f32[96,1024]{1,0:T(8,128)S(1)}, u32[]{:S(2)}, u32[]{:S(2)}) collective-permute-start(f32[96,1024]{1,0:T(8,128)S(1)} %all_gather.3), channel_id=1, source_target_pairs={{4,0},{29,1},{6,2},{31,3},{8,4},{1,5},{10,6},{3,7},{12,8},{5,9},{1... | collective-permute-start | bytes 1179656 | tf_op jit(solution)/shard_map/ppermute | solution.py:94
  50.2 19.2 %collective-permute-start.2 = (f32[96,1024]{1,0:T(8,128)S(1)}, f32[96,1024]{1,0:T(8,128)S(1)}, u32[]{:S(2)}, u32[]{:S(2)}) collective-permute-start(f32[96,1024]{1,0:T(8,128)S(1)} %all_gather.3), channel_id=1, source_target_pairs={{30,0},{31,1},{0,2},{1,3},{2,4},{3,5},{4,6},{5,7},{6,8},{7,9},{8,1... | collective-permute-start | bytes 1179656 | tf_op jit(solution)/shard_map/ppermute | solution.py:94
  52.1 0.7 collective-permute-start.4
  52.8 31.6 %collective-permute-start.5 = (f32[24,384]{1,0:T(8,128)S(1)}, f32[24,384]{1,0:T(8,128)S(1)}, u32[]{:S(2)}, u32[]{:S(2)}) collective-permute-start(f32[24,384]{1,0:T(8,128)S(1)} %slice_select_fusion), channel_id=1, source_target_pairs={{0,1},{1,0},{2,3},{3,2},{4,5},{5,4},{6,7},{7,6},{8,9},{9,8},{10,11... | collective-permute-start | bytes 110600 | tf_op jit(solution)/shard_map/ppermute | solution.py:87
  60.3 10.4 %copy-start.2 = (f32[96,1024]{1,0:T(8,128)}, f32[96,1024]{1,0:T(8,128)S(1)}, u32[]{:S(2)}) copy-start(f32[96,1024]{1,0:T(8,128)S(1)} %collective-permute-done) | copy-start | bytes 1179652
  64.4 6.2 %copy-start.3 = (f32[96,1024]{1,0:T(8,128)}, f32[96,1024]{1,0:T(8,128)S(1)}, u32[]{:S(2)}) copy-start(f32[96,1024]{1,0:T(8,128)S(1)} %collective-permute-done.1) | copy-start | bytes 1179652
  69.4 1.3 copy-start.4
  70.7 45.8 %collective-permute-start.3 = (f32[4,96,1024]{2,1,0:T(8,128)}, f32[4,96,1024]{2,1,0:T(8,128)}, u32[]{:S(2)}, u32[]{:S(2)}) collective-permute-start(f32[4,96,1024]{2,1,0:T(8,128)} %pad_maximum_fusion), channel_id=1, source_target_pairs={{0,1},{1,0},{2,3},{3,2},{4,5},{5,4},{6,7},{7,6},{8,9},{9,8},{10,11... | collective-permute-start | bytes 4718600 | tf_op jit(solution)/shard_map/ppermute | solution.py:98
  85.6 29.9 %all-to-all-start.2 = ((f32[16,48,384]{2,1,0:T(8,128)}), f32[16,48,384]{2,1,0:T(8,128)S(1)}, u32[]{:S(2)}, u32[]{:S(2)}) async-start(f32[16,48,384]{2,1,0:T(8,128)} %broadcast_in_dim.18), calls=%async_computation.2 | async-start | bytes 2359296 | tf_op jit(solution)/shard_map/all_to_all | solution.py:23
  120.1 3.2 %copy-start.1 = (f32[3,4,4,2,8,1024]{5,4,3,2,1,0:T(8,128)}, f32[3,4,4,2,8,1024]{5,4,3,2,1,0:T(8,128)S(1)}, u32[]{:S(2)}) copy-start(f32[3,4,4,2,8,1024]{5,4,3,2,1,0:T(8,128)S(1)} %copy.60) | copy-start | bytes 9437188
  125.3 8.4 %copy-start.6 = (f32[16,2,1,8,384]{4,3,2,1,0:T(8,128)S(1)}, f32[16,2,1,8,384]{4,3,2,1,0:T(8,128)}, u32[]{:S(2)}) copy-start(f32[16,2,1,8,384]{4,3,2,1,0:T(8,128)} %get-tuple-element.15) | copy-start | bytes 1179652
  125.3 21.1 %all-to-all-start.1 = ((f32[16,48,384]{2,1,0:T(8,128)}), f32[16,48,384]{2,1,0:T(8,128)S(1)}, u32[]{:S(2)}, u32[]{:S(2)}) async-start(f32[16,48,384]{2,1,0:T(8,128)} %bitcast.29), calls=%async_computation.1 | async-start | bytes 2359296 | tf_op jit(solution)/shard_map/all_to_all | solution.py:23
  129.1 6.0 %copy-start.5 = (f32[16,2,1,8,384]{4,3,2,1,0:T(8,128)S(1)}, f32[16,2,1,8,384]{4,3,2,1,0:T(8,128)}, u32[]{:S(2)}) copy-start(f32[16,2,1,8,384]{4,3,2,1,0:T(8,128)} %get-tuple-element.16) | copy-start | bytes 1179652
  135.1 1.5 copy-start.7
  146.4 41.2 %copy-start.8 = (f32[48,384]{1,0:T(8,128)}, f32[48,384]{1,0:T(8,128)S(1)}, u32[]{:S(2)}) copy-start(f32[48,384]{1,0:T(8,128)S(1)} %reduce_sum.27) | copy-start | bytes 221188

commit v10 on v9

--- a/solution.py
+++ b/solution.py
@@ -51,6 +51,10 @@
         for first in range(NEAR)
         for c in range(cores)
     ]
+    far_chips = [
+        [cores * (first + NEAR * i) + c for i in range(far) for c in range(cores)]
+        for first in range(NEAR)
+    ]
     near_groups = [
         [cores * (NEAR * i + j) + c for j in range(NEAR) for c in range(cores)] for i in range(far)
     ]
@@ -79,7 +83,7 @@
         "col",
         axis=0,
         tiled=True,
-        axis_index_groups=far_groups,
+        axis_index_groups=far_chips,
     )
 
     left, right = turned[:, :width], turned[:, width:]
@@ -93,20 +97,30 @@
         moves = [((c + cores * steps[c % cores]) % cols, c) for c in range(cols)]
         return lax.ppermute(block, "col", moves)
 
-    near = [own] + [from_chip(own, steps) for steps in ((1, 1), (2, -2), (-1, -1))]
-    mine = jnp.stack(near)
-    theirs = lax.ppermute(mine, "col", swap)
-    both = jnp.stack([jnp.where(core == 0, mine, theirs), jnp.where(core == 0, theirs, mine)])
-    both = both.reshape(cores, NEAR, far, NSUPER, nb_cols, height + nb)
+    wide = height + nb
+    own = own.reshape(far, cores, slab, wide)
+    half = jnp.where(core == 0, own[:, 0], own[:, 1]).reshape(far * slab, wide)
+    beside = from_chip(own.reshape(far * cores * slab, wide), (1, -1))
+    across = from_chip(half, (2, -2))
+    beside_other = lax.ppermute(beside, "col", swap)
+    across_other = lax.ppermute(across, "col", swap)
+    shape = (far, cores, NSUPER, nb_cols, wide)
+    after = jnp.where(core == 0, beside, beside_other).reshape(shape)
+    before = jnp.where(core == 0, beside_other, beside).reshape(shape)
+    halves = [
+        jnp.where(core == 0, across, across_other).reshape(far, slab, wide),
+        jnp.where(core == 0, across_other, across).reshape(far, slab, wide),
+    ]
+    blocks = [own.reshape(shape), after, jnp.stack(halves, axis=1).reshape(shape), before]
     turnover = chip % NEAR
     places = []
     for place in range(NEAR):
-        choice = both[:, place]
+        choice = blocks[place]
         for t in range(1, NEAR):
-            choice = jnp.where(turnover == t, both[:, (place - t) % NEAR], choice)
+            choice = jnp.where(turnover == t, blocks[(place - t) % NEAR], choice)
         places.append(choice)
     ordered = jnp.stack(places)
-    ordered = jnp.transpose(ordered, (3, 2, 0, 1, 4, 5)).reshape(NSUPER, nb, height + nb)
+    ordered = jnp.transpose(ordered, (3, 1, 0, 2, 4, 5)).reshape(NSUPER, nb, wide)
     panel = [ordered[k, :, :height] for k in range(NSUPER)]
     chain = [ordered[p, :, height:] for p in range(npair)]
 

time: 190 us -> 176 us (0.926)
  waiting for transfers between devices: 41.5 us -> 25.1 us
  starting transfers between devices: 51.1 us -> 44 us
  blocking collectives: 65.7 us -> 72.5 us
    ppermute x3 -> x2, waiting for transfers between devices: 9.09 us -> 0.01 us  [from_chip(): return lax.ppermute(block, 'col', moves)]
    ppermute x1 -> x2, starting transfers between devices: 13.7 us -> 6.17 us  [the longest x1 4.25 us: per_device(): across_other = lax.ppermute(across, 'col', swap)]
    all_to_all x3, waiting for transfers between devices: 32.4 us -> 25.1 us  [exchange(): lax.all_to_all(blocks, axis, 0, 0, tiled=True, axis_index_groups=groups)]
    ppermute x3 -> x2, starting transfers between devices: 7.74 us -> 15 us  [from_chip(): return lax.ppermute(block, 'col', moves)]
    all_gather x1, blocking collectives: 26.6 us -> 32.5 us  [per_device(): lax.all_gather(jnp.concatenate([local_panel, chain_cols], axis=1), 'col',...]
    ppermute x1, starting transfers between devices: 7.44 us -> 1.92 us  [per_device(): other = lax.ppermute(jnp.where(core == 0, right, left), 'col', swap)]
    select_n x3 -> x4, other arithmetic: 3.14 us -> 5 us  [the longest x1 2.09 us: per_device(): jnp.where(core == 0, across, across_other).reshape(far, slab, wide)]
  transfers between devices with their start and end apart: 9 -> 9, of which waited for: 5 -> 3; matrix products, arithmetic and copies ran while one was open for 8% -> 10% of each run, Pallas kernels for 0% -> 0%
where the time goes in v10:
time: 176 us; the launch traced here: 175 us
  blocking collectives  72.5 us (41%)
  starting transfers between devices  44 us (25%)
  waiting for transfers between devices  25.1 us (14%)
  matrix products  15.6 us (9%)
  other arithmetic  9.68 us (6%)
  local copies, waits for them, and re-layouts  7.14 us (4%)
    all_to_all x3, blocking collectives, exchange(): lax.all_to_all(blocks, axis, 0, 0, tiled=True, axis_index_groups=groups)  40 us
    all_gather x1, blocking collectives, per_device(): lax.all_gather(jnp.concatenate([local_panel, chain_cols], axis=1), 'col',...  32.5 us
    all_to_all x3, waiting for transfers between devices, exchange(): lax.all_to_all(blocks, axis, 0, 0, tiled=True, axis_index_groups=groups)  25.1 us
    all_to_all x3, starting transfers between devices, exchange(): lax.all_to_all(blocks, axis, 0, 0, tiled=True, axis_index_groups=groups)  20.2 us
    dot_general x17, matrix products, contract(): lax.dot_general(left, right, (((left_dim,), (right_dim,)), ((), ())), pre...  15.6 us
    ppermute x2, starting transfers between devices, from_chip(): return lax.ppermute(block, 'col', moves)  15 us
    ppermute x1, starting transfers between devices, per_device(): across_other = lax.ppermute(across, 'col', swap)  4.25 us
  transfers between devices with their start and end apart: 9, of which 3 were waited for; matrix products, arithmetic and copies ran while one was open for 10% of the time, Pallas kernels for 0%

profile of v10, /device:TPU:1, one launch (start us, length us, event | category | flops | bytes accessed | tf_op | source)
XLA Modules:
  0.0 175.1 jit_solution(14888061637345257470)
XLA Ops:
  0.7 0.9 copy.47
  3.2 7.6 %all-to-all-start = ((f32[16,1,768]{2,1,0:T(1,128)}), f32[16,1,768]{2,1,0:T(1,128)S(1)}, u32[]{:S(2)}, u32[]{:S(2)}) async-start(f32[16,1,768]{2,1,0:T(1,128)} %broadcast_in_dim.16), calls=%async_computation | async-start | bytes 98304 | tf_op jit(solution)/shard_map/all_to_all | solution.py:23
  11.6 0.9 multiply_bitcast_fusion
  13.2 4.0 %all-to-all-done = f32[16,1,768]{2,1,0:T(1,128)S(1)} async-done(((f32[16,1,768]{2,1,0:T(1,128)}), f32[16,1,768]{2,1,0:T(1,128)S(1)}, u32[]{:S(2)}, u32[]{:S(2)}) %all-to-all-start) | async-done | bytes 49184 | tf_op jit(solution)/shard_map/all_to_all | solution.py:23
  17.7 32.5 %all_gather.3 = f32[192,1024]{1,0:T(8,128)S(1)} all-gather(f32[24,1024]{1,0:T(8,128)S(1)} %pad_maximum_fusion.2), channel_id=1, replica_groups={{0,1,8,9,16,17,24,25},{2,3,10,11,18,19,26,27},{4,5,12,13,20,21,28,29},{..., dimensions={0}, use_global_device_ids=true | all-gather | bytes 884736 | tf_op jit(solution)/shard_map/all_gather | solution.py:81
  50.2 8.7 %collective-permute-start = (f32[192,1024]{1,0:T(8,128)S(1)}, f32[192,1024]{1,0:T(8,128)}, u32[]{:S(2)}, u32[]{:S(2)}) collective-permute-start(f32[192,1024]{1,0:T(8,128)S(1)} %all_gather.3), channel_id=1, source_target_pairs={{2,0},{31,1},{4,2},{1,3},{6,4},{3,5},{8,6},{5,7},{10,8},{7,9},{12,... | collective-permute-start | bytes 2359304 | tf_op jit(solution)/shard_map/ppermute | solution.py:98
  59.0 1.9 %collective-permute-start.5 = (f32[24,384]{1,0:T(8,128)S(1)}, f32[24,384]{1,0:T(8,128)S(1)}, u32[]{:S(2)}, u32[]{:S(2)}) collective-permute-start(f32[24,384]{1,0:T(8,128)S(1)} %slice_select_fusion.1), channel_id=1, source_target_pairs={{0,1},{1,0},{2,3},{3,2},{4,5},{5,4},{6,7},{7,6},{8,9},{9,8},{10,11... | collective-permute-start | bytes 110600 | tf_op jit(solution)/shard_map/ppermute | solution.py:91
  61.7 6.3 %collective-permute-start.2 = (f32[96,1024]{1,0:T(8,128)}, f32[96,1024]{1,0:T(8,128)}, u32[]{:S(2)}, u32[]{:S(2)}) collective-permute-start(f32[96,1024]{1,0:T(8,128)} %bitcast.7), channel_id=1, source_target_pairs={{4,0},{29,1},{6,2},{31,3},{8,4},{1,5},{10,6},{3,7},{12,8},{5,9},{1... | collective-permute-start | bytes 1179656 | tf_op jit(solution)/shard_map/ppermute | solution.py:98
  68.1 1.1 broadcast_in_dim.18
  69.2 8.8 %all-to-all-start.2 = ((f32[16,48,384]{2,1,0:T(8,128)}), f32[16,48,384]{2,1,0:T(8,128)S(1)}, u32[]{:S(2)}, u32[]{:S(2)}) async-start(f32[16,48,384]{2,1,0:T(8,128)} %broadcast_in_dim.18), calls=%async_computation.2 | async-start | bytes 2359296 | tf_op jit(solution)/shard_map/all_to_all | solution.py:23
  78.0 4.3 %collective-permute-start.3 = (f32[96,1024]{1,0:T(8,128)}, f32[96,1024]{1,0:T(8,128)}, u32[]{:S(2)}, u32[]{:S(2)}) collective-permute-start(f32[96,1024]{1,0:T(8,128)} %collective-permute-done.2), channel_id=1, source_target_pairs={{0,1},{1,0},{2,3},{3,2},{4,5},{5,4},{6,7},{7,6},{8,9},{9,8},{10,11... | collective-permute-start | bytes 1179656 | tf_op jit(solution)/shard_map/ppermute | solution.py:106
  82.3 1.9 %collective-permute-start.1 = (f32[192,1024]{1,0:T(8,128)}, f32[192,1024]{1,0:T(8,128)}, u32[]{:S(2)}, u32[]{:S(2)}) collective-permute-start(f32[192,1024]{1,0:T(8,128)} %collective-permute-done), channel_id=1, source_target_pairs={{0,1},{1,0},{2,3},{3,2},{4,5},{5,4},{6,7},{7,6},{8,9},{9,8},{10,11... | collective-permute-start | bytes 2359304 | tf_op jit(solution)/shard_map/ppermute | solution.py:105
  84.9 0.9 fusion.25
  85.9 2.1 %broadcast_select_fusion.3 = (f32[96,1024]{1,0:T(8,128)}, f32[96,1024]{1,0:T(8,128)}) fusion(f32[96,1024]{1,0:T(8,128)} %collective-permute-done.2, f32[96,1024]{1,0:T(8,128)} %collective-permute-done.3, pred[]{:T(512)S(6)} %eq.14), kind=kLoop, calls=%fused_computation.47 | loop fusion | flops 196608 | bytes 1572865 | tf_op jit(solution)/shard_map/jit(_where)/select_n | solution.py:111
  87.9 11.6 %all-to-all-done.2 = f32[16,48,384]{2,1,0:T(8,128)S(1)} async-done(((f32[16,48,384]{2,1,0:T(8,128)}), f32[16,48,384]{2,1,0:T(8,128)S(1)}, u32[]{:S(2)}, u32[]{:S(2)}) %all-to-all-start.2) | async-done | bytes 1179680 | tf_op jit(solution)/shard_map/all_to_all | solution.py:23
  99.5 1.0 fusion.61
  100.5 1.5 broadcast_select_fusion
  105.4 0.8 fusion.2
  106.6 0.8 fusion.1
  107.5 1.1 pad_maximum_fusion
  108.6 3.8 %all-to-all-start.1 = ((f32[16,48,384]{2,1,0:T(8,128)}), f32[16,48,384]{2,1,0:T(8,128)S(1)}, u32[]{:S(2)}, u32[]{:S(2)}) async-start(f32[16,48,384]{2,1,0:T(8,128)} %bitcast.28), calls=%async_computation.1 | async-start | bytes 2359296 | tf_op jit(solution)/shard_map/all_to_all | solution.py:23
  113.2 1.3 convolution_subtract_fusion.5
  114.5 1.3 convolution_subtract_fusion.4
  115.8 1.9 %convolution_subtract_fusion.3 = f32[48,256]{1,0:T(8,128)} fusion(f32[48,256]{1,0:T(8,128)S(1)} %convolution_subtract_fusion.4, f32[48,256]{1,0:T(8,128)S(1)} %convolution_subtract_fusion.5, f32[3,256,1024]{2,1,0:T(8,128)} %bitcast.106), kind=kOutput, calls=%fused_computation.18 | convolution fusion | flops 37761024 | bytes 409600 | tf_op jit(solution)/shard_map/dot_general | solution.py:13
  117.7 1.5 convolution_subtract_fusion.2
  119.2 1.3 convolution_subtract_fusion.1
  120.6 1.3 convolution_subtract_fusion
  121.9 9.5 %all-to-all-done.1 = f32[16,48,384]{2,1,0:T(8,128)S(1)} async-done(((f32[16,48,384]{2,1,0:T(8,128)}), f32[16,48,384]{2,1,0:T(8,128)S(1)}, u32[]{:S(2)}, u32[]{:S(2)}) %all-to-all-start.1) | async-done | bytes 1179680 | tf_op jit(solution)/shard_map/all_to_all | solution.py:23
  132.1 1.5 fusion.9
  133.8 10.2 %all_to_all.30 = f32[8,1,4608]{2,1,0:T(1,128)S(1)} all-to-all(f32[8,1,4608]{2,1,0:T(1,128)S(1)} %reshape.315), channel_id=1, replica_groups={{0,1,2,3,4,5,6,7},{8,9,10,11,12,13,14,15},{16,17,18,19,20,21,22,23},{24..., dimensions={0} | all-to-all | bytes 294912 | tf_op jit(solution)/shard_map/all_to_all | solution.py:23
  144.2 18.7 %all_to_all.31 = f32[4,1,4608]{2,1,0:T(1,128)S(1)} all-to-all(f32[4,1,4608]{2,1,0:T(1,128)S(1)} %broadcast_in_dim.19), channel_id=1, replica_groups={{0,8,16,24},{1,9,17,25},{2,10,18,26},{3,11,19,27},{4,12,20,28},{5,13,21..., dimensions={0} | all-to-all | bytes 147456 | tf_op jit(solution)/shard_map/all_to_all | solution.py:23
  163.1 11.0 %all_to_all.32 = f32[8,1,4608]{2,1,0:T(1,128)S(1)} all-to-all(f32[8,1,4608]{2,1,0:T(1,128)S(1)} %broadcast_in_dim.40), channel_id=1, replica_groups={{0,1,2,3,4,5,6,7},{8,9,10,11,12,13,14,15},{16,17,18,19,20,21,22,23},{24..., dimensions={0} | all-to-all | bytes 294912 | tf_op jit(solution)/shard_map/all_to_all | solution.py:23
  (71 shorter events, 11.7 us)
Async XLA Ops:
  0.6 102.9 %copy-start = (f32[768,384]{1,0:T(8,128)S(1)}, f32[768,384]{1,0:T(8,128)}, u32[]{:S(2)}) copy-start(f32[768,384]{1,0:T(8,128)} %param.5) | copy-start | bytes 3538948
  3.2 14.0 %all-to-all-start = ((f32[16,1,768]{2,1,0:T(1,128)}), f32[16,1,768]{2,1,0:T(1,128)S(1)}, u32[]{:S(2)}, u32[]{:S(2)}) async-start(f32[16,1,768]{2,1,0:T(1,128)} %broadcast_in_dim.16), calls=%async_computation | async-start | bytes 98304 | tf_op jit(solution)/shard_map/all_to_all | solution.py:23
  12.5 46.5 %collective-permute-start.4 = (f32[24,768]{1,0:T(8,128)S(1)}, f32[24,768]{1,0:T(8,128)S(1)}, u32[]{:S(2)}, u32[]{:S(2)}) collective-permute-start(f32[24,768]{1,0:T(8,128)S(1)} %multiply_bitcast_fusion), channel_id=1, source_target_pairs={{0,0},{1,1},{2,32},{3,33},{4,64},{5,65},{6,96},{7,97},{8,128},{9,1... | collective-permute-start | bytes 221192 | tf_op jit(solution)/shard_map/ppermute | solution.py:79
  17.6 67.3 %copy-start.2 = (f32[48,16,16]{0,2,1:T(8,128)}, f32[48,16,16]{0,2,1:T(8,128)S(1)}, u32[]{:S(2)}) copy-start(f32[48,16,16]{0,2,1:T(8,128)S(1)} %copy.49) | copy-start | bytes 147460
  50.2 32.1 %collective-permute-start = (f32[192,1024]{1,0:T(8,128)S(1)}, f32[192,1024]{1,0:T(8,128)}, u32[]{:S(2)}, u32[]{:S(2)}) collective-permute-start(f32[192,1024]{1,0:T(8,128)S(1)} %all_gather.3), channel_id=1, source_target_pairs={{2,0},{31,1},{4,2},{1,3},{6,4},{3,5},{8,6},{5,7},{10,8},{7,9},{12,... | collective-permute-start | bytes 2359304 | tf_op jit(solution)/shard_map/ppermute | solution.py:98
  59.0 9.0 %collective-permute-start.5 = (f32[24,384]{1,0:T(8,128)S(1)}, f32[24,384]{1,0:T(8,128)S(1)}, u32[]{:S(2)}, u32[]{:S(2)}) collective-permute-start(f32[24,384]{1,0:T(8,128)S(1)} %slice_select_fusion.1), channel_id=1, source_target_pairs={{0,1},{1,0},{2,3},{3,2},{4,5},{5,4},{6,7},{7,6},{8,9},{9,8},{10,11... | collective-permute-start | bytes 110600 | tf_op jit(solution)/shard_map/ppermute | solution.py:91
  61.7 16.3 %collective-permute-start.2 = (f32[96,1024]{1,0:T(8,128)}, f32[96,1024]{1,0:T(8,128)}, u32[]{:S(2)}, u32[]{:S(2)}) collective-permute-start(f32[96,1024]{1,0:T(8,128)} %bitcast.7), channel_id=1, source_target_pairs={{4,0},{29,1},{6,2},{31,3},{8,4},{1,5},{10,6},{3,7},{12,8},{5,9},{1... | collective-permute-start | bytes 1179656 | tf_op jit(solution)/shard_map/ppermute | solution.py:98
  69.2 30.3 %all-to-all-start.2 = ((f32[16,48,384]{2,1,0:T(8,128)}), f32[16,48,384]{2,1,0:T(8,128)S(1)}, u32[]{:S(2)}, u32[]{:S(2)}) async-start(f32[16,48,384]{2,1,0:T(8,128)} %broadcast_in_dim.18), calls=%async_computation.2 | async-start | bytes 2359296 | tf_op jit(solution)/shard_map/all_to_all | solution.py:23
  78.0 7.8 %collective-permute-start.3 = (f32[96,1024]{1,0:T(8,128)}, f32[96,1024]{1,0:T(8,128)}, u32[]{:S(2)}, u32[]{:S(2)}) collective-permute-start(f32[96,1024]{1,0:T(8,128)} %collective-permute-done.2), channel_id=1, source_target_pairs={{0,1},{1,0},{2,3},{3,2},{4,5},{5,4},{6,7},{7,6},{8,9},{9,8},{10,11... | collective-permute-start | bytes 1179656 | tf_op jit(solution)/shard_map/ppermute | solution.py:106
  82.3 18.2 %collective-permute-start.1 = (f32[192,1024]{1,0:T(8,128)}, f32[192,1024]{1,0:T(8,128)}, u32[]{:S(2)}, u32[]{:S(2)}) collective-permute-start(f32[192,1024]{1,0:T(8,128)} %collective-permute-done), channel_id=1, source_target_pairs={{0,1},{1,0},{2,3},{3,2},{4,5},{5,4},{6,7},{7,6},{8,9},{9,8},{10,11... | collective-permute-start | bytes 2359304 | tf_op jit(solution)/shard_map/ppermute | solution.py:105
  99.5 2.5 %copy-start.5 = (f32[96,1024]{1,0:T(8,128)S(1)}, f32[96,1024]{1,0:T(8,128)}, u32[]{:S(2)}) copy-start(f32[96,1024]{1,0:T(8,128)} %get-tuple-element.14) | copy-start | bytes 1179652
  99.5 2.5 %copy-start.6 = (f32[96,1024]{1,0:T(8,128)S(1)}, f32[96,1024]{1,0:T(8,128)}, u32[]{:S(2)}) copy-start(f32[96,1024]{1,0:T(8,128)} %get-tuple-element.15) | copy-start | bytes 1179652
  103.5 3.2 %copy-start.1 = (f32[3,4,4,2,8,1024]{5,4,3,2,1,0:T(8,128)}, f32[3,4,4,2,8,1024]{5,4,3,2,1,0:T(8,128)S(1)}, u32[]{:S(2)}) copy-start(f32[3,4,4,2,8,1024]{5,4,3,2,1,0:T(8,128)S(1)} %copy.53) | copy-start | bytes 9437188
  107.5 5.0 %copy-start.3 = (f32[48,16,16]{0,2,1:T(8,128)S(1)}, f32[48,16,16]{0,2,1:T(8,128)}, u32[]{:S(2)}) copy-start(f32[48,16,16]{0,2,1:T(8,128)} %copy-done.2) | copy-start | bytes 147460
  107.5 5.3 %copy-start.10 = (f32[48]{0:T(128)S(1)}, f32[48]{0:T(128)}, u32[]{:S(2)}) copy-start(f32[48]{0:T(128)} %pad.9.clone) | copy-start | bytes 580
  107.5 7.0 %copy-start.9 = (f32[48,256]{1,0:T(8,128)S(1)}, f32[48,256]{1,0:T(8,128)}, u32[]{:S(2)}) copy-start(f32[48,256]{1,0:T(8,128)} %fusion.25) | copy-start | bytes 147460
  108.6 10.6 %copy-start.4 = (f32[16,2,1,8,384]{4,3,2,1,0:T(8,128)S(1)}, f32[16,2,1,8,384]{4,3,2,1,0:T(8,128)}, u32[]{:S(2)}) copy-start(f32[16,2,1,8,384]{4,3,2,1,0:T(8,128)} %get-tuple-element.12) | copy-start | bytes 1179652
  108.6 22.8 %all-to-all-start.1 = ((f32[16,48,384]{2,1,0:T(8,128)}), f32[16,48,384]{2,1,0:T(8,128)S(1)}, u32[]{:S(2)}, u32[]{:S(2)}) async-start(f32[16,48,384]{2,1,0:T(8,128)} %bitcast.28), calls=%async_computation.1 | async-start | bytes 2359296 | tf_op jit(solution)/shard_map/all_to_all | solution.py:23
  112.8 4.9 %copy-start.7 = (f32[48,256]{1,0:T(8,128)}, f32[48,256]{1,0:T(8,128)S(1)}, u32[]{:S(2)}) copy-start(f32[48,256]{1,0:T(8,128)S(1)} %fusion.29) | copy-start | bytes 147460
  114.5 3.3 %copy-start.8 = (f32[48,256]{1,0:T(8,128)}, f32[48,256]{1,0:T(8,128)S(1)}, u32[]{:S(2)}) copy-start(f32[48,256]{1,0:T(8,128)S(1)} %convolution_subtract_fusion.5) | copy-start | bytes 147460

commit v11 on v10

--- a/solution.py
+++ b/solution.py
@@ -86,11 +86,13 @@
         axis_index_groups=far_chips,
     )
 
-    left, right = turned[:, :width], turned[:, width:]
-    kept = jnp.where(core == 0, left, right)
-    other = lax.ppermute(jnp.where(core == 0, right, left), "col", swap)
-    pieces = [jnp.where(core == 0, kept, other), jnp.where(core == 0, other, kept)]
-    col_panel = spread(jnp.concatenate(pieces, axis=0), "row")
+    plane_groups = [
+        [r * cols + cores * z + c for r in range(rows) for c in range(cores)] for z in range(chips)
+    ]
+    pieces = jnp.stack([turned[:, c * width : (c + 1) * width] for c in range(cores)])
+    pieces = jnp.broadcast_to(pieces[None], (rows, cores, slab, width))
+    pieces = pieces.reshape(rows * cores, slab, width)
+    col_panel = exchange(pieces, ("row", "col"), plane_groups)
     col_panel = col_panel.reshape(rows, cores, NSUPER, nb_cols, width)
 
     def from_chip(block, steps):

time: 176 us -> 175 us (level)
  waiting for transfers between devices: 25.1 us -> 21.6 us
    all_to_all x3, waiting for transfers between devices: 25.1 us -> 12.2 us  [exchange(): lax.all_to_all(blocks, axis, 0, 0, tiled=True, axis_index_groups=groups)]
    ppermute x2, waiting for transfers between devices: 0.01 us -> 9.35 us  [from_chip(): return lax.ppermute(block, 'col', moves)]
    all_to_all x3, starting transfers between devices: 20.2 us -> 26.6 us  [exchange(): lax.all_to_all(blocks, axis, 0, 0, tiled=True, axis_index_groups=groups)]
    ppermute x2, starting transfers between devices: 15 us -> 12.1 us  [from_chip(): return lax.ppermute(block, 'col', moves)]
    ppermute x1 -> x0, starting transfers between devices: 1.92 us -> none  [per_device(): other = lax.ppermute(jnp.where(core == 0, right, left), 'col', swap)]
  transfers between devices with their start and end apart: 9 -> 8, of which waited for: 3 -> 3; matrix products, arithmetic and copies ran while one was open for 10% -> 10% of each run, Pallas kernels for 0% -> 0%
where the time goes in v11:
time: 175 us
  blocking collectives  74 us (42%)
  starting transfers between devices  45.5 us (26%)
  waiting for transfers between devices  21.6 us (12%)
  matrix products  15.6 us (9%)
  other arithmetic  9.65 us (6%)
  local copies, waits for them, and re-layouts  7.07 us (4%)
    all_to_all x3, blocking collectives, exchange(): lax.all_to_all(blocks, axis, 0, 0, tiled=True, axis_index_groups=groups)  41.5 us
    all_gather x1, blocking collectives, per_device(): lax.all_gather(jnp.concatenate([local_panel, chain_cols], axis=1), 'col',...  32.5 us
    all_to_all x3, starting transfers between devices, exchange(): lax.all_to_all(blocks, axis, 0, 0, tiled=True, axis_index_groups=groups)  26.6 us
    dot_general x17, matrix products, contract(): lax.dot_general(left, right, (((left_dim,), (right_dim,)), ((), ())), pre...  15.6 us
    all_to_all x3, waiting for transfers between devices, exchange(): lax.all_to_all(blocks, axis, 0, 0, tiled=True, axis_index_groups=groups)  12.2 us
    ppermute x2, starting transfers between devices, from_chip(): return lax.ppermute(block, 'col', moves)  12.1 us
    ppermute x2, waiting for transfers between devices, from_chip(): return lax.ppermute(block, 'col', moves)  9.35 us
    ppermute x1, starting transfers between devices, per_device(): across_other = lax.ppermute(across, 'col', swap)  4.22 us
  transfers between devices with their start and end apart: 8, of which 3 were waited for; matrix products, arithmetic and copies ran while one was open for 10% of the time, Pallas kernels for 0%

profile of v11, /device:TPU:1, one launch (start us, length us, event | category | flops | bytes accessed | tf_op | source)
XLA Modules:
  0.0 174.5 jit_solution(14478205348929509776)
XLA Ops:
  0.7 0.9 copy.47
  3.2 7.6 %all-to-all-start = ((f32[16,1,768]{2,1,0:T(1,128)}), f32[16,1,768]{2,1,0:T(1,128)S(1)}, u32[]{:S(2)}, u32[]{:S(2)}) async-start(f32[16,1,768]{2,1,0:T(1,128)} %broadcast_in_dim.16), calls=%async_computation | async-start | bytes 98304 | tf_op jit(solution)/shard_map/all_to_all | solution.py:23
  11.6 0.9 multiply_bitcast_fusion
  13.2 4.0 %all-to-all-done = f32[16,1,768]{2,1,0:T(1,128)S(1)} async-done(((f32[16,1,768]{2,1,0:T(1,128)}), f32[16,1,768]{2,1,0:T(1,128)S(1)}, u32[]{:S(2)}, u32[]{:S(2)}) %all-to-all-start) | async-done | bytes 49184 | tf_op jit(solution)/shard_map/all_to_all | solution.py:23
  17.7 32.5 %all_gather.3 = f32[192,1024]{1,0:T(8,128)S(1)} all-gather(f32[24,1024]{1,0:T(8,128)S(1)} %pad_maximum_fusion.2), channel_id=1, replica_groups={{0,1,8,9,16,17,24,25},{2,3,10,11,18,19,26,27},{4,5,12,13,20,21,28,29},{..., dimensions={0}, use_global_device_ids=true | all-gather | bytes 884736 | tf_op jit(solution)/shard_map/all_gather | solution.py:81
  50.2 8.7 %collective-permute-start = (f32[192,1024]{1,0:T(8,128)S(1)}, f32[192,1024]{1,0:T(8,128)}, u32[]{:S(2)}, u32[]{:S(2)}) collective-permute-start(f32[192,1024]{1,0:T(8,128)S(1)} %all_gather.3), channel_id=1, source_target_pairs={{2,0},{31,1},{4,2},{1,3},{6,4},{3,5},{8,6},{5,7},{10,8},{7,9},{12,... | collective-permute-start | bytes 2359304 | tf_op jit(solution)/shard_map/ppermute | solution.py:100
  59.0 1.1 broadcast_in_dim.18
  60.1 12.0 %all-to-all-start.2 = ((f32[32,24,384]{2,1,0:T(8,128)}), f32[32,24,384]{2,1,0:T(8,128)S(1)}, u32[]{:S(2)}, u32[]{:S(2)}) async-start(f32[32,24,384]{2,1,0:T(8,128)} %bitcast.119), calls=%async_computation.2 | async-start | bytes 2359296 | tf_op jit(solution)/shard_map/all_to_all | solution.py:23
  72.9 3.4 %collective-permute-start.2 = (f32[96,1024]{1,0:T(8,128)}, f32[96,1024]{1,0:T(8,128)}, u32[]{:S(2)}, u32[]{:S(2)}) collective-permute-start(f32[96,1024]{1,0:T(8,128)} %bitcast.7), channel_id=1, source_target_pairs={{4,0},{29,1},{6,2},{31,3},{8,4},{1,5},{10,6},{3,7},{12,8},{5,9},{1... | collective-permute-start | bytes 1179656 | tf_op jit(solution)/shard_map/ppermute | solution.py:100
  76.4 9.4 %collective-permute-done.2 = f32[96,1024]{1,0:T(8,128)} collective-permute-done((f32[96,1024]{1,0:T(8,128)}, f32[96,1024]{1,0:T(8,128)}, u32[]{:S(2)}, u32[]{:S(2)}) %collective-permute-start.2) | collective-permute-done | bytes 393248 | tf_op jit(solution)/shard_map/ppermute | solution.py:100
  85.7 4.2 %collective-permute-start.3 = (f32[96,1024]{1,0:T(8,128)}, f32[96,1024]{1,0:T(8,128)}, u32[]{:S(2)}, u32[]{:S(2)}) collective-permute-start(f32[96,1024]{1,0:T(8,128)} %collective-permute-done.2), channel_id=1, source_target_pairs={{0,1},{1,0},{2,3},{3,2},{4,5},{5,4},{6,7},{7,6},{8,9},{9,8},{10,11... | collective-permute-start | bytes 1179656 | tf_op jit(solution)/shard_map/ppermute | solution.py:108
  90.0 1.9 %collective-permute-start.1 = (f32[192,1024]{1,0:T(8,128)}, f32[192,1024]{1,0:T(8,128)}, u32[]{:S(2)}, u32[]{:S(2)}) collective-permute-start(f32[192,1024]{1,0:T(8,128)} %collective-permute-done), channel_id=1, source_target_pairs={{0,1},{1,0},{2,3},{3,2},{4,5},{5,4},{6,7},{7,6},{8,9},{9,8},{10,11... | collective-permute-start | bytes 2359304 | tf_op jit(solution)/shard_map/ppermute | solution.py:107
  92.5 0.9 fusion.25
  93.4 2.1 %broadcast_select_fusion.3 = (f32[96,1024]{1,0:T(8,128)}, f32[96,1024]{1,0:T(8,128)}) fusion(f32[96,1024]{1,0:T(8,128)} %collective-permute-done.2, f32[96,1024]{1,0:T(8,128)} %collective-permute-done.3, pred[]{:T(512)S(6)} %eq.14), kind=kLoop, calls=%fused_computation.47 | loop fusion | flops 196608 | bytes 1572865 | tf_op jit(solution)/shard_map/jit(_where)/select_n | solution.py:113
  95.5 1.0 fusion.61
  96.5 1.5 broadcast_select_fusion
  99.6 0.8 convolution_negate_fusion
  101.5 0.8 fusion.2
  102.7 0.8 fusion.1
  103.5 1.1 pad_maximum_fusion
  104.7 7.0 %all-to-all-start.1 = ((f32[16,48,384]{2,1,0:T(8,128)}), f32[16,48,384]{2,1,0:T(8,128)S(1)}, u32[]{:S(2)}, u32[]{:S(2)}) async-start(f32[16,48,384]{2,1,0:T(8,128)} %bitcast.28), calls=%async_computation.1 | async-start | bytes 2359296 | tf_op jit(solution)/shard_map/all_to_all | solution.py:23
  112.3 1.3 convolution_subtract_fusion.5
  113.7 1.3 convolution_subtract_fusion.4
  115.0 1.9 %convolution_subtract_fusion.3 = f32[48,256]{1,0:T(8,128)} fusion(f32[48,256]{1,0:T(8,128)S(1)} %convolution_subtract_fusion.4, f32[48,256]{1,0:T(8,128)S(1)} %convolution_subtract_fusion.5, f32[3,256,1024]{2,1,0:T(8,128)} %bitcast.111), kind=kOutput, calls=%fused_computation.18 | convolution fusion | flops 37761024 | bytes 409600 | tf_op jit(solution)/shard_map/dot_general | solution.py:13
  116.9 1.5 convolution_subtract_fusion.1
  118.4 1.3 convolution_subtract_fusion.2
  119.7 1.3 convolution_subtract_fusion
  121.1 8.2 %all-to-all-done.1 = f32[16,48,384]{2,1,0:T(8,128)S(1)} async-done(((f32[16,48,384]{2,1,0:T(8,128)}), f32[16,48,384]{2,1,0:T(8,128)S(1)}, u32[]{:S(2)}, u32[]{:S(2)}) %all-to-all-start.1) | async-done | bytes 1179680 | tf_op jit(solution)/shard_map/all_to_all | solution.py:23
  130.0 1.5 fusion.9
  131.7 11.8 %all_to_all.30 = f32[8,1,4608]{2,1,0:T(1,128)S(1)} all-to-all(f32[8,1,4608]{2,1,0:T(1,128)S(1)} %reshape.319), channel_id=1, replica_groups={{0,1,2,3,4,5,6,7},{8,9,10,11,12,13,14,15},{16,17,18,19,20,21,22,23},{24..., dimensions={0} | all-to-all | bytes 294912 | tf_op jit(solution)/shard_map/all_to_all | solution.py:23
  143.6 18.7 %all_to_all.31 = f32[4,1,4608]{2,1,0:T(1,128)S(1)} all-to-all(f32[4,1,4608]{2,1,0:T(1,128)S(1)} %broadcast_in_dim.19), channel_id=1, replica_groups={{0,8,16,24},{1,9,17,25},{2,10,18,26},{3,11,19,27},{4,12,20,28},{5,13,21..., dimensions={0} | all-to-all | bytes 147456 | tf_op jit(solution)/shard_map/all_to_all | solution.py:23
  162.4 11.0 %all_to_all.32 = f32[8,1,4608]{2,1,0:T(1,128)S(1)} all-to-all(f32[8,1,4608]{2,1,0:T(1,128)S(1)} %broadcast_in_dim.40), channel_id=1, replica_groups={{0,1,2,3,4,5,6,7},{8,9,10,11,12,13,14,15},{16,17,18,19,20,21,22,23},{24..., dimensions={0} | all-to-all | bytes 294912 | tf_op jit(solution)/shard_map/all_to_all | solution.py:23
  (68 shorter events, 10.8 us)
Async XLA Ops:
  0.6 99.0 %copy-start = (f32[768,384]{1,0:T(8,128)S(1)}, f32[768,384]{1,0:T(8,128)}, u32[]{:S(2)}) copy-start(f32[768,384]{1,0:T(8,128)} %param.5) | copy-start | bytes 3538948
  3.2 14.0 %all-to-all-start = ((f32[16,1,768]{2,1,0:T(1,128)}), f32[16,1,768]{2,1,0:T(1,128)S(1)}, u32[]{:S(2)}, u32[]{:S(2)}) async-start(f32[16,1,768]{2,1,0:T(1,128)} %broadcast_in_dim.16), calls=%async_computation | async-start | bytes 98304 | tf_op jit(solution)/shard_map/all_to_all | solution.py:23
  12.5 46.5 %collective-permute-start.4 = (f32[24,768]{1,0:T(8,128)S(1)}, f32[24,768]{1,0:T(8,128)S(1)}, u32[]{:S(2)}, u32[]{:S(2)}) collective-permute-start(f32[24,768]{1,0:T(8,128)S(1)} %multiply_bitcast_fusion), channel_id=1, source_target_pairs={{0,0},{1,1},{2,32},{3,33},{4,64},{5,65},{6,96},{7,97},{8,128},{9,1... | collective-permute-start | bytes 221192 | tf_op jit(solution)/shard_map/ppermute | solution.py:79
  17.6 74.9 %copy-start.2 = (f32[48,16,16]{0,2,1:T(8,128)}, f32[48,16,16]{0,2,1:T(8,128)S(1)}, u32[]{:S(2)}) copy-start(f32[48,16,16]{0,2,1:T(8,128)S(1)} %copy.49) | copy-start | bytes 147460
  50.2 39.7 %collective-permute-start = (f32[192,1024]{1,0:T(8,128)S(1)}, f32[192,1024]{1,0:T(8,128)}, u32[]{:S(2)}, u32[]{:S(2)}) collective-permute-start(f32[192,1024]{1,0:T(8,128)S(1)} %all_gather.3), channel_id=1, source_target_pairs={{2,0},{31,1},{4,2},{1,3},{6,4},{3,5},{8,6},{5,7},{10,8},{7,9},{12,... | collective-permute-start | bytes 2359304 | tf_op jit(solution)/shard_map/ppermute | solution.py:100
  60.1 35.4 %all-to-all-start.2 = ((f32[32,24,384]{2,1,0:T(8,128)}), f32[32,24,384]{2,1,0:T(8,128)S(1)}, u32[]{:S(2)}, u32[]{:S(2)}) async-start(f32[32,24,384]{2,1,0:T(8,128)} %bitcast.119), calls=%async_computation.2 | async-start | bytes 2359296 | tf_op jit(solution)/shard_map/all_to_all | solution.py:23
  72.9 12.8 %collective-permute-start.2 = (f32[96,1024]{1,0:T(8,128)}, f32[96,1024]{1,0:T(8,128)}, u32[]{:S(2)}, u32[]{:S(2)}) collective-permute-start(f32[96,1024]{1,0:T(8,128)} %bitcast.7), channel_id=1, source_target_pairs={{4,0},{29,1},{6,2},{31,3},{8,4},{1,5},{10,6},{3,7},{12,8},{5,9},{1... | collective-permute-start | bytes 1179656 | tf_op jit(solution)/shard_map/ppermute | solution.py:100
  85.7 7.7 %collective-permute-start.3 = (f32[96,1024]{1,0:T(8,128)}, f32[96,1024]{1,0:T(8,128)}, u32[]{:S(2)}, u32[]{:S(2)}) collective-permute-start(f32[96,1024]{1,0:T(8,128)} %collective-permute-done.2), channel_id=1, source_target_pairs={{0,1},{1,0},{2,3},{3,2},{4,5},{5,4},{6,7},{7,6},{8,9},{9,8},{10,11... | collective-permute-start | bytes 1179656 | tf_op jit(solution)/shard_map/ppermute | solution.py:108
  90.0 6.6 %collective-permute-start.1 = (f32[192,1024]{1,0:T(8,128)}, f32[192,1024]{1,0:T(8,128)}, u32[]{:S(2)}, u32[]{:S(2)}) collective-permute-start(f32[192,1024]{1,0:T(8,128)} %collective-permute-done), channel_id=1, source_target_pairs={{0,1},{1,0},{2,3},{3,2},{4,5},{5,4},{6,7},{7,6},{8,9},{9,8},{10,11... | collective-permute-start | bytes 2359304 | tf_op jit(solution)/shard_map/ppermute | solution.py:107
  95.5 2.5 %copy-start.5 = (f32[96,1024]{1,0:T(8,128)S(1)}, f32[96,1024]{1,0:T(8,128)}, u32[]{:S(2)}) copy-start(f32[96,1024]{1,0:T(8,128)} %get-tuple-element.14) | copy-start | bytes 1179652
  95.5 2.5 %copy-start.6 = (f32[96,1024]{1,0:T(8,128)S(1)}, f32[96,1024]{1,0:T(8,128)}, u32[]{:S(2)}) copy-start(f32[96,1024]{1,0:T(8,128)} %get-tuple-element.15) | copy-start | bytes 1179652
  99.5 3.2 %copy-start.1 = (f32[3,4,4,2,8,1024]{5,4,3,2,1,0:T(8,128)}, f32[3,4,4,2,8,1024]{5,4,3,2,1,0:T(8,128)S(1)}, u32[]{:S(2)}) copy-start(f32[3,4,4,2,8,1024]{5,4,3,2,1,0:T(8,128)S(1)} %copy.53) | copy-start | bytes 9437188
  103.5 8.1 %copy-start.3 = (f32[48,16,16]{0,2,1:T(8,128)S(1)}, f32[48,16,16]{0,2,1:T(8,128)}, u32[]{:S(2)}) copy-start(f32[48,16,16]{0,2,1:T(8,128)} %copy-done.2) | copy-start | bytes 147460
  103.5 8.5 %copy-start.10 = (f32[48]{0:T(128)S(1)}, f32[48]{0:T(128)}, u32[]{:S(2)}) copy-start(f32[48]{0:T(128)} %pad.9.clone) | copy-start | bytes 580
  103.5 10.1 %copy-start.9 = (f32[48,256]{1,0:T(8,128)S(1)}, f32[48,256]{1,0:T(8,128)}, u32[]{:S(2)}) copy-start(f32[48,256]{1,0:T(8,128)} %fusion.25) | copy-start | bytes 147460
  104.7 13.7 %copy-start.4 = (f32[16,2,1,8,384]{4,3,2,1,0:T(8,128)S(1)}, f32[16,2,1,8,384]{4,3,2,1,0:T(8,128)}, u32[]{:S(2)}) copy-start(f32[16,2,1,8,384]{4,3,2,1,0:T(8,128)} %get-tuple-element.11) | copy-start | bytes 1179652
  104.7 24.6 %all-to-all-start.1 = ((f32[16,48,384]{2,1,0:T(8,128)}), f32[16,48,384]{2,1,0:T(8,128)S(1)}, u32[]{:S(2)}, u32[]{:S(2)}) async-start(f32[16,48,384]{2,1,0:T(8,128)} %bitcast.28), calls=%async_computation.1 | async-start | bytes 2359296 | tf_op jit(solution)/shard_map/all_to_all | solution.py:23
  112.0 6.4 %copy-start.7 = (f32[48,256]{1,0:T(8,128)}, f32[48,256]{1,0:T(8,128)S(1)}, u32[]{:S(2)}) copy-start(f32[48,256]{1,0:T(8,128)S(1)} %fusion.29) | copy-start | bytes 147460
  113.6 4.7 %copy-start.8 = (f32[48,256]{1,0:T(8,128)}, f32[48,256]{1,0:T(8,128)S(1)}, u32[]{:S(2)}) copy-start(f32[48,256]{1,0:T(8,128)S(1)} %convolution_subtract_fusion.5) | copy-start | bytes 147460

commit v12 on v11

--- a/solution.py
+++ b/solution.py
@@ -107,20 +107,20 @@
     beside_other = lax.ppermute(beside, "col", swap)
     across_other = lax.ppermute(across, "col", swap)
     shape = (far, cores, NSUPER, nb_cols, wide)
-    after = jnp.where(core == 0, beside, beside_other).reshape(shape)
-    before = jnp.where(core == 0, beside_other, beside).reshape(shape)
     halves = [
         jnp.where(core == 0, across, across_other).reshape(far, slab, wide),
         jnp.where(core == 0, across_other, across).reshape(far, slab, wide),
     ]
-    blocks = [own.reshape(shape), after, jnp.stack(halves, axis=1).reshape(shape), before]
-    turnover = chip % NEAR
+    two = jnp.stack(halves, axis=1).reshape(shape)
+    first = core == 0
     places = []
     for place in range(NEAR):
-        choice = blocks[place]
-        for t in range(1, NEAR):
-            choice = jnp.where(turnover == t, blocks[(place - t) % NEAR], choice)
-        places.append(choice)
+        delta = (place - chip) % NEAR
+        from_beside = jnp.where(first, delta == 1, delta == NEAR - 1)
+        from_other = jnp.where(first, delta == NEAR - 1, delta == 1)
+        choice = jnp.where(from_other, beside_other.reshape(shape), two)
+        choice = jnp.where(from_beside, beside.reshape(shape), choice)
+        places.append(jnp.where(delta == 0, own.reshape(shape), choice))
     ordered = jnp.stack(places)
     ordered = jnp.transpose(ordered, (3, 1, 0, 2, 4, 5)).reshape(NSUPER, nb, wide)
     panel = [ordered[k, :, :height] for k in range(NSUPER)]
@@ -136,7 +136,7 @@
     incoming = exchange(outgoing.reshape(rows, own_rows, width), "row")
     new_rows = jnp.sum(incoming, axis=0)
 
-    exact = lax.Precision.HIGHEST
+    exact = lax.Precision.HIGH
     col_panel = [col_panel[:, :, k].reshape(nb, width) for k in range(NSUPER)]
     solved = []
     for k in range(NSUPER):

time: 175 us -> 176 us (level)
  waiting for transfers between devices: 21.6 us -> 19.3 us
    all_to_all x3, waiting for transfers between devices: 12.2 us -> 9.96 us  [exchange(): lax.all_to_all(blocks, axis, 0, 0, tiled=True, axis_index_groups=groups)]
  transfers between devices with their start and end apart: 8 -> 8, of which waited for: 3 -> 3; matrix products, arithmetic and copies ran while one was open for 10% -> 11% of each run, Pallas kernels for 0% -> 0%
where the time goes in v12:
time: 176 us; the launch traced here: 175 us
  blocking collectives  73.7 us (42%)
  starting transfers between devices  45.5 us (26%)
  waiting for transfers between devices  19.3 us (11%)
  matrix products  16.3 us (9%)
  other arithmetic  10.7 us (6%)
  local copies, waits for them, and re-layouts  8.76 us (5%)
    all_to_all x3, blocking collectives, exchange(): lax.all_to_all(blocks, axis, 0, 0, tiled=True, axis_index_groups=groups)  41.2 us
    all_gather x1, blocking collectives, per_device(): lax.all_gather(jnp.concatenate([local_panel, chain_cols], axis=1), 'col',...  32.5 us
    all_to_all x3, starting transfers between devices, exchange(): lax.all_to_all(blocks, axis, 0, 0, tiled=True, axis_index_groups=groups)  26.5 us
    dot_general x17, matrix products, contract(): lax.dot_general(left, right, (((left_dim,), (right_dim,)), ((), ())), pre...  16.3 us
    ppermute x2, starting transfers between devices, from_chip(): return lax.ppermute(block, 'col', moves)  12.1 us
    all_to_all x3, waiting for transfers between devices, exchange(): lax.all_to_all(blocks, axis, 0, 0, tiled=True, axis_index_groups=groups)  9.96 us
    ppermute x2, waiting for transfers between devices, from_chip(): return lax.ppermute(block, 'col', moves)  9.35 us
    ppermute x1, starting transfers between devices, per_device(): across_other = lax.ppermute(across, 'col', swap)  4.22 us
  transfers between devices with their start and end apart: 8, of which 3 were waited for; matrix products, arithmetic and copies ran while one was open for 11% of the time, Pallas kernels for 0%

profile of v12, /device:TPU:1, one launch (start us, length us, event | category | flops | bytes accessed | tf_op | source)
XLA Modules:
  0.0 175.4 jit_solution(15249674519151378984)
XLA Ops:
  3.2 7.6 %all-to-all-start = ((f32[16,1,768]{2,1,0:T(1,128)}), f32[16,1,768]{2,1,0:T(1,128)S(1)}, u32[]{:S(2)}, u32[]{:S(2)}) async-start(f32[16,1,768]{2,1,0:T(1,128)} %broadcast_in_dim.16), calls=%async_computation | async-start | bytes 98304 | tf_op jit(solution)/shard_map/all_to_all | solution.py:23
  11.6 0.9 multiply_bitcast_fusion
  13.2 4.0 %all-to-all-done = f32[16,1,768]{2,1,0:T(1,128)S(1)} async-done(((f32[16,1,768]{2,1,0:T(1,128)}), f32[16,1,768]{2,1,0:T(1,128)S(1)}, u32[]{:S(2)}, u32[]{:S(2)}) %all-to-all-start) | async-done | bytes 49184 | tf_op jit(solution)/shard_map/all_to_all | solution.py:23
  17.7 32.5 %all_gather.3 = f32[192,1024]{1,0:T(8,128)S(1)} all-gather(f32[24,1024]{1,0:T(8,128)S(1)} %pad_maximum_fusion.2), channel_id=1, replica_groups={{0,1,8,9,16,17,24,25},{2,3,10,11,18,19,26,27},{4,5,12,13,20,21,28,29},{..., dimensions={0}, use_global_device_ids=true | all-gather | bytes 884736 | tf_op jit(solution)/shard_map/all_gather | solution.py:81
  50.2 8.7 %collective-permute-start = (f32[192,1024]{1,0:T(8,128)S(1)}, f32[192,1024]{1,0:T(8,128)}, u32[]{:S(2)}, u32[]{:S(2)}) collective-permute-start(f32[192,1024]{1,0:T(8,128)S(1)} %all_gather.3), channel_id=1, source_target_pairs={{2,0},{31,1},{4,2},{1,3},{6,4},{3,5},{8,6},{5,7},{10,8},{7,9},{12,... | collective-permute-start | bytes 2359304 | tf_op jit(solution)/shard_map/ppermute | solution.py:100
  59.0 1.1 broadcast_in_dim.18
  60.1 12.0 %all-to-all-start.2 = ((f32[32,24,384]{2,1,0:T(8,128)}), f32[32,24,384]{2,1,0:T(8,128)S(1)}, u32[]{:S(2)}, u32[]{:S(2)}) async-start(f32[32,24,384]{2,1,0:T(8,128)} %bitcast.120), calls=%async_computation.2 | async-start | bytes 2359296 | tf_op jit(solution)/shard_map/all_to_all | solution.py:23
  73.0 3.4 %collective-permute-start.2 = (f32[96,1024]{1,0:T(8,128)}, f32[96,1024]{1,0:T(8,128)}, u32[]{:S(2)}, u32[]{:S(2)}) collective-permute-start(f32[96,1024]{1,0:T(8,128)} %bitcast.9), channel_id=1, source_target_pairs={{4,0},{29,1},{6,2},{31,3},{8,4},{1,5},{10,6},{3,7},{12,8},{5,9},{1... | collective-permute-start | bytes 1179656 | tf_op jit(solution)/shard_map/ppermute | solution.py:100
  76.4 9.4 %collective-permute-done.2 = f32[96,1024]{1,0:T(8,128)} collective-permute-done((f32[96,1024]{1,0:T(8,128)}, f32[96,1024]{1,0:T(8,128)}, u32[]{:S(2)}, u32[]{:S(2)}) %collective-permute-start.2) | collective-permute-done | bytes 393248 | tf_op jit(solution)/shard_map/ppermute | solution.py:100
  85.7 4.2 %collective-permute-start.3 = (f32[96,1024]{1,0:T(8,128)}, f32[96,1024]{1,0:T(8,128)}, u32[]{:S(2)}, u32[]{:S(2)}) collective-permute-start(f32[96,1024]{1,0:T(8,128)} %collective-permute-done.2), channel_id=1, source_target_pairs={{0,1},{1,0},{2,3},{3,2},{4,5},{5,4},{6,7},{7,6},{8,9},{9,8},{10,11... | collective-permute-start | bytes 1179656 | tf_op jit(solution)/shard_map/ppermute | solution.py:108
  90.0 1.9 %collective-permute-start.1 = (f32[192,1024]{1,0:T(8,128)}, f32[192,1024]{1,0:T(8,128)}, u32[]{:S(2)}, u32[]{:S(2)}) collective-permute-start(f32[192,1024]{1,0:T(8,128)} %collective-permute-done), channel_id=1, source_target_pairs={{0,1},{1,0},{2,3},{3,2},{4,5},{5,4},{6,7},{7,6},{8,9},{9,8},{10,11... | collective-permute-start | bytes 2359304 | tf_op jit(solution)/shard_map/ppermute | solution.py:107
  92.6 0.9 fusion.25
  93.5 1.9 %broadcast_select_fusion.1 = (f32[96,1024]{1,0:T(8,128)S(1)}, f32[96,1024]{1,0:T(8,128)}) fusion(f32[96,1024]{1,0:T(8,128)} %collective-permute-done.2, f32[96,1024]{1,0:T(8,128)} %collective-permute-done.3, pred[]{:T(512)S(6)} %eq.60), kind=kLoop, calls=%fused_computation.45 | loop fusion | flops 196608 | bytes 1572865 | tf_op jit(solution)/shard_map/jit(_where)/select_n | solution.py:111
  95.5 1.0 fusion.61
  96.5 1.5 select_select_fusion.2
  98.1 1.7 select_select_fusion.3
  102.2 0.9 fusion.60
  105.1 1.1 pad_maximum_fusion
  106.3 6.9 %all-to-all-start.1 = ((f32[16,48,384]{2,1,0:T(8,128)}), f32[16,48,384]{2,1,0:T(8,128)S(1)}, u32[]{:S(2)}, u32[]{:S(2)}) async-start(f32[16,48,384]{2,1,0:T(8,128)} %bitcast.28), calls=%async_computation.1 | async-start | bytes 2359296 | tf_op jit(solution)/shard_map/all_to_all | solution.py:23
  114.0 1.1 convolution_subtract_fusion.6
  115.4 1.2 convolution_subtract_fusion.4
  116.6 0.9 fusion.27
  117.6 1.2 convolution_subtract_fusion.5
  118.8 1.2 convolution_subtract_fusion.3
  120.0 1.5 convolution_subtract_fusion.1
  121.5 1.3 convolution_subtract_fusion.2
  123.6 1.3 convolution_subtract_fusion
  125.0 5.9 %all-to-all-done.1 = f32[16,48,384]{2,1,0:T(8,128)S(1)} async-done(((f32[16,48,384]{2,1,0:T(8,128)}), f32[16,48,384]{2,1,0:T(8,128)S(1)}, u32[]{:S(2)}, u32[]{:S(2)}) %all-to-all-start.1) | async-done | bytes 1179680 | tf_op jit(solution)/shard_map/all_to_all | solution.py:23
  131.0 1.7 fusion.9
  132.8 11.5 %all_to_all.30 = f32[8,1,4608]{2,1,0:T(1,128)S(1)} all-to-all(f32[8,1,4608]{2,1,0:T(1,128)S(1)} %reshape.325), channel_id=1, replica_groups={{0,1,2,3,4,5,6,7},{8,9,10,11,12,13,14,15},{16,17,18,19,20,21,22,23},{24..., dimensions={0} | all-to-all | bytes 294912 | tf_op jit(solution)/shard_map/all_to_all | solution.py:23
  144.4 18.7 %all_to_all.31 = f32[4,1,4608]{2,1,0:T(1,128)S(1)} all-to-all(f32[4,1,4608]{2,1,0:T(1,128)S(1)} %broadcast_in_dim.19), channel_id=1, replica_groups={{0,8,16,24},{1,9,17,25},{2,10,18,26},{3,11,19,27},{4,12,20,28},{5,13,21..., dimensions={0} | all-to-all | bytes 147456 | tf_op jit(solution)/shard_map/all_to_all | solution.py:23
  163.3 11.0 %all_to_all.32 = f32[8,1,4608]{2,1,0:T(1,128)S(1)} all-to-all(f32[8,1,4608]{2,1,0:T(1,128)S(1)} %broadcast_in_dim.40), channel_id=1, replica_groups={{0,1,2,3,4,5,6,7},{8,9,10,11,12,13,14,15},{16,17,18,19,20,21,22,23},{24..., dimensions={0} | all-to-all | bytes 294912 | tf_op jit(solution)/shard_map/all_to_all | solution.py:23
  (64 shorter events, 13.7 us)
Async XLA Ops:
  0.6 99.9 %copy-start = (f32[768,384]{1,0:T(8,128)S(1)}, f32[768,384]{1,0:T(8,128)}, u32[]{:S(2)}) copy-start(f32[768,384]{1,0:T(8,128)} %param.5) | copy-start | bytes 3538948
  3.2 14.0 %all-to-all-start = ((f32[16,1,768]{2,1,0:T(1,128)}), f32[16,1,768]{2,1,0:T(1,128)S(1)}, u32[]{:S(2)}, u32[]{:S(2)}) async-start(f32[16,1,768]{2,1,0:T(1,128)} %broadcast_in_dim.16), calls=%async_computation | async-start | bytes 98304 | tf_op jit(solution)/shard_map/all_to_all | solution.py:23
  12.5 46.5 %collective-permute-start.4 = (f32[24,768]{1,0:T(8,128)S(1)}, f32[24,768]{1,0:T(8,128)S(1)}, u32[]{:S(2)}, u32[]{:S(2)}) collective-permute-start(f32[24,768]{1,0:T(8,128)S(1)} %multiply_bitcast_fusion), channel_id=1, source_target_pairs={{0,0},{1,1},{2,32},{3,33},{4,64},{5,65},{6,96},{7,97},{8,128},{9,1... | collective-permute-start | bytes 221192 | tf_op jit(solution)/shard_map/ppermute | solution.py:79
  17.6 75.0 %copy-start.4 = (f32[48,16,16]{0,2,1:T(8,128)}, f32[48,16,16]{0,2,1:T(8,128)S(1)}, u32[]{:S(2)}) copy-start(f32[48,16,16]{0,2,1:T(8,128)S(1)} %copy.49) | copy-start | bytes 147460
  50.2 39.7 %collective-permute-start = (f32[192,1024]{1,0:T(8,128)S(1)}, f32[192,1024]{1,0:T(8,128)}, u32[]{:S(2)}, u32[]{:S(2)}) collective-permute-start(f32[192,1024]{1,0:T(8,128)S(1)} %all_gather.3), channel_id=1, source_target_pairs={{2,0},{31,1},{4,2},{1,3},{6,4},{3,5},{8,6},{5,7},{10,8},{7,9},{12,... | collective-permute-start | bytes 2359304 | tf_op jit(solution)/shard_map/ppermute | solution.py:100
  60.1 35.4 %all-to-all-start.2 = ((f32[32,24,384]{2,1,0:T(8,128)}), f32[32,24,384]{2,1,0:T(8,128)S(1)}, u32[]{:S(2)}, u32[]{:S(2)}) async-start(f32[32,24,384]{2,1,0:T(8,128)} %bitcast.120), calls=%async_computation.2 | async-start | bytes 2359296 | tf_op jit(solution)/shard_map/all_to_all | solution.py:23
  73.0 12.8 %collective-permute-start.2 = (f32[96,1024]{1,0:T(8,128)}, f32[96,1024]{1,0:T(8,128)}, u32[]{:S(2)}, u32[]{:S(2)}) collective-permute-start(f32[96,1024]{1,0:T(8,128)} %bitcast.9), channel_id=1, source_target_pairs={{4,0},{29,1},{6,2},{31,3},{8,4},{1,5},{10,6},{3,7},{12,8},{5,9},{1... | collective-permute-start | bytes 1179656 | tf_op jit(solution)/shard_map/ppermute | solution.py:100
  85.7 7.8 %collective-permute-start.3 = (f32[96,1024]{1,0:T(8,128)}, f32[96,1024]{1,0:T(8,128)}, u32[]{:S(2)}, u32[]{:S(2)}) collective-permute-start(f32[96,1024]{1,0:T(8,128)} %collective-permute-done.2), channel_id=1, source_target_pairs={{0,1},{1,0},{2,3},{3,2},{4,5},{5,4},{6,7},{7,6},{8,9},{9,8},{10,11... | collective-permute-start | bytes 1179656 | tf_op jit(solution)/shard_map/ppermute | solution.py:108
  90.0 6.6 %collective-permute-start.1 = (f32[192,1024]{1,0:T(8,128)}, f32[192,1024]{1,0:T(8,128)}, u32[]{:S(2)}, u32[]{:S(2)}) collective-permute-start(f32[192,1024]{1,0:T(8,128)} %collective-permute-done), channel_id=1, source_target_pairs={{0,1},{1,0},{2,3},{3,2},{4,5},{5,4},{6,7},{7,6},{8,9},{9,8},{10,11... | collective-permute-start | bytes 2359304 | tf_op jit(solution)/shard_map/ppermute | solution.py:107
  95.5 2.6 %copy-start.2 = (f32[96,1024]{1,0:T(8,128)S(1)}, f32[96,1024]{1,0:T(8,128)}, u32[]{:S(2)}) copy-start(f32[96,1024]{1,0:T(8,128)} %get-tuple-element.12) | copy-start | bytes 1179652
  100.6 3.7 %copy-start.1 = (f32[3,4,4,2,8,1024]{5,4,3,2,1,0:T(8,128)}, f32[3,4,4,2,8,1024]{5,4,3,2,1,0:T(8,128)S(1)}, u32[]{:S(2)}) copy-start(f32[3,4,4,2,8,1024]{5,4,3,2,1,0:T(8,128)S(1)} %copy.53) | copy-start | bytes 9437188
  105.1 10.0 %copy-start.5 = (f32[48,16,16]{0,2,1:T(8,128)S(1)}, f32[48,16,16]{0,2,1:T(8,128)}, u32[]{:S(2)}) copy-start(f32[48,16,16]{0,2,1:T(8,128)} %copy-done.4) | copy-start | bytes 147460
  105.1 14.9 %copy-start.3 = (f32[16,2,1,8,384]{4,3,2,1,0:T(8,128)S(1)}, f32[16,2,1,8,384]{4,3,2,1,0:T(8,128)}, u32[]{:S(2)}) copy-start(f32[16,2,1,8,384]{4,3,2,1,0:T(8,128)} %get-tuple-element.10) | copy-start | bytes 1179652
  106.3 15.2 %copy-start.6 = (f32[16,2,1,8,384]{4,3,2,1,0:T(8,128)S(1)}, f32[16,2,1,8,384]{4,3,2,1,0:T(8,128)}, u32[]{:S(2)}) copy-start(f32[16,2,1,8,384]{4,3,2,1,0:T(8,128)} %get-tuple-element.8) | copy-start | bytes 1179652
  106.3 24.6 %all-to-all-start.1 = ((f32[16,48,384]{2,1,0:T(8,128)}), f32[16,48,384]{2,1,0:T(8,128)S(1)}, u32[]{:S(2)}, u32[]{:S(2)}) async-start(f32[16,48,384]{2,1,0:T(8,128)} %bitcast.28), calls=%async_computation.1 | async-start | bytes 2359296 | tf_op jit(solution)/shard_map/all_to_all | solution.py:23
  122.9 0.8 copy-start.7
  130.9 44.4 %copy-start.8 = (f32[48,384]{1,0:T(8,128)}, f32[48,384]{1,0:T(8,128)S(1)}, u32[]{:S(2)}) copy-start(f32[48,384]{1,0:T(8,128)S(1)} %reduce_sum.27) | copy-start | bytes 221188
